TPU v7x, 32 devices: a whole 2x2x4 slice. The times are simulated.
32 devices in a mesh: region: 2 (over y), space: 8 (over z, x), day: 2 (over core).
Axes of the slice: x: 2, y: 2, z: 4, core: 2. Of those that a mesh axis runs over, the one named last changes fastest.
Arguments:
- observed: float32 [4, 64, 4096], P('day', ('region', 'space')), parts along dimension 1, may hold values from -20 to 20
- gap_mask: int32 [4, 64, 4096], P('day', ('region', 'space')), parts along dimension 1, may hold values 0 or 1
- sea_mask: int32 [64, 4096], P(('region', 'space')), parts along dimension 0, may hold values 0 or 1
- stencil: bfloat16 [9, 64, 4096], P(None, ('region', 'space')), parts along dimension 1, may hold values from 0.019897461 to 0.19921875
- precision: float32 [64, 4096], P(('region', 'space')), parts along dimension 0, may hold values from 0.5 to 4
- noise_precision: float32 [64, 4096], P(('region', 'space')), parts along dimension 0, may hold values from 0.5 to 8
- perturbation: bfloat16 [2, 4, 64, 4096], P(None, 'day', ('region', 'space')), parts along dimension 2, may hold values from -6 to 6
Outputs:
- posterior_mean: float32 [4, 64, 4096], P('day', ('region', 'space')), parts along dimension 1
- fitted: float32 [2, 64, 4096], P(None, ('region', 'space'), 'day'), parts along dimension 1
There are 2 independent parts, one for each index of `region`. A program takes and returns all parts, laid end to end along the dimension named above; each array names one. Nothing has to cross between parts.
All inputs are finite; a program needn't handle non-finite values. No bound on the sum of `gap_mask` or of `sea_mask` on one device may be relied on, other than what follows from the above.
Results may differ from a plain program's by a relative error of at most 0.0003.
Values sent between devices are 32-bit elements; how exact they have to be, the bound alone decides.
No kernel may reach another device: no remote copies, remote signals or barrier semaphores. Data moves between devices by JAX's collectives and lax.ppermute only.
A program may use at most 64 MiB of HBM per device.

v0:
```python
import jax
import jax.numpy as jnp
from jax import lax
from jax.sharding import PartitionSpec as P

ITERS = 2


OFFSETS = ((-1, -1), (-1, 0), (-1, 1), (0, -1), (0, 0), (0, 1), (1, -1), (1, 0), (1, 1))
RIDGE = 1.0


def padded(x, sides, width):
    for axis, dim in sides:
        size, length = (lax.axis_size(axis), x.shape[dim])
        up = [(i, (i + 1) % size) for i in range(size - 1)]
        down = [(j, i) for i, j in up]
        last = lax.slice_in_dim(x, length - width, length, axis=dim)
        first = lax.slice_in_dim(x, 0, width, axis=dim)
        before = lax.ppermute(last, axis, up)
        after = lax.ppermute(first, axis, down)
        x = jnp.concatenate([before, x, after], axis=dim)
    return x


def from_behind(x, axis, by):
    size = lax.axis_size(axis)
    pairs = [(i, i + by) for i in range(size) if 0 <= i + by < size]
    return lax.ppermute(x, axis, pairs)


def column_shift(values, col_step):
    if col_step == 0:
        return values
    zero_column = jnp.zeros_like(values[..., :1])
    if col_step > 0:
        return jnp.concatenate([values[..., 1:], zero_column], -1)
    return jnp.concatenate([zero_column, values[..., :-1]], -1)


def forward_rows(values, coefficients):
    height = coefficients.shape[1]
    result = jnp.zeros(values[..., 1:-1, :].shape, jnp.float32)
    for position, (row_step, col_step) in enumerate(OFFSETS):
        rows_taken = values[..., 1 + row_step : 1 + row_step + height, :]
        result = result + coefficients[position] * column_shift(rows_taken, col_step)
    return result


def transposed_rows(values, coefficients):
    height = values.shape[-2] - 2
    result = jnp.zeros(values[..., 1:-1, :].shape, jnp.float32)
    for position, (row_step, col_step) in enumerate(OFFSETS):
        product = coefficients[position] * values
        rows_taken = product[..., 1 - row_step : 1 - row_step + height, :]
        result = result + column_shift(rows_taken, -col_step)
    return result


def local_sums(first, second):
    return jnp.sum(first * second, axis=(1, 2, 3))


def expand(scalars):
    return scalars[:, None, None, None]


def fit_cells(totals):
    diag_first = totals[0] + RIDGE
    cross_term = totals[1]
    diag_second = totals[2] + RIDGE
    determinant = diag_first * diag_second - cross_term * cross_term
    persistence = (diag_second * totals[3] - cross_term * totals[4]) / determinant
    diffusion = (diag_first * totals[4] - cross_term * totals[3]) / determinant
    return jnp.stack([persistence, diffusion], 0)


def shards(observed, gap_mask, sea_mask, stencil, precision, noise_precision, perturbation):
    sea_float = sea_mask.astype(jnp.float32)
    coefficients = stencil.astype(jnp.float32)
    observed_precision = noise_precision * gap_mask.astype(jnp.float32)
    base_side = sea_float * observed_precision * observed
    spread = sea_float * jnp.sqrt(precision + observed_precision)
    right_sides = jnp.stack(
        [
            base_side,
            base_side + spread * perturbation[0].astype(jnp.float32),
            base_side + spread * perturbation[1].astype(jnp.float32),
        ],
        0,
    )
    static_rim = padded(coefficients, (("space", 1),), 1)
    day_number = lax.axis_index("day")
    day_total = lax.axis_size("day")

    def residual_norms(residual):
        return lax.psum(local_sums(residual, residual), ("space", "day"))

    solution = jnp.zeros_like(right_sides)
    residual = right_sides
    direction = right_sides
    norm_now = residual_norms(residual)
    for iteration in range(ITERS):
        masked = sea_float * direction
        padded_state = padded(masked, (("space", 2),), 1)
        apply_before_plane = from_behind(padded_state[:, -1:], "day", 1)
        apply_earlier = jnp.concatenate([apply_before_plane, padded_state[:, :-1]], 1)
        innovation = masked - forward_rows(apply_earlier, coefficients)
        weighted = precision * innovation
        weighted_padded = padded(weighted, (("space", 2),), 1)
        after_plane = from_behind(weighted_padded[:, :1], "day", -1)
        following = jnp.concatenate([weighted_padded[:, 1:], after_plane], 1)
        applied = weighted - transposed_rows(following, static_rim) + observed_precision * masked
        applied = sea_float * applied + (1.0 - sea_float) * direction
        curvature = lax.psum(local_sums(direction, applied), ("space", "day"))
        step_size = norm_now / curvature
        solution = solution + expand(step_size) * direction
        residual = residual - expand(step_size) * applied
        if iteration + 1 < ITERS:
            norm_next = residual_norms(residual)
            direction = residual + expand(norm_next / norm_now) * direction
            norm_now = norm_next
    samples = solution[1:]
    sample_padded = padded(samples, (("space", 2),), 1)
    before_plane = from_behind(sample_padded[:, -1:], "day", 1)
    earlier = jnp.concatenate([before_plane, sample_padded[:, :-1]], 1)
    centre = earlier[:, :, 1:-1]
    height = centre.shape[2]
    laplacian = -8.0 * centre
    for row_step, col_step in OFFSETS:
        if row_step != 0 or col_step != 0:
            laplacian = laplacian + column_shift(
                earlier[:, :, 1 + row_step : 1 + row_step + height], col_step
            )
    stacked = jnp.stack(
        [
            jnp.sum(centre * centre, axis=(0, 1)),
            jnp.sum(centre * laplacian, axis=(0, 1)),
            jnp.sum(laplacian * laplacian, axis=(0, 1)),
            jnp.sum(centre * samples, axis=(0, 1)),
            jnp.sum(laplacian * samples, axis=(0, 1)),
        ],
        0,
    )
    totals = lax.psum(stacked, "day")
    breadth = totals.shape[2] // day_total
    totals = lax.dynamic_slice_in_dim(totals, day_number * breadth, breadth, 2)
    return (solution[0], fit_cells(totals))


def solution(mesh):
    placed = (
        P("day", ("region", "space"), None),
        P("day", ("region", "space"), None),
        P(("region", "space"), None),
        P(None, ("region", "space"), None),
        P(("region", "space"), None),
        P(("region", "space"), None),
        P(None, "day", ("region", "space"), None),
    )
    return jax.shard_map(
        shards,
        mesh=mesh,
        in_specs=placed,
        out_specs=(P("day", ("region", "space"), None), P(None, ("region", "space"), "day")),
        check_vma=False,
    )
```

profile of v0, /device:TPU:0, one launch (start us, length us, event | category | flops | bytes accessed | tf_op | source)
XLA Modules:
  0.0 208.1 jit_solution(12920346424859504822)
XLA Ops:
  7.3 1.5 fusion.136
  8.8 1.3 collective-permute-start.4
  10.2 5.5 %collective-permute-start.3 = (f32[9,1,4096]{2,0,1:T(8,128)S(1)}, f32[9,1,4096]{2,0,1:T(8,128)S(1)}, u32[]{:S(2)}, u32[]{:S(2)}) collective-permute-start(f32[9,1,4096]{2,0,1:T(8,128)S(1)} %copy.10), channel_id=1, source_target_pairs={{0,2},{2,4},{4,6},{6,8},{8,10},{10,12},{12,14},{1,3},{3,5},{5,7},{... | collective-permute-start | bytes 442376 | tf_op jit(solution)/shard_map/ppermute | solution.py:20
  16.3 4.8 %collective-permute-start = (f32[3,2,1,4096]{3,2,1,0:T(1,128)S(1)}, f32[3,2,1,4096]{3,2,1,0:T(1,128)S(1)}, u32[]{:S(2)}, u32[]{:S(2)}) collective-permute-start(f32[3,2,1,4096]{3,2,1,0:T(1,128)S(1)} %get-tuple-element.83), channel_id=1, source_target_pairs={{0,2},{2,4},{4,6},{6,8},{8,10},{10,12},{12,14},{1,3},{3,5},{5,7},{... | collective-permute-start | bytes 294920 | tf_op jit(solution)/shard_map/ppermute | solution.py:20
  21.2 1.3 collective-permute-start.1
  22.6 7.4 %collective-permute-done = f32[3,2,1,4096]{3,2,1,0:T(1,128)S(1)} collective-permute-done((f32[3,2,1,4096]{3,2,1,0:T(1,128)S(1)}, f32[3,2,1,4096]{3,2,1,0:T(1,128)S(1)}, u32[]{:S(2)}, u32[]{:S(2)}) %collective-permute-start) | collective-permute-done | bytes 98336 | tf_op jit(solution)/shard_map/ppermute | solution.py:20
  30.3 1.9 collective-permute-start.2
  35.6 4.4 %collective-permute-start.5 = (f32[3,2,1,4096]{3,2,1,0:T(1,128)S(1)}, f32[3,2,1,4096]{3,2,1,0:T(1,128)S(1)}, u32[]{:S(2)}, u32[]{:S(2)}) collective-permute-start(f32[3,2,1,4096]{3,2,1,0:T(1,128)S(1)} %get-tuple-element.81), channel_id=1, source_target_pairs={{0,2},{2,4},{4,6},{6,8},{8,10},{10,12},{12,14},{1,3},{3,5},{5,7},{... | collective-permute-start | bytes 294920 | tf_op jit(solution)/shard_map/ppermute | solution.py:20
  40.0 1.3 collective-permute-start.6
  42.5 4.1 %collective-permute-done.6 = f32[3,2,1,4096]{3,2,1,0:T(1,128)S(1)} collective-permute-done((f32[3,2,1,4096]{3,2,1,0:T(1,128)S(1)}, f32[3,2,1,4096]{3,2,1,0:T(1,128)S(1)}, u32[]{:S(2)}, u32[]{:S(2)}) %collective-permute-start.6) | collective-permute-done | bytes 98336 | tf_op jit(solution)/shard_map/ppermute | solution.py:21
  47.0 1.3 collective-permute-start.7
  48.8 1.8 collective-permute-done.7
  52.6 30.4 %all-reduce.30 = (f32[3]{0:T(128)S(1)}, f32[3]{0:T(128)S(1)}) all-reduce(f32[3]{0:T(128)S(1)} %get-tuple-element.6, f32[3]{0:T(128)S(1)} %get-tuple-element.5), channel_id=1, replica_groups=mesh['region'=2,'space'=8,'day'=2] {'space','day'}, use_global_device_ids=true, to_apply=%region_1.0 | all-reduce | flops 6 | bytes 48 | tf_op jit(solution)/shard_map/psum | solution.py:97
  83.3 29.5 %psum.37 = f32[3]{0:T(128)S(1)} all-reduce(f32[3]{0:T(128)S(1)} %multiply_reduce_fusion), channel_id=1, replica_groups=mesh['region'=2,'space'=8,'day'=2] {'space','day'}, use_global_device_ids=true, to_apply=%region_5.0 | all-reduce | flops 3 | bytes 24 | tf_op jit(solution)/shard_map/psum | solution.py:97
  113.2 1.3 collective-permute-start.8
  114.5 1.3 collective-permute-start.9
  115.8 3.1 %collective-permute-done.8 = f32[3,2,1,4096]{3,2,1,0:T(1,128)S(1)} collective-permute-done((f32[3,2,1,4096]{3,2,1,0:T(1,128)S(1)}, f32[3,2,1,4096]{3,2,1,0:T(1,128)S(1)}, u32[]{:S(2)}, u32[]{:S(2)}) %collective-permute-start.8) | collective-permute-done | bytes 98336 | tf_op jit(solution)/shard_map/ppermute | solution.py:20
  119.0 2.1 collective-permute-done.9
  121.4 1.3 collective-permute-start.10
  122.7 1.3 collective-permute-done.10
  126.0 2.7 %collective-permute-start.11 = (f32[3,2,1,4096]{3,2,1,0:T(1,128)S(1)}, f32[3,2,1,4096]{3,2,1,0:T(1,128)S(1)}, u32[]{:S(2)}, u32[]{:S(2)}) collective-permute-start(f32[3,2,1,4096]{3,2,1,0:T(1,128)S(1)} %get-tuple-element.77), channel_id=1, source_target_pairs={{0,2},{2,4},{4,6},{6,8},{8,10},{10,12},{12,14},{1,3},{3,5},{5,7},{... | collective-permute-start | bytes 294920 | tf_op jit(solution)/shard_map/ppermute | solution.py:20
  128.7 1.3 collective-permute-start.12
  131.3 4.1 %collective-permute-done.12 = f32[3,2,1,4096]{3,2,1,0:T(1,128)S(1)} collective-permute-done((f32[3,2,1,4096]{3,2,1,0:T(1,128)S(1)}, f32[3,2,1,4096]{3,2,1,0:T(1,128)S(1)}, u32[]{:S(2)}, u32[]{:S(2)}) %collective-permute-start.12) | collective-permute-done | bytes 98336 | tf_op jit(solution)/shard_map/ppermute | solution.py:21
  135.7 1.5 collective-permute-start.13
  137.2 2.1 %collective-permute-done.13 = f32[3,1,6,4096]{3,2,1,0:T(8,128)S(1)} collective-permute-done((f32[3,1,6,4096]{3,2,1,0:T(8,128)S(1)}, f32[3,1,6,4096]{3,2,1,0:T(8,128)S(1)}, u32[]{:S(2)}, u32[]{:S(2)}) %collective-permute-start.13) | collective-permute-done | bytes 294944 | tf_op jit(solution)/shard_map/ppermute | solution.py:29
  141.2 29.7 %psum.38 = f32[3]{0:T(128)S(1)} all-reduce(f32[3]{0:T(128)S(1)} %fusion.103), channel_id=1, replica_groups=mesh['region'=2,'space'=8,'day'=2] {'space','day'}, use_global_device_ids=true, to_apply=%region_7.0 | all-reduce | flops 3 | bytes 24 | tf_op jit(solution)/shard_map/psum | solution.py:115
  171.2 1.3 collective-permute-start.14
  172.5 1.3 collective-permute-start.15
  173.8 1.5 collective-permute-done.14
  175.4 3.3 %collective-permute-done.15 = f32[2,2,1,4096]{3,2,1,0:T(1,128)S(1)} collective-permute-done((f32[2,2,1,4096]{3,2,1,0:T(1,128)S(1)}, f32[2,2,1,4096]{3,2,1,0:T(1,128)S(1)}, u32[]{:S(2)}, u32[]{:S(2)}) %collective-permute-start.15) | collective-permute-done | bytes 65568 | tf_op jit(solution)/shard_map/ppermute | solution.py:21
  178.9 1.3 collective-permute-start.16
  184.3 15.5 %all-reduce.33.cloned.1.call-done = f32[5,4,4096]{2,1,0:T(4,128)} async-done(((f32[5,4,4096]{2,1,0:T(4,128)}), f32[5,4,4096]{2,1,0:T(4,128)}) %all-reduce.33.cloned.1.call-update) | async-done | bytes 327696 | tf_op jit(solution)/shard_map/psum | solution.py:145
  (88 shorter events, 20.8 us)
Async XLA Ops:
  7.2 8.6 %copy-start.4 = (s32[4,4096]{1,0:T(4,128)S(1)}, s32[4,4096]{1,0:T(4,128)}, u32[]{:S(2)}) copy-start(s32[4,4096]{1,0:T(4,128)} %param.9) | copy-start | bytes 196612
  7.2 8.6 %copy-start.2 = (f32[2,4,4096]{2,1,0:T(4,128)S(1)}, f32[2,4,4096]{2,1,0:T(4,128)}, u32[]{:S(2)}) copy-start(f32[2,4,4096]{2,1,0:T(4,128)} %param.7) | copy-start | bytes 393220
  7.2 8.6 %copy-start.7 = (f32[4,4096]{1,0:T(4,128)S(1)}, f32[4,4096]{1,0:T(4,128)}, u32[]{:S(2)}) copy-start(f32[4,4096]{1,0:T(4,128)} %param.12) | copy-start | bytes 196612
  7.2 8.6 %copy-start.5 = (s32[2,4,4096]{2,1,0:T(4,128)S(1)}, s32[2,4,4096]{2,1,0:T(4,128)}, u32[]{:S(2)}) copy-start(s32[2,4,4096]{2,1,0:T(4,128)} %param.8) | copy-start | bytes 393220
  7.2 8.7 %copy-start.1 = (f32[4,4096]{1,0:T(4,128)S(1)}, f32[4,4096]{1,0:T(4,128)}, u32[]{:S(2)}) copy-start(f32[4,4096]{1,0:T(4,128)} %param.11) | copy-start | bytes 196612
  7.2 8.7 %copy-start.6 = (bf16[2,2,4,4096]{3,2,1,0:T(4,128)(2,1)S(1)}, bf16[2,2,4,4096]{3,2,1,0:T(4,128)(2,1)}, u32[]{:S(2)}) copy-start(bf16[2,2,4,4096]{3,2,1,0:T(4,128)(2,1)} %param.13) | copy-start | bytes 393220
  7.2 192.5 %all-reduce.33.cloned.1.call-start = ((), (), s32[]{:S(2)}) async-start(), calls=%async_computation | async-start | bytes 655360 | tf_op jit(solution)/shard_map/psum | solution.py:145
  8.8 23.4 %collective-permute-start.4 = (f32[9,1,4096]{2,0,1:T(8,128)S(1)}, f32[9,1,4096]{2,0,1:T(8,128)S(1)}, u32[]{:S(2)}, u32[]{:S(2)}) collective-permute-start(f32[9,1,4096]{2,0,1:T(8,128)S(1)} %copy.11), channel_id=1, source_target_pairs={{2,0},{4,2},{6,4},{8,6},{10,8},{12,10},{14,12},{3,1},{5,3},{7,5},{... | collective-permute-start | bytes 442376 | tf_op jit(solution)/shard_map/ppermute | solution.py:21
  10.2 22.2 %collective-permute-start.3 = (f32[9,1,4096]{2,0,1:T(8,128)S(1)}, f32[9,1,4096]{2,0,1:T(8,128)S(1)}, u32[]{:S(2)}, u32[]{:S(2)}) collective-permute-start(f32[9,1,4096]{2,0,1:T(8,128)S(1)} %copy.10), channel_id=1, source_target_pairs={{0,2},{2,4},{4,6},{6,8},{8,10},{10,12},{12,14},{1,3},{3,5},{5,7},{... | collective-permute-start | bytes 442376 | tf_op jit(solution)/shard_map/ppermute | solution.py:20
  15.9 6.6 %copy-start = (bf16[9,4,4096]{2,1,0:T(4,128)(2,1)S(1)}, bf16[9,4,4096]{2,1,0:T(4,128)(2,1)}, u32[]{:S(2)}) copy-start(bf16[9,4,4096]{2,1,0:T(4,128)(2,1)} %param.10) | copy-start | bytes 884740
  16.3 13.6 %collective-permute-start = (f32[3,2,1,4096]{3,2,1,0:T(1,128)S(1)}, f32[3,2,1,4096]{3,2,1,0:T(1,128)S(1)}, u32[]{:S(2)}, u32[]{:S(2)}) collective-permute-start(f32[3,2,1,4096]{3,2,1,0:T(1,128)S(1)} %get-tuple-element.83), channel_id=1, source_target_pairs={{0,2},{2,4},{4,6},{6,8},{8,10},{10,12},{12,14},{1,3},{3,5},{5,7},{... | collective-permute-start | bytes 294920 | tf_op jit(solution)/shard_map/ppermute | solution.py:20
  21.2 8.8 %collective-permute-start.1 = (f32[3,2,1,4096]{3,2,1,0:T(1,128)S(1)}, f32[3,2,1,4096]{3,2,1,0:T(1,128)S(1)}, u32[]{:S(2)}, u32[]{:S(2)}) collective-permute-start(f32[3,2,1,4096]{3,2,1,0:T(1,128)S(1)} %get-tuple-element.84), channel_id=1, source_target_pairs={{2,0},{4,2},{6,4},{8,6},{10,8},{12,10},{14,12},{3,1},{5,3},{7,5},{... | collective-permute-start | bytes 294920 | tf_op jit(solution)/shard_map/ppermute | solution.py:21
  30.3 3.3 %collective-permute-start.2 = (f32[3,1,6,4096]{3,2,1,0:T(8,128)S(1)}, f32[3,1,6,4096]{3,2,1,0:T(8,128)S(1)}, u32[]{:S(2)}, u32[]{:S(2)}) collective-permute-start(f32[3,1,6,4096]{3,2,1,0:T(8,128)S(1)} %get-tuple-element.56), channel_id=1, source_target_pairs={{0,1},{2,3},{4,5},{6,7},{8,9},{10,11},{12,13},{14,15},{16,17},{18,... | collective-permute-start | bytes 884744 | tf_op jit(solution)/shard_map/ppermute | solution.py:29
  35.6 7.0 %collective-permute-start.5 = (f32[3,2,1,4096]{3,2,1,0:T(1,128)S(1)}, f32[3,2,1,4096]{3,2,1,0:T(1,128)S(1)}, u32[]{:S(2)}, u32[]{:S(2)}) collective-permute-start(f32[3,2,1,4096]{3,2,1,0:T(1,128)S(1)} %get-tuple-element.81), channel_id=1, source_target_pairs={{0,2},{2,4},{4,6},{6,8},{8,10},{10,12},{12,14},{1,3},{3,5},{5,7},{... | collective-permute-start | bytes 294920 | tf_op jit(solution)/shard_map/ppermute | solution.py:20
  40.0 6.7 %collective-permute-start.6 = (f32[3,2,1,4096]{3,2,1,0:T(1,128)S(1)}, f32[3,2,1,4096]{3,2,1,0:T(1,128)S(1)}, u32[]{:S(2)}, u32[]{:S(2)}) collective-permute-start(f32[3,2,1,4096]{3,2,1,0:T(1,128)S(1)} %get-tuple-element.82), channel_id=1, source_target_pairs={{2,0},{4,2},{6,4},{8,6},{10,8},{12,10},{14,12},{3,1},{5,3},{7,5},{... | collective-permute-start | bytes 294920 | tf_op jit(solution)/shard_map/ppermute | solution.py:21
  47.0 3.6 %collective-permute-start.7 = (f32[3,1,6,4096]{3,2,1,0:T(8,128)S(1)}, f32[3,1,6,4096]{3,2,1,0:T(8,128)S(1)}, u32[]{:S(2)}, u32[]{:S(2)}) collective-permute-start(f32[3,1,6,4096]{3,2,1,0:T(8,128)S(1)} %get-tuple-element.49), channel_id=1, source_target_pairs={{1,0},{3,2},{5,4},{7,6},{9,8},{11,10},{13,12},{15,14},{17,16},{19,... | collective-permute-start | bytes 884744 | tf_op jit(solution)/shard_map/ppermute | solution.py:29
  113.2 5.7 %collective-permute-start.8 = (f32[3,2,1,4096]{3,2,1,0:T(1,128)S(1)}, f32[3,2,1,4096]{3,2,1,0:T(1,128)S(1)}, u32[]{:S(2)}, u32[]{:S(2)}) collective-permute-start(f32[3,2,1,4096]{3,2,1,0:T(1,128)S(1)} %get-tuple-element.79), channel_id=1, source_target_pairs={{0,2},{2,4},{4,6},{6,8},{8,10},{10,12},{12,14},{1,3},{3,5},{5,7},{... | collective-permute-start | bytes 294920 | tf_op jit(solution)/shard_map/ppermute | solution.py:20
  114.5 6.5 %collective-permute-start.9 = (f32[3,2,1,4096]{3,2,1,0:T(1,128)S(1)}, f32[3,2,1,4096]{3,2,1,0:T(1,128)S(1)}, u32[]{:S(2)}, u32[]{:S(2)}) collective-permute-start(f32[3,2,1,4096]{3,2,1,0:T(1,128)S(1)} %get-tuple-element.80), channel_id=1, source_target_pairs={{2,0},{4,2},{6,4},{8,6},{10,8},{12,10},{14,12},{3,1},{5,3},{7,5},{... | collective-permute-start | bytes 294920 | tf_op jit(solution)/shard_map/ppermute | solution.py:21
  121.4 2.6 %collective-permute-start.10 = (f32[3,1,6,4096]{3,2,1,0:T(8,128)S(1)}, f32[3,1,6,4096]{3,2,1,0:T(8,128)S(1)}, u32[]{:S(2)}, u32[]{:S(2)}) collective-permute-start(f32[3,1,6,4096]{3,2,1,0:T(8,128)S(1)} %get-tuple-element.41), channel_id=1, source_target_pairs={{0,1},{2,3},{4,5},{6,7},{8,9},{10,11},{12,13},{14,15},{16,17},{18,... | collective-permute-start | bytes 884744 | tf_op jit(solution)/shard_map/ppermute | solution.py:29
  126.0 5.3 %collective-permute-start.11 = (f32[3,2,1,4096]{3,2,1,0:T(1,128)S(1)}, f32[3,2,1,4096]{3,2,1,0:T(1,128)S(1)}, u32[]{:S(2)}, u32[]{:S(2)}) collective-permute-start(f32[3,2,1,4096]{3,2,1,0:T(1,128)S(1)} %get-tuple-element.77), channel_id=1, source_target_pairs={{0,2},{2,4},{4,6},{6,8},{8,10},{10,12},{12,14},{1,3},{3,5},{5,7},{... | collective-permute-start | bytes 294920 | tf_op jit(solution)/shard_map/ppermute | solution.py:20
  128.7 6.7 %collective-permute-start.12 = (f32[3,2,1,4096]{3,2,1,0:T(1,128)S(1)}, f32[3,2,1,4096]{3,2,1,0:T(1,128)S(1)}, u32[]{:S(2)}, u32[]{:S(2)}) collective-permute-start(f32[3,2,1,4096]{3,2,1,0:T(1,128)S(1)} %get-tuple-element.78), channel_id=1, source_target_pairs={{2,0},{4,2},{6,4},{8,6},{10,8},{12,10},{14,12},{3,1},{5,3},{7,5},{... | collective-permute-start | bytes 294920 | tf_op jit(solution)/shard_map/ppermute | solution.py:21
  135.7 3.6 %collective-permute-start.13 = (f32[3,1,6,4096]{3,2,1,0:T(8,128)S(1)}, f32[3,1,6,4096]{3,2,1,0:T(8,128)S(1)}, u32[]{:S(2)}, u32[]{:S(2)}) collective-permute-start(f32[3,1,6,4096]{3,2,1,0:T(8,128)S(1)} %get-tuple-element.34), channel_id=1, source_target_pairs={{1,0},{3,2},{5,4},{7,6},{9,8},{11,10},{13,12},{15,14},{17,16},{19,... | collective-permute-start | bytes 884744 | tf_op jit(solution)/shard_map/ppermute | solution.py:29
  171.2 4.1 %collective-permute-start.14 = (f32[2,2,1,4096]{3,2,1,0:T(1,128)S(1)}, f32[2,2,1,4096]{3,2,1,0:T(1,128)S(1)}, u32[]{:S(2)}, u32[]{:S(2)}) collective-permute-start(f32[2,2,1,4096]{3,2,1,0:T(1,128)S(1)} %get-tuple-element.75), channel_id=1, source_target_pairs={{0,2},{2,4},{4,6},{6,8},{8,10},{10,12},{12,14},{1,3},{3,5},{5,7},{... | collective-permute-start | bytes 196616 | tf_op jit(solution)/shard_map/ppermute | solution.py:20
  172.5 6.2 %collective-permute-start.15 = (f32[2,2,1,4096]{3,2,1,0:T(1,128)S(1)}, f32[2,2,1,4096]{3,2,1,0:T(1,128)S(1)}, u32[]{:S(2)}, u32[]{:S(2)}) collective-permute-start(f32[2,2,1,4096]{3,2,1,0:T(1,128)S(1)} %get-tuple-element.76), channel_id=1, source_target_pairs={{2,0},{4,2},{6,4},{8,6},{10,8},{12,10},{14,12},{3,1},{5,3},{7,5},{... | collective-permute-start | bytes 196616 | tf_op jit(solution)/shard_map/ppermute | solution.py:21
  178.9 2.4 %collective-permute-start.16 = (f32[2,1,6,4096]{3,2,1,0:T(8,128)S(1)}, f32[2,1,6,4096]{3,2,1,0:T(8,128)S(1)}, u32[]{:S(2)}, u32[]{:S(2)}) collective-permute-start(f32[2,1,6,4096]{3,2,1,0:T(8,128)S(1)} %get-tuple-element.72), channel_id=1, source_target_pairs={{0,1},{2,3},{4,5},{6,7},{8,9},{10,11},{12,13},{14,15},{16,17},{18,... | collective-permute-start | bytes 589832 | tf_op jit(solution)/shard_map/ppermute | solution.py:29
  182.8 0.7 copy-start.3
Sparse Core Ops, SparseCore 0:
  183.7 15.9 all-reduce.32
where the time goes:
time: 209 us; the launch traced here: 208 us
  blocking collectives  89.6 us (43%)
  waiting for transfers between devices  50.6 us (24%)
  starting transfers between devices  35.2 us (17%)
  between operations  14.7 us (7%)
  other arithmetic  13.1 us (6%)
  local copies, waits for them, and re-layouts  4.99 us (2%)
    psum x2, blocking collectives, residual_norms(): return lax.psum(local_sums(residual, residual), ('space', 'day'))  59.9 us
    psum x1, blocking collectives, shards(): curvature = lax.psum(local_sums(direction, applied), ('space', 'day'))  29.7 us
    ppermute x6, starting transfers between devices, padded(): before = lax.ppermute(last, axis, up)  20 us
    psum x1, waiting for transfers between devices, shards(): totals = lax.psum(stacked, 'day')  15.5 us
    ppermute x6, waiting for transfers between devices, padded(): before = lax.ppermute(last, axis, up)  14.2 us
    ppermute x6, waiting for transfers between devices, padded(): after = lax.ppermute(first, axis, down)  13.6 us
    ppermute x6, starting transfers between devices, padded(): after = lax.ppermute(first, axis, down)  7.75 us
    ppermute x5, starting transfers between devices, from_behind(): return lax.ppermute(x, axis, pairs)  7.33 us
  transfers between devices with their start and end apart: 18, of which 15 were waited for; matrix products, arithmetic and copies ran while one was open for 1% of the time, Pallas kernels for 0%

commit v1 on v0

v1 whole, which is shorter than its diff:
```python
import jax
import jax.numpy as jnp
from jax import lax
from jax.sharding import PartitionSpec as P

OFFSETS = ((-1, -1), (-1, 0), (-1, 1), (0, -1), (0, 0), (0, 1), (1, -1), (1, 0), (1, 1))
RIDGE = 1.0
LANES = 128


def send(x, space_of, day_of=lambda d: d):
    spaces, days = lax.axis_size("space"), lax.axis_size("day")
    pairs = []
    for s in range(spaces):
        for d in range(days):
            to_s, to_d = space_of(s), day_of(d)
            if 0 <= to_s < spaces:
                pairs.append((s * days + d, to_s * days + to_d))
    return lax.ppermute(x, ("space", "day"), pairs)


def column_shift(values, col_step):
    if col_step == 0:
        return values
    zero_column = jnp.zeros_like(values[..., :1])
    if col_step > 0:
        return jnp.concatenate([values[..., 1:], zero_column], -1)
    return jnp.concatenate([zero_column, values[..., :-1]], -1)


def forward(values, above, below, coefficients):
    rows = values.shape[-2]
    wide = jnp.concatenate([above[..., None, :], values, below[..., None, :]], -2)
    shifted = {c: column_shift(wide, c) for c in (-1, 0, 1)}
    total = 0.0
    for position, (a, c) in enumerate(OFFSETS):
        total = total + coefficients[position] * shifted[c][..., 1 + a : 1 + a + rows, :]
    return total


def transposed(values, coefficients):
    total = 0.0
    for c in (-1, 0, 1):
        part = 0.0
        for a in (-1, 0, 1):
            product = coefficients[3 * (a + 1) + c + 1] * values
            pad = [(0, 0)] * (values.ndim - 2) + [(1 + a, 1 - a), (0, 0)]
            part = part + jnp.pad(product, pad)
        total = total + column_shift(part, -c)
    return total


def fit_cells(totals):
    diag_first = totals[0] + RIDGE
    cross_term = totals[1]
    diag_second = totals[2] + RIDGE
    determinant = diag_first * diag_second - cross_term * cross_term
    persistence = (diag_second * totals[3] - cross_term * totals[4]) / determinant
    diffusion = (diag_first * totals[4] - cross_term * totals[3]) / determinant
    return jnp.stack([persistence, diffusion], 0)


def shards(observed, gap_mask, sea_mask, stencil, precision, noise_precision, perturbation):
    cols = observed.shape[-1]
    days = lax.axis_size("day")
    spaces = lax.axis_size("space")
    day = lax.axis_index("day")
    half = cols // days
    width = half + LANES
    start = day * (cols - width)
    other_start = (1 - day) * (cols - width)
    own = day * LANES

    def window(x, at=None):
        return lax.dynamic_slice_in_dim(x, start if at is None else at, width, x.ndim - 1)

    sea_all = sea_mask.astype(jnp.float32)
    obs_all = noise_precision * gap_mask.astype(jnp.float32)
    base = sea_all * obs_all * observed
    spread = sea_all * jnp.sqrt(precision + obs_all)
    fields = jnp.stack(
        [base, base + spread * perturbation[0].astype(jnp.float32), base + spread * perturbation[1].astype(jnp.float32), obs_all], 0
    )
    mine = window(fields)
    theirs = send(window(fields, other_start), lambda s: s, lambda d: 1 - d)
    is_first = day == 0
    both = jnp.concatenate([jnp.where(is_first, mine, theirs), jnp.where(is_first, theirs, mine)], 1)
    side, obs = both[:3], both[3]

    sea = window(sea_all)
    prec = window(precision)
    coefficients = window(stencil).astype(jnp.float32)

    def edge(row):
        return jnp.concatenate([side[:, :3, row].reshape(9, width), sea[row][None]], 0)

    above = send(edge(-1), lambda s: s + 1)
    below = send(edge(0), lambda s: s - 1)
    sea_above, sea_below = above[9], below[9]
    above, below = above[:9].reshape(3, 3, width), below[:9].reshape(3, 3, width)

    moved = forward(side[:, :3], above, below, coefficients)
    innovation = jnp.concatenate([side[:, :1], side[:, 1:] - moved], 1)
    weighted = prec * innovation
    scattered = transposed(weighted[:, 1:], coefficients)
    image = weighted + obs * side
    partial = sea * jnp.concatenate([image[:, :3] - scattered[:, :, 1:-1], image[:, 3:]], 1)

    to_above = jnp.stack([partial[:, :3, 0], scattered[:, :, 0]], 0).reshape(18, width)
    to_below = jnp.stack([partial[:, :3, -1], scattered[:, :, -1]], 0).reshape(18, width)
    from_above = send(to_below, lambda s: s + 1).reshape(2, 3, 3, width)
    from_below = send(to_above, lambda s: s - 1).reshape(2, 3, 3, width)
    fixed = jnp.concatenate(
        [
            partial[:, :3, :1] - sea[:1] * from_above[1][:, :, None],
            partial[:, :3, 1:-1],
            partial[:, :3, -1:] - sea[-1:] * from_below[1][:, :, None],
        ],
        2,
    )
    image = jnp.concatenate([fixed, partial[:, 3:]], 1)
    image_above = from_above[0] - sea_above * scattered[:, :, 0]
    image_below = from_below[0] - sea_below * scattered[:, :, -1]

    image_moved = forward(image[:, :3], image_above, image_below, coefficients)
    image_innovation = jnp.concatenate([image[:, :1], image[:, 1:] - image_moved], 1)

    def inner(x):
        return lax.dynamic_slice_in_dim(x, own, half, x.ndim - 1)

    b, z = inner(side), inner(image)

    def sums(x):
        return jnp.sum(x, axis=(1, 2, 3))

    energy = prec * image_innovation * image_innovation + obs * image * image
    scalars = jnp.stack([sums(b * b), sums(b * z), sums(z * z), sums(inner(energy))], 0)
    days_here = image.shape[1] // days
    image_swap = lax.dynamic_slice_in_dim(z[0], (1 - day) * days_here, days_here, 0)
    image_theirs = send(image_swap, lambda s: s, lambda d: 1 - d)

    if spaces & (spaces - 1) == 0:
        scalars = scalars + send(scalars, lambda s: s, lambda d: 1 - d)
        bit = 1
        while bit < spaces:
            scalars = scalars + send(scalars, lambda s: s ^ bit)
            bit *= 2
    else:
        scalars = lax.psum(scalars, ("space", "day"))
    m0, m1, m2, m3 = scalars
    first_step = m0 / m1
    norm_next = first_step * first_step * m2 - m0
    ratio = norm_next / m0
    grown = 1.0 + ratio
    curvature = grown * grown * m1 - 2.0 * first_step * grown * m2 + first_step * first_step * m3
    second_step = norm_next / curvature
    on_side = first_step + second_step * grown
    on_image = -second_step * first_step

    image_mine = lax.dynamic_slice_in_dim(z[0], day * days_here, days_here, 0)
    image_days = jnp.concatenate(
        [jnp.where(is_first, image_mine, image_theirs), jnp.where(is_first, image_theirs, image_mine)], -1
    )
    posterior = on_side[0] * base + on_image[0] * image_days

    def expand(v):
        return v[1:, None, None, None]

    wide_side = jnp.concatenate([above[1:, :, None], side[1:, :3], below[1:, :, None]], 2)
    wide_image = jnp.concatenate([image_above[1:, :, None], image[1:, :3], image_below[1:, :, None]], 2)
    earlier = expand(on_side) * wide_side + expand(on_image) * wide_image
    rows = side.shape[2]
    box = earlier[:, :, :rows] + earlier[:, :, 1 : 1 + rows] + earlier[:, :, 2:]
    centre = earlier[:, :, 1 : 1 + rows]
    box = box + column_shift(box, 1) + column_shift(box, -1)
    laplacian = inner(box - 9.0 * centre)
    centre = inner(centre)
    target = expand(on_side) * b[1:, 1:] + expand(on_image) * z[1:, 1:]
    totals = jnp.stack(
        [
            jnp.sum(centre * centre, axis=(0, 1)),
            jnp.sum(centre * laplacian, axis=(0, 1)),
            jnp.sum(laplacian * laplacian, axis=(0, 1)),
            jnp.sum(centre * target, axis=(0, 1)),
            jnp.sum(laplacian * target, axis=(0, 1)),
        ],
        0,
    )
    return posterior, fit_cells(totals)


def solution(mesh):
    placed = (
        P("day", ("region", "space"), None),
        P("day", ("region", "space"), None),
        P(("region", "space"), None),
        P(None, ("region", "space"), None),
        P(("region", "space"), None),
        P(("region", "space"), None),
        P(None, "day", ("region", "space"), None),
    )
    return jax.shard_map(
        shards,
        mesh=mesh,
        in_specs=placed,
        out_specs=(P("day", ("region", "space"), None), P(None, ("region", "space"), "day")),
        check_vma=False,
    )
```

time: 209 us -> 86.5 us (0.41)
  blocking collectives: 89.6 us -> 0 us
  waiting for transfers between devices: 50.6 us -> 20.8 us
  local copies, waits for them, and re-layouts: 4.99 us -> 30.7 us
  starting transfers between devices: 35.2 us -> 17.7 us
  between operations: 14.7 us -> 1.38 us
    psum x3 -> x0, blocking collectives: 89.6 us -> none  [the longest x2 59.9 us: residual_norms(): return lax.psum(local_sums(residual, residual), ('space', 'day'))]
    ppermute x17 -> x10, starting transfers between devices: 35.1 us -> 17.7 us  [send(): return lax.ppermute(x, ('space', 'day'), pairs)]
    psum x1 -> x0, waiting for transfers between devices: 15.5 us -> none  [shards(): totals = lax.psum(stacked, 'day')]
    ppermute x17 -> x10, waiting for transfers between devices: 35.1 us -> 20.8 us  [send(): return lax.ppermute(x, ('space', 'day'), pairs)]
    unnamed x20 -> x91, local copies, waits for them, and re-layouts: 0.8 us -> 8.23 us
    slice x17 -> x18, local copies, waits for them, and re-layouts: 2.74 us -> 8.83 us  [the longest x2 3.02 us: shards(): sea_above, sea_below = (above[9], below[9])]
    mul x6 -> x4, other arithmetic: 4.5 us -> 0.81 us  [the longest x1 0.53 us: transposed(): product = coefficients[3 * (a + 1) + c + 1] * values]
    broadcast_in_dim x0 -> x2, local copies, waits for them, and re-layouts: none -> 3.06 us  [the longest x1 1.53 us: shards(): below[1:, :, None]]
  transfers between devices with their start and end apart: 18 -> 10, of which waited for: 15 -> 7; matrix products, arithmetic and copies ran while one was open for 1% -> 19% of each run, Pallas kernels for 0% -> 0%
where the time goes in v1:
time: 86.5 us; the launch traced here: 85.5 us
  local copies, waits for them, and re-layouts  30.7 us (35%)
  waiting for transfers between devices  20.8 us (24%)
  starting transfers between devices  17.7 us (20%)
  other arithmetic  15 us (17%)
  between operations  1.38 us (2%)
    ppermute x10, waiting for transfers between devices, send(): return lax.ppermute(x, ('space', 'day'), pairs)  20.8 us
    ppermute x10, starting transfers between devices, send(): return lax.ppermute(x, ('space', 'day'), pairs)  17.7 us
    unnamed x91, local copies, waits for them, and re-layouts  8.23 us
    squeeze x2, local copies, waits for them, and re-layouts, shards(): image_above = from_above[0] - sea_above * scattered[:, :, 0]  3.17 us
    slice x2, local copies, waits for them, and re-layouts, shards(): sea_above, sea_below = (above[9], below[9])  3.02 us
    unnamed x3, other arithmetic  1.85 us
    another operation x3, other arithmetic, shards(): jnp.stack([base, base + spread * perturbation[0].astype(jnp.float32), bas...  1.81 us
  transfers between devices with their start and end apart: 10, of which 7 were waited for; matrix products, arithmetic and copies ran while one was open for 19% of the time, Pallas kernels for 0%

profile of v1, /device:TPU:0, one launch (start us, length us, event | category | flops | bytes accessed | tf_op | source)
XLA Modules:
  0.0 85.5 jit_solution(12432152644782418486)
XLA Ops:
  0.6 0.9 %convert_element_type.33 = f32[4,4096]{1,0:T(4,128)S(1)} convert(s32[4,4096]{1,0:T(4,128)} %param.9) | non-fusion elementwise | flops 16384 | bytes 131072 | tf_op jit(solution)/shard_map/convert_element_type | solution.py:77
  1.6 0.8 copy-done.23
  2.5 1.2 %fusion.52 = (f32[1,2,4,4096]{3,1,0,2:T(2,128)S(1)}, f32[2,4,4096]{2,0,1:T(2,128)S(1)}) fusion(bf16[1,2,4,4096]{3,2,1,0:T(4,128)(2,1)S(1)} %get-tuple-element.82, f32[4,4096]{1,0:T(4,128)S(1)} %copy-done.25, f32[4,4096]{1,0:T(4,128)S(1)} %convert_element_type.33, s32[2,4,4096]{2,1,0:T(4,128)S(1)} %copy-done.23, f32[4,4096]{1,0:T(4,128)S(1)} %copy-done.36, ...), kind=kLoop, calls=%fused_computation.132 | loop fusion | flops 294912 | bytes 786432 | tf_op jit(solution)/shard_map/stack | solution.py:81
  8.0 1.3 %collective-permute-start.2 = (f32[10,2176]{1,0:T(8,128)S(1)}, f32[10,2176]{1,0:T(8,128)S(1)}, u32[]{:S(2)}, u32[]{:S(2)}) collective-permute-start(f32[10,2176]{1,0:T(8,128)S(1)} %pad_maximum_fusion.10), channel_id=1, source_target_pairs={{2,0},{3,1},{4,2},{5,3},{6,4},{7,5},{8,6},{9,7},{10,8},{11,9},{12,... | collective-permute-start | bytes 261128 | tf_op jit(solution)/shard_map/ppermute | solution.py:19
  9.4 5.2 %collective-permute-start.1 = (f32[10,2176]{1,0:T(8,128)S(1)}, f32[10,2176]{1,0:T(8,128)S(1)}, u32[]{:S(2)}, u32[]{:S(2)}) collective-permute-start(f32[10,2176]{1,0:T(8,128)S(1)} %pad_maximum_fusion.9), channel_id=1, source_target_pairs={{0,2},{1,3},{2,4},{3,5},{4,6},{5,7},{6,8},{7,9},{8,10},{9,11},{10,... | collective-permute-start | bytes 261128 | tf_op jit(solution)/shard_map/ppermute | solution.py:19
  15.4 1.4 %collective-permute-done.2 = f32[10,2176]{1,0:T(8,128)S(1)} collective-permute-done((f32[10,2176]{1,0:T(8,128)S(1)}, f32[10,2176]{1,0:T(8,128)S(1)}, u32[]{:S(2)}, u32[]{:S(2)}) %collective-permute-start.2) | collective-permute-done | bytes 87072 | tf_op jit(solution)/shard_map/ppermute | solution.py:19
  16.8 3.1 %collective-permute-done.1 = f32[10,2176]{1,0:T(8,128)S(1)} collective-permute-done((f32[10,2176]{1,0:T(8,128)S(1)}, f32[10,2176]{1,0:T(8,128)S(1)}, u32[]{:S(2)}, u32[]{:S(2)}) %collective-permute-start.1) | collective-permute-done | bytes 87072 | tf_op jit(solution)/shard_map/ppermute | solution.py:19
  21.0 1.0 %fusion.9 = f32[3,3,4,2176]{3,1,0,2:T(4,128)S(1)} fusion(f32[3,3,6,2175]{3,1,0,2:T(4,128)S(1)} %get-tuple-element.42, f32[3,3,6,2175]{3,1,0,2:T(4,128)S(1)} %get-tuple-element.41, f32[4,2,4,2176]{3,1,0,2:T(2,128)S(1)} %get-tuple-element.38, f32[4,2,4,2176]{3,1,0,2:T(2,128)S(1)} %get-tuple-element.37, f32[3,3,1,2176]{3,1,0,2:T(4,128)S(1)} %broadcast_in_dim_reshape.7, ...), kind=kLoop, calls=%fused_computation.42 | loop fusion | flops 1645056 | bytes 2593360 | tf_op jit(solution)/shard_map/sub | solution.py:103
  22.0 1.2 %multiply_add_fusion = (f32[3,4,4,2176]{3,1,0,2:T(4,128)S(1)}, f32[3,4,4,2176]{3,1,0,2:T(4,128)}, f32[3,4,4,2176]{3,1,0,2:T(4,128)S(1)}) fusion(f32[4,4,2176]{2,0,1:T(4,128)S(1)} %fusion.47, f32[4,2,4,2176]{3,1,0,2:T(2,128)S(1)} %get-tuple-element.37, f32[4,2,4,2176]{3,1,0,2:T(2,128)S(1)} %get-tuple-element.38, f32[3,3,4,2176]{3,1,0,2:T(4,128)S(1)} %fusion.9, ...), kind=kLoop, calls=%fused_computation.85 | loop fusion | flops 522240 | bytes 2402304 | tf_op jit(solution)/shard_map/add | solution.py:106
  27.6 1.7 %reshape.176 = f32[18,2176]{1,0:T(8,128)} reshape(f32[2,3,3,2176]{3,2,1,0:T(4,128)} %pad_maximum_fusion.7) | data formatting | bytes 313344 | tf_op jit(solution)/shard_map/reshape | solution.py:110
  29.3 5.2 %collective-permute-start.3 = (f32[18,2176]{1,0:T(8,128)}, f32[18,2176]{1,0:T(8,128)}, u32[]{:S(2)}, u32[]{:S(2)}) collective-permute-start(f32[18,2176]{1,0:T(8,128)} %reshape.176), channel_id=1, source_target_pairs={{0,2},{1,3},{2,4},{3,5},{4,6},{5,7},{6,8},{7,9},{8,10},{9,11},{10,... | collective-permute-start | bytes 470024 | tf_op jit(solution)/shard_map/ppermute | solution.py:19
  34.5 1.5 %slice_reduce_fusion = f32[2176]{0:T(1024)} fusion(f32[10,2176]{1,0:T(8,128)} %copy-done.30), kind=kLoop, calls=%fused_computation.179 | loop fusion | bytes 17408 | tf_op jit(solution)/shard_map/slice | solution.py:99
  37.4 1.5 %broadcast_in_dim.9 = f32[2,3,1,2176]{3,1,0,2:T(4,128)} reshape(f32[6,2176]{1,0:T(8,128)} %slice.406) | data formatting | bytes 104448 | tf_op jit(solution)/shard_map/broadcast_in_dim | solution.py:169
  39.0 1.5 %slice.405 = f32[6,2176]{1,0:T(8,128)} slice(f32[10,2176]{1,0:T(8,128)} %copy-done.32), slice={[3:9], [0:2176]} | slice | bytes 104448 | tf_op jit(solution)/shard_map/slice | solution.py:169
  40.5 1.5 %broadcast_in_dim.8 = f32[2,3,1,2176]{3,1,0,2:T(4,128)} reshape(f32[6,2176]{1,0:T(8,128)} %slice.405) | data formatting | bytes 104448 | tf_op jit(solution)/shard_map/broadcast_in_dim | solution.py:169
  42.0 1.5 %slice_reduce_fusion.1 = f32[2176]{0:T(1024)} fusion(f32[10,2176]{1,0:T(8,128)} %copy-done.32), kind=kLoop, calls=%fused_computation.180 | loop fusion | bytes 17408 | tf_op jit(solution)/shard_map/slice | solution.py:99
  43.5 1.7 %fusion.76 = (f32[9,2176]{1,0:T(8,128)}, f32[9,2176]{1,0:T(8,128)}) fusion(f32[18,2176]{1,0:T(8,128)} %collective-permute-done.3), kind=kLoop, calls=%fused_computation.210 | loop fusion | bytes 313344 | tf_op jit(solution)/shard_map/slice | solution.py:115
  45.2 1.6 %squeeze.30 = f32[3,3,2176]{2,1,0:T(4,128)} reshape(f32[9,2176]{1,0:T(8,128)} %get-tuple-element.76) | data formatting | bytes 156672 | tf_op jit(solution)/shard_map/squeeze | solution.py:122
  46.8 1.6 %squeeze.26 = f32[3,3,1,2176]{3,1,0,2:T(4,128)} reshape(f32[9,2176]{1,0:T(8,128)} %get-tuple-element.76) | data formatting | bytes 156672 | tf_op jit(solution)/shard_map/squeeze | solution.py:122
  48.4 1.6 %broadcast_in_dim_squeeze.4 = f32[3,3,1,2176]{3,1,0,2:T(4,128)} reshape(f32[9,2176]{1,0:T(8,128)} %get-tuple-element.75) | data formatting | bytes 156672 | tf_op jit(solution)/shard_map/broadcast_in_dim;squeeze | solution.py:115
  50.0 1.7 %constant_dynamic-update-slice_fusion.4 = (f32[3,3,6,2176]{3,1,0,2:T(4,128)}, f32[3,3,1,2176]{3,1,0,2:T(4,128)}, f32[3,3,1,2176]{3,1,0,2:T(4,128)S(1)}) fusion(f32[3,3,1,2176]{3,1,0,2:T(4,128)} %squeeze.26, f32[2176]{0:T(1024)} %slice_reduce_fusion.1, f32[3,3,6,2175]{3,1,0,2:T(4,128)S(1)} %get-tuple-element.85, f32[3,3,4,2176]{3,1,0,2:T(4,128)S(1)} %get-tuple-element.57, ...), kind=kLoop, calls=%fused_computation.178 | loop fusion | flops 117503 | bytes 2253904
  53.5 1.5 %collective-permute-start.4 = (f32[18,2176]{1,0:T(8,128)S(1)}, f32[18,2176]{1,0:T(8,128)S(1)}, u32[]{:S(2)}, u32[]{:S(2)}) collective-permute-start(f32[18,2176]{1,0:T(8,128)S(1)} %reshape.177), channel_id=1, source_target_pairs={{2,0},{3,1},{4,2},{5,3},{6,4},{7,5},{8,6},{9,7},{10,8},{11,9},{12,... | collective-permute-start | bytes 470024 | tf_op jit(solution)/shard_map/ppermute | solution.py:19
  55.1 7.2 %collective-permute-done.4 = f32[18,2176]{1,0:T(8,128)S(1)} collective-permute-done((f32[18,2176]{1,0:T(8,128)S(1)}, f32[18,2176]{1,0:T(8,128)S(1)}, u32[]{:S(2)}, u32[]{:S(2)}) %collective-permute-start.4) | collective-permute-done | bytes 156704 | tf_op jit(solution)/shard_map/ppermute | solution.py:19
  66.4 1.1 %fusion.24 = f32[3,3,4,2176]{3,1,0,2:T(4,128)S(1)} fusion(f32[3,3,6,2175]{3,1,0,2:T(4,128)S(1)} %get-tuple-element.40, f32[3,3,6,2175]{3,1,0,2:T(4,128)S(1)} %get-tuple-element.39, f32[3,4,4,2176]{3,1,0,2:T(4,128)S(1)} %pad_maximum_fusion.6, f32[3,3,2,2176]{3,1,0,2:T(4,128)S(1)} %get-tuple-element.49, f32[3,3,1,2176]{3,1,0,2:T(4,128)S(1)} %get-tuple-element.24, ...), kind=kLoop, calls=%fused_computation.57 | loop fusion | flops 1880064 | bytes 2349648 | tf_op jit(solution)/shard_map/sub | solution.py:126
  68.4 1.1 %collective-permute-done.5 = f32[4,3]{1,0:T(4,128)S(1)} collective-permute-done((f32[4,3]{1,0:T(4,128)S(1)}, f32[4,3]{1,0:T(4,128)S(1)}, u32[]{:S(2)}, u32[]{:S(2)}) %collective-permute-start.5) | collective-permute-done | bytes 80 | tf_op jit(solution)/shard_map/ppermute | solution.py:19
  69.6 1.0 %collective-permute-start.6 = (f32[4,3]{1,0:T(4,128)S(1)}, f32[4,3]{1,0:T(4,128)S(1)}, u32[]{:S(2)}, u32[]{:S(2)}) collective-permute-start(f32[4,3]{1,0:T(4,128)S(1)} %fusion.65), channel_id=1, source_target_pairs={{0,2},{1,3},{2,0},{3,1},{4,6},{5,7},{6,4},{7,5},{8,10},{9,11},{10,... | collective-permute-start | bytes 152 | tf_op jit(solution)/shard_map/ppermute | solution.py:19
  70.6 2.6 %collective-permute-done.6 = f32[4,3]{1,0:T(4,128)S(1)} collective-permute-done((f32[4,3]{1,0:T(4,128)S(1)}, f32[4,3]{1,0:T(4,128)S(1)}, u32[]{:S(2)}, u32[]{:S(2)}) %collective-permute-start.6) | collective-permute-done | bytes 80 | tf_op jit(solution)/shard_map/ppermute | solution.py:19
  73.2 0.9 %collective-permute-start.7 = (f32[4,3]{1,0:T(4,128)S(1)}, f32[4,3]{1,0:T(4,128)S(1)}, u32[]{:S(2)}, u32[]{:S(2)}) collective-permute-start(f32[4,3]{1,0:T(4,128)S(1)} %fusion.78), channel_id=1, source_target_pairs={{0,4},{1,5},{2,6},{3,7},{4,0},{5,1},{6,2},{7,3},{8,12},{9,13},{10,... | collective-permute-start | bytes 152 | tf_op jit(solution)/shard_map/ppermute | solution.py:19
  74.2 2.7 %collective-permute-done.7 = f32[4,3]{1,0:T(4,128)S(1)} collective-permute-done((f32[4,3]{1,0:T(4,128)S(1)}, f32[4,3]{1,0:T(4,128)S(1)}, u32[]{:S(2)}, u32[]{:S(2)}) %collective-permute-start.7) | collective-permute-done | bytes 80 | tf_op jit(solution)/shard_map/ppermute | solution.py:19
  76.9 1.9 %collective-permute-start.8 = (f32[4,3]{1,0:T(4,128)S(1)}, f32[4,3]{1,0:T(4,128)S(1)}, u32[]{:S(2)}, u32[]{:S(2)}) collective-permute-start(f32[4,3]{1,0:T(4,128)S(1)} %add.255), channel_id=1, source_target_pairs={{0,8},{1,9},{2,10},{3,11},{4,12},{5,13},{6,14},{7,15},{8,0},{9,1},... | collective-permute-start | bytes 152 | tf_op jit(solution)/shard_map/ppermute | solution.py:19
  78.8 2.6 %collective-permute-done.8 = f32[4,3]{1,0:T(4,128)S(1)} collective-permute-done((f32[4,3]{1,0:T(4,128)S(1)}, f32[4,3]{1,0:T(4,128)S(1)}, u32[]{:S(2)}, u32[]{:S(2)}) %collective-permute-start.8) | collective-permute-done | bytes 80 | tf_op jit(solution)/shard_map/ppermute | solution.py:19
  82.1 0.9 %multiply_reduce_fusion.3 = (f32[4,2048]{1,0:T(4,128)S(1)}, f32[4,2048]{1,0:T(4,128)S(1)}, f32[4,2048]{1,0:T(4,128)S(1)}, f32[4,2048]{1,0:T(4,128)S(1)}, f32[4,2048]{1,0:T(4,128)S(1)}) fusion(f32[2,3,4,2176]{3,1,0,2:T(4,128)S(1)} %get-tuple-element.48, s32[]{:T(128)S(6)} %select_n.51, f32[2,3,4,2175]{3,1,0,2:T(4,128)S(1)} %get-tuple-element.71, ...), kind=kLoop, calls=%fused_computation.104 | loop fusion | flops 794624 | bytes 1367896 | tf_op jit(solution)/shard_map/reduce_sum | solution.py:181
  (169 shorter events, 21.7 us)
Async XLA Ops:
  4.7 1.2 %copy-start.42 = (bf16[9,4,4096]{2,1,0:T(4,128)(2,1)S(1)}, bf16[9,4,4096]{2,1,0:T(4,128)(2,1)}, u32[]{:S(2)}) copy-start(bf16[9,4,4096]{2,1,0:T(4,128)(2,1)} %param.10) | copy-start | bytes 884740
  4.7 2.6 %collective-permute-start = (f32[4,2,4,2176]{3,1,0,2:T(2,128)S(1)}, f32[4,2,4,2176]{3,1,0,2:T(2,128)S(1)}, u32[]{:S(2)}, u32[]{:S(2)}) collective-permute-start(f32[4,2,4,2176]{3,1,0,2:T(2,128)S(1)} %constant_dynamic-slice_fusion.5), channel_id=1, source_target_pairs={{0,1},{1,0},{2,3},{3,2},{4,5},{5,4},{6,7},{7,6},{8,9},{9,8},{10,11... | collective-permute-start | bytes 835592 | tf_op jit(solution)/shard_map/ppermute | solution.py:19
  5.9 17.2 %copy-start.9 = (f32[4,2176]{1,0:T(4,128)}, f32[4,2176]{1,0:T(4,128)S(1)}, u32[]{:S(2)}) copy-start(f32[4,2176]{1,0:T(4,128)S(1)} %get-tuple-element.64) | copy-start | bytes 104452
  6.0 17.2 %copy-start.11 = (f32[4,2176]{1,0:T(4,128)}, f32[4,2176]{1,0:T(4,128)S(1)}, u32[]{:S(2)}) copy-start(f32[4,2176]{1,0:T(4,128)S(1)} %get-tuple-element.65) | copy-start | bytes 104452
  6.0 17.2 %copy-start.13 = (f32[4,2176]{1,0:T(4,128)}, f32[4,2176]{1,0:T(4,128)S(1)}, u32[]{:S(2)}) copy-start(f32[4,2176]{1,0:T(4,128)S(1)} %get-tuple-element.66) | copy-start | bytes 104452
  6.0 17.2 %copy-start.15 = (f32[4,2176]{1,0:T(4,128)}, f32[4,2176]{1,0:T(4,128)S(1)}, u32[]{:S(2)}) copy-start(f32[4,2176]{1,0:T(4,128)S(1)} %get-tuple-element.67) | copy-start | bytes 104452
  6.0 17.2 %copy-start.17 = (f32[4,2176]{1,0:T(4,128)}, f32[4,2176]{1,0:T(4,128)S(1)}, u32[]{:S(2)}) copy-start(f32[4,2176]{1,0:T(4,128)S(1)} %get-tuple-element.68) | copy-start | bytes 104452
  6.0 17.2 %copy-start.19 = (f32[4,2176]{1,0:T(4,128)}, f32[4,2176]{1,0:T(4,128)S(1)}, u32[]{:S(2)}) copy-start(f32[4,2176]{1,0:T(4,128)S(1)} %get-tuple-element.69) | copy-start | bytes 104452
  6.0 17.2 %copy-start.21 = (f32[4,2176]{1,0:T(4,128)}, f32[4,2176]{1,0:T(4,128)S(1)}, u32[]{:S(2)}) copy-start(f32[4,2176]{1,0:T(4,128)S(1)} %get-tuple-element.70) | copy-start | bytes 104452
  8.0 8.7 %collective-permute-start.2 = (f32[10,2176]{1,0:T(8,128)S(1)}, f32[10,2176]{1,0:T(8,128)S(1)}, u32[]{:S(2)}, u32[]{:S(2)}) collective-permute-start(f32[10,2176]{1,0:T(8,128)S(1)} %pad_maximum_fusion.10), channel_id=1, source_target_pairs={{2,0},{3,1},{4,2},{5,3},{6,4},{7,5},{8,6},{9,7},{10,8},{11,9},{12,... | collective-permute-start | bytes 261128 | tf_op jit(solution)/shard_map/ppermute | solution.py:19
  9.4 10.6 %collective-permute-start.1 = (f32[10,2176]{1,0:T(8,128)S(1)}, f32[10,2176]{1,0:T(8,128)S(1)}, u32[]{:S(2)}, u32[]{:S(2)}) collective-permute-start(f32[10,2176]{1,0:T(8,128)S(1)} %pad_maximum_fusion.9), channel_id=1, source_target_pairs={{0,2},{1,3},{2,4},{3,5},{4,6},{5,7},{6,8},{7,9},{8,10},{9,11},{10,... | collective-permute-start | bytes 261128 | tf_op jit(solution)/shard_map/ppermute | solution.py:19
  16.8 3.1 %copy-start.30 = (f32[10,2176]{1,0:T(8,128)}, f32[10,2176]{1,0:T(8,128)S(1)}, u32[]{:S(2)}) copy-start(f32[10,2176]{1,0:T(8,128)S(1)} %collective-permute-done.2) | copy-start | bytes 261124
  24.7 2.2 %copy-start.5 = (f32[3,3,1,2176]{3,1,0,2:T(4,128)}, f32[3,3,1,2176]{3,1,0,2:T(4,128)S(1)}, u32[]{:S(2)}) copy-start(f32[3,3,1,2176]{3,1,0,2:T(4,128)S(1)} %pad_add_fusion.6) | copy-start | bytes 235012
  29.3 7.5 %copy-start.31 = (f32[10,2176]{1,0:T(8,128)S(1)}, f32[10,2176]{1,0:T(8,128)}, u32[]{:S(2)}) copy-start(f32[10,2176]{1,0:T(8,128)} %copy-done.30) | copy-start | bytes 261124
  29.3 14.2 %collective-permute-start.3 = (f32[18,2176]{1,0:T(8,128)}, f32[18,2176]{1,0:T(8,128)}, u32[]{:S(2)}, u32[]{:S(2)}) collective-permute-start(f32[18,2176]{1,0:T(8,128)} %reshape.176), channel_id=1, source_target_pairs={{0,2},{1,3},{2,4},{3,5},{4,6},{5,7},{6,8},{7,9},{8,10},{9,11},{10,... | collective-permute-start | bytes 470024 | tf_op jit(solution)/shard_map/ppermute | solution.py:19
  50.0 2.4 %copy-start.27 = (f32[1,3,3,2176]{3,2,1,0:T(4,128)S(1)}, f32[1,3,3,2176]{3,2,1,0:T(4,128)}, u32[]{:S(2)}) copy-start(f32[1,3,3,2176]{3,2,1,0:T(4,128)} %get-tuple-element.51) | copy-start | bytes 235012
  51.7 1.1 %copy-start = (f32[3,3,6,2176]{3,1,0,2:T(4,128)S(1)}, f32[3,3,6,2176]{3,1,0,2:T(4,128)}, u32[]{:S(2)}) copy-start(f32[3,3,6,2176]{3,1,0,2:T(4,128)} %get-tuple-element.25) | copy-start | bytes 1410052
  53.4 1.6 %copy-start.8 = (f32[3,3,1,2176]{3,1,0,2:T(4,128)S(1)}, f32[3,3,1,2176]{3,1,0,2:T(4,128)}, u32[]{:S(2)}) copy-start(f32[3,3,1,2176]{3,1,0,2:T(4,128)} %copy-done.7) | copy-start | bytes 235012
  53.4 1.6 %copy-start.33 = (f32[3,3,2176]{2,1,0:T(4,128)S(1)}, f32[3,3,2176]{2,1,0:T(4,128)}, u32[]{:S(2)}) copy-start(f32[3,3,2176]{2,1,0:T(4,128)} %squeeze.30) | copy-start | bytes 235012
  53.4 1.6 %copy-start.40 = (f32[2176]{0:T(1024)S(1)}, f32[2176]{0:T(1024)}, u32[]{:S(2)}) copy-start(f32[2176]{0:T(1024)} %slice_reduce_fusion.1) | copy-start | bytes 26116
  53.5 8.7 %collective-permute-start.4 = (f32[18,2176]{1,0:T(8,128)S(1)}, f32[18,2176]{1,0:T(8,128)S(1)}, u32[]{:S(2)}, u32[]{:S(2)}) collective-permute-start(f32[18,2176]{1,0:T(8,128)S(1)} %reshape.177), channel_id=1, source_target_pairs={{2,0},{3,1},{4,2},{5,3},{6,4},{7,5},{8,6},{9,7},{10,8},{11,9},{12,... | collective-permute-start | bytes 470024 | tf_op jit(solution)/shard_map/ppermute | solution.py:19
  64.6 19.2 %collective-permute-start.9 = (f32[2,4,2048]{2,0,1:T(2,128)S(1)}, f32[2,4,2048]{2,0,1:T(2,128)S(1)}, u32[]{:S(2)}, u32[]{:S(2)}) collective-permute-start(f32[2,4,2048]{2,0,1:T(2,128)S(1)} %dynamic-slice_bitcast_fusion), channel_id=1, source_target_pairs={{0,1},{1,0},{2,3},{3,2},{4,5},{5,4},{6,7},{7,6},{8,9},{9,8},{10,11... | collective-permute-start | bytes 196616 | tf_op jit(solution)/shard_map/ppermute | solution.py:19
  66.4 1.1 %slice-start = ((f32[3,3,4,2176]{3,1,0,2:T(4,128)}), f32[3,1,4,2176]{3,1,0,2:T(1,128)S(1)}, s32[]{:S(2)}) async-start(f32[3,3,4,2176]{3,1,0,2:T(4,128)} %copy-done.4), calls=%async_computation | async-start | bytes 208896 | tf_op jit(solution)/shard_map/slice | solution.py:126
  66.4 1.1 %copy-start.24 = (f32[4,4,2048]{2,0,1:T(4,128)S(1)}, f32[4,4,2048]{2,0,1:T(4,128)}, u32[]{:S(2)}) copy-start(f32[4,4,2048]{2,0,1:T(4,128)} %constant_dynamic-slice_fusion) | copy-start | bytes 393220
  66.4 1.1 %copy-start.38 = (f32[4,2048]{1,0:T(4,128)S(1)}, f32[4,2048]{1,0:T(4,128)}, u32[]{:S(2)}) copy-start(f32[4,2048]{1,0:T(4,128)} %constant_dynamic-slice_fusion.1) | copy-start | bytes 98308
  67.6 14.0 %copy-start.34 = (f32[2,3,1,2176]{3,1,0,2:T(4,128)S(1)}, f32[2,3,1,2176]{3,1,0,2:T(4,128)}, u32[]{:S(2)}) copy-start(f32[2,3,1,2176]{3,1,0,2:T(4,128)} %broadcast_in_dim.9) | copy-start | bytes 156676
  67.6 14.0 %copy-start.35 = (f32[2,3,1,2176]{3,1,0,2:T(4,128)S(1)}, f32[2,3,1,2176]{3,1,0,2:T(4,128)}, u32[]{:S(2)}) copy-start(f32[2,3,1,2176]{3,1,0,2:T(4,128)} %broadcast_in_dim.8) | copy-start | bytes 156676
  68.3 13.3 %slice-start.1 = ((f32[3,3,4,2176]{3,1,0,2:T(4,128)}), f32[2,3,4,2176]{3,1,0,2:T(4,128)S(1)}, s32[]{:S(2)}) async-start(f32[3,3,4,2176]{3,1,0,2:T(4,128)} %copy-done.4), calls=%async_computation.1 | async-start | bytes 557056 | tf_op jit(solution)/shard_map/slice | solution.py:170
  68.3 1.2 %collective-permute-start.5 = (f32[4,3]{1,0:T(4,128)S(1)}, f32[4,3]{1,0:T(4,128)S(1)}, u32[]{:S(2)}, u32[]{:S(2)}) collective-permute-start(f32[4,3]{1,0:T(4,128)S(1)} %pad_maximum_fusion.12), channel_id=1, source_target_pairs={{0,1},{1,0},{2,3},{3,2},{4,5},{5,4},{6,7},{7,6},{8,9},{9,8},{10,11... | collective-permute-start | bytes 152 | tf_op jit(solution)/shard_map/ppermute | solution.py:19
  69.6 3.7 %collective-permute-start.6 = (f32[4,3]{1,0:T(4,128)S(1)}, f32[4,3]{1,0:T(4,128)S(1)}, u32[]{:S(2)}, u32[]{:S(2)}) collective-permute-start(f32[4,3]{1,0:T(4,128)S(1)} %fusion.65), channel_id=1, source_target_pairs={{0,2},{1,3},{2,0},{3,1},{4,6},{5,7},{6,4},{7,5},{8,10},{9,11},{10,... | collective-permute-start | bytes 152 | tf_op jit(solution)/shard_map/ppermute | solution.py:19
  73.2 3.7 %collective-permute-start.7 = (f32[4,3]{1,0:T(4,128)S(1)}, f32[4,3]{1,0:T(4,128)S(1)}, u32[]{:S(2)}, u32[]{:S(2)}) collective-permute-start(f32[4,3]{1,0:T(4,128)S(1)} %fusion.78), channel_id=1, source_target_pairs={{0,4},{1,5},{2,6},{3,7},{4,0},{5,1},{6,2},{7,3},{8,12},{9,13},{10,... | collective-permute-start | bytes 152 | tf_op jit(solution)/shard_map/ppermute | solution.py:19
  76.9 4.5 %collective-permute-start.8 = (f32[4,3]{1,0:T(4,128)S(1)}, f32[4,3]{1,0:T(4,128)S(1)}, u32[]{:S(2)}, u32[]{:S(2)}) collective-permute-start(f32[4,3]{1,0:T(4,128)S(1)} %add.255), channel_id=1, source_target_pairs={{0,8},{1,9},{2,10},{3,11},{4,12},{5,13},{6,14},{7,15},{8,0},{9,1},... | collective-permute-start | bytes 152 | tf_op jit(solution)/shard_map/ppermute | solution.py:19
  (25 other events, 21.0 us)

commit v2 on v1

v2 whole, which is shorter than its diff:
```python
import jax
import jax.numpy as jnp
from jax import lax
from jax.experimental import pallas as pl
from jax.experimental.pallas import tpu as pltpu
from jax.sharding import PartitionSpec as P

RIDGE = 1.0
LANES = 128
FIELDS = 3
F32 = jnp.float32

M_PLANE, T_PLANE, Q_PLANE, H_PLANE, PLANES = 0, 9, 18, 21, 24


def send(x, space_of, day_of=lambda d: d):
    spaces, days = lax.axis_size("space"), lax.axis_size("day")
    pairs = []
    for s in range(spaces):
        for d in range(days):
            to_s, to_d = space_of(s), day_of(d)
            if 0 <= to_s < spaces:
                pairs.append((s * days + d, to_s * days + to_d))
    return lax.ppermute(x, ("space", "day"), pairs)


def position(axis):
    return lax.broadcasted_iota(jnp.int32, (8, LANES), axis)


def rolled(x, step, axis):
    return pltpu.roll(x, step % x.shape[axis], axis)


def tile(t):
    return pl.ds(t * LANES, LANES)


def dynamic_tile(start, t):
    return pl.ds(pl.multiple_of(start + t * LANES, LANES), LANES)


def doubled(x):
    return jnp.concatenate([x, x], 0)


class Shift:
    def __init__(self, step):
        self.step, self.edge, self.tiles = step, (0 if step > 0 else LANES - 1), []

    def push(self, x):
        self.tiles.append(rolled(x, self.step, 1))

    def take(self, t):
        beside = t - self.step
        here = self.tiles[t]
        other = self.tiles[beside] if 0 <= beside < len(self.tiles) else jnp.zeros_like(here)
        return jnp.where(position(1) == self.edge, other, here)


def right_sides_kernel(observed, gap, sea, precision, noise, perturbation, mine, give):
    day = lax.axis_index("day")
    tiles = mine.shape[-1] // LANES
    reach = observed.shape[-1] - mine.shape[-1]
    for out, side in ((mine, day), (give, 1 - day)):
        start = side * reach
        for t in range(tiles):
            at = dynamic_tile(start, t)
            both = lambda ref, *lead: jnp.concatenate([ref[(*lead, 0, slice(None), at)], ref[(*lead, 1, slice(None), at)]], 0)
            wet = doubled(sea[:, at].astype(F32))
            seen = doubled(noise[:, at]) * both(gap).astype(F32)
            base = wet * seen * both(observed)
            spread = wet * jnp.sqrt(doubled(precision[:, at]) + seen)
            out[0, :, tile(t)] = base
            out[1, :, tile(t)] = base + spread * both(perturbation, 0).astype(F32)
            out[2, :, tile(t)] = base + spread * both(perturbation, 1).astype(F32)
            out[3, :, tile(t)] = seen


def coefficients_kernel(stencil, sea, precision, planes, cells):
    day = lax.axis_index("day")
    width = planes.shape[-1]
    tiles = width // LANES
    start = day * (stencil.shape[-1] - width)
    row = position(0) % 4
    shifts = {(a, c): Shift(c) for a in (-1, 0, 1) for c in (-1, 1)}
    for t in range(tiles + 1):
        if t < tiles:
            at = dynamic_tile(start, t)
            cells[0, :, tile(t)] = doubled(sea[:, at].astype(F32))
            cells[1, :, tile(t)] = doubled(precision[:, at])
            own = {}
            for a in (-1, 0, 1):
                for c in (-1, 0, 1):
                    k = 3 * (a + 1) + c + 1
                    s = doubled(stencil[k, :, at].astype(F32))
                    own[a, c] = s
                    moved = s if a == 0 else jnp.where(row == (0 if a > 0 else 3), 0.0, rolled(s, a, 0))
                    planes[T_PLANE + k, :, tile(t)] = moved
                    if c == 0:
                        planes[M_PLANE + k, :, tile(t)] = s
                    else:
                        shifts[a, c].push(s)
            for c in (-1, 0, 1):
                planes[Q_PLANE + c + 1, :, tile(t)] = jnp.where(row == 0, own[-1, c], jnp.where(row == 3, own[1, c], 0.0))
            planes[H_PLANE + 1, :, tile(t)] = jnp.where(row == 0, own[-1, 0], jnp.where(row == 3, own[1, 0], 0.0))
        if t >= 1:
            for c in (-1, 1):
                got = {}
                for a in (-1, 0, 1):
                    got[a] = shifts[a, c].take(t - 1)
                    planes[M_PLANE + 3 * (a + 1) + c + 1, :, tile(t - 1)] = got[a]
                planes[H_PLANE + c + 1, :, tile(t - 1)] = jnp.where(row == 0, got[-1], jnp.where(row == 3, got[1], 0.0))


def edges_kernel(mine, got, cells, to_below, to_above):
    day = lax.axis_index("day")
    for which in (0, 1):
        early, late = ((mine, got), (got, mine))[which]

        @pl.when(day == which)
        def _():
            for out, r in ((to_below, 3), (to_above, 0)):
                for f in range(FIELDS):
                    out[3 * f, :, :] = early[f, r : r + 1, :]
                    out[3 * f + 1, :, :] = early[f, 4 + r : 5 + r, :]
                    out[3 * f + 2, :, :] = late[f, r : r + 1, :]

    to_below[9, :, :] = cells[0, 3:4, :]
    to_above[9, :, :] = cells[0, 0:1, :]


def apply_rows(planes, at, base, terms):
    sums = []
    for c in (0, 1, 2):
        total = planes[base + c, :, at] * terms[0]
        total = total + planes[base + 3 + c, :, at] * terms[1]
        total = total + planes[base + 6 + c, :, at] * terms[2]
        sums.append(total)
    return sums


def inside_kernel(mine, got, planes, pairs, moved):
    day = lax.axis_index("day")
    tiles = mine.shape[-1] // LANES
    row = position(0) % 4
    first = day == 0
    for f in range(FIELDS + 1):
        for half in (0, 1):
            shifts = (Shift(1), Shift(-1))
            middle = []
            for t in range(tiles + 1):
                if t < tiles:
                    x, y = mine[f, :, tile(t)], got[f, :, tile(t)]
                    u = jnp.where(first, x, y) if half == 0 else jnp.where(first, y, x)
                    pairs[half, f, :, tile(t)] = u
                    if f < FIELDS:
                        up = jnp.where(row == 0, 0.0, rolled(u, 1, 0))
                        down = jnp.where(row == 3, 0.0, rolled(u, -1, 0))
                        left, centre, right = apply_rows(planes, tile(t), M_PLANE, (up, u, down))
                        shifts[0].push(left)
                        shifts[1].push(right)
                        middle.append(centre)
                if t >= 1 and f < FIELDS:
                    moved[half, f, :, tile(t - 1)] = middle[t - 1] + shifts[0].take(t - 1) + shifts[1].take(t - 1)


def placed(above, below, index, at):
    row = position(0)
    spread = lambda ref, k: jnp.broadcast_to(ref[k, :, at], (8, LANES))
    first, second = index
    out = jnp.where(row < 2, spread(above, first), spread(below, first))
    if second is not None:
        late = jnp.where(row < 6, spread(above, second), spread(below, second))
        out = jnp.where(row < 4, out, late)
    return out


def split_rows(below, above, plane, x, at, first, second):
    if first is not None:
        above[plane + first, :, at] = x[0:1]
        below[plane + first, :, at] = x[3:4]
    if second is not None:
        above[plane + second, :, at] = x[4:5]
        below[plane + second, :, at] = x[7:8]


def image_kernel(pairs, moved, planes, cells, above, below, image, rims, to_below, to_above):
    tiles = moved.shape[-1] // LANES
    row = position(0)
    low = row < 4
    for f in range(FIELDS):
        incoming = [(Shift(1), Shift(-1)) for _ in (0, 1)]
        scatter = [(Shift(-1), Shift(1)) for _ in (0, 1)]
        leaving = [(Shift(-1), Shift(1)) for _ in (0, 1)]
        kept = {}
        for t in range(tiles + 2):
            if t < tiles:
                at = tile(t)
                for half in (0, 1):
                    rim = placed(above, below, (3 * f, 3 * f + 1) if half == 0 else (3 * f + 2, None), at)
                    if f > 0:
                        rims[half, f - 1, :, at] = rim
                    incoming[half][0].push(planes[H_PLANE, :, at] * rim)
                    kept["in", half, t] = planes[H_PLANE + 1, :, at] * rim
                    incoming[half][1].push(planes[H_PLANE + 2, :, at] * rim)
            if 1 <= t <= tiles:
                q = t - 1
                at = tile(q)
                m = [
                    moved[half, f, :, at] + kept.pop(("in", half, q)) + incoming[half][0].take(q) + incoming[half][1].take(q)
                    for half in (0, 1)
                ]
                before = (jnp.where(low, 0.0, rolled(m[0], 4, 0)), rolled(jnp.where(low, m[1], m[0]), 4, 0))
                for half in (0, 1):
                    u = pairs[half, f, :, at]
                    w = cells[1, :, at] * (u - before[half])
                    left, centre, right = apply_rows(planes, at, T_PLANE, (rolled(w, -1, 0), w, rolled(w, 1, 0)))
                    scatter[half][0].push(left)
                    scatter[half][1].push(right)
                    leaving[half][0].push(planes[Q_PLANE, :, at] * w)
                    leaving[half][1].push(planes[Q_PLANE + 2, :, at] * w)
                    kept[half, q] = (w + pairs[half, FIELDS, :, at] * u, centre, planes[Q_PLANE + 1, :, at] * w)
            if t >= 2:
                q = t - 2
                at = tile(q)
                s, out = [], []
                for half in (0, 1):
                    own, centre, edge = kept.pop((half, q))
                    s.append(centre + scatter[half][0].take(q) + scatter[half][1].take(q))
                    out.append(edge + leaving[half][0].take(q) + leaving[half][1].take(q))
                    kept["own", half] = own
                after = (rolled(jnp.where(low, s[1], s[0]), 4, 0), jnp.where(low, rolled(s[1], 4, 0), 0.0))
                for half in (0, 1):
                    z = cells[0, :, at] * (kept.pop(("own", half)) - after[half])
                    image[half, f, :, at] = z
                    split_rows(to_below, to_above, 0, z, at, 3 * f + 2 * half, 3 * f + 1 if half == 0 else None)
                split_rows(to_below, to_above, 9, out[0], at, None, 3 * f)
                split_rows(to_below, to_above, 9, out[1], at, 3 * f + 1, 3 * f + 2)


def sums_kernel(pairs, part, planes, cells, sea_above, sea_below, to_below, to_above, above, below, image, rims, swap):
    day = lax.axis_index("day")
    tiles = part.shape[-1] // LANES
    row = position(0)
    low = row < 4
    edge = (row % 4 == 0) | (row % 4 == 3)
    rows = []
    for f in range(FIELDS):
        shifts = [(Shift(1), Shift(-1)) for _ in (0, 1)]
        kept = {}
        totals = [None] * 4
        for t in range(tiles + 1):
            if t < tiles:
                at = tile(t)
                wet = cells[0, :, at]
                wet_rim = placed(sea_above, sea_below, (9, 9), at)
                for half in (0, 1):
                    days = (3 * f, 3 * f + 1) if half == 0 else (3 * f + 2, None)
                    late = tuple(None if k is None else 9 + k for k in days)
                    came = placed(above, below, late, at)
                    keep = edge if half == 0 else edge & low
                    z = part[half, f, :, at] - jnp.where(keep, wet * came, 0.0)
                    rim = placed(above, below, days, at) - wet_rim * placed(to_above, to_below, late, at)
                    image[half, f, :, at] = z
                    if f > 0:
                        rims[half, f - 1, :, at] = rim
                    up = jnp.where(row % 4 == 0, rim, rolled(z, 1, 0))
                    down = jnp.where(row % 4 == 3, rim, rolled(z, -1, 0))
                    left, centre, right = apply_rows(planes, at, M_PLANE, (up, z, down))
                    shifts[half][0].push(left)
                    shifts[half][1].push(right)
                    kept[half, t] = (z, centre)
            if t >= 1:
                q = t - 1
                at = tile(q)
                z, m = [], []
                for half in (0, 1):
                    own, centre = kept.pop((half, q))
                    z.append(own)
                    m.append(centre + shifts[half][0].take(q) + shifts[half][1].take(q))
                before = (jnp.where(low, 0.0, rolled(m[0], 4, 0)), rolled(jnp.where(low, m[1], m[0]), 4, 0))
                terms = [0.0] * 4
                for half in (0, 1):
                    b = pairs[half, f, :, at]
                    gap = z[half] - before[half]
                    terms[0] = terms[0] + b * b
                    terms[1] = terms[1] + b * z[half]
                    terms[2] = terms[2] + z[half] * z[half]
                    terms[3] = terms[3] + (cells[1, :, at] * gap * gap + pairs[half, FIELDS, :, at] * z[half] * z[half])
                if q == 0:
                    terms = [jnp.where(day == 0, x, 0.0) for x in terms]
                elif q == tiles - 1:
                    terms = [jnp.where(day == 0, 0.0, x) for x in terms]
                totals = [x if y is None else x + y for x, y in zip(terms, totals)]
        rows += [jnp.sum(x, axis=0, keepdims=True) for x in totals]
    for k, x in enumerate(rows):
        swap[tiles - 1 + k // 8, k % 8 : k % 8 + 1, :] = x
    swap[tiles, 4:8, :] = jnp.zeros((4, LANES), F32)
    for which in (0, 1):

        @pl.when(day == which)
        def _():
            for t in range(tiles - 1):
                swap[t, :, :] = image[1 - which, 0, :, tile(t + which)]


def fit_kernel(scalars, mine, give, pairs, image, theirs, side_rims, image_rims, posterior, fitted):
    day = lax.axis_index("day")
    tiles = mine.shape[-1] // LANES
    row = position(0)
    low = row < 4
    weights = []
    for f in range(FIELDS):
        m = []
        for k in range(4 * f, 4 * f + 4):
            total = jnp.sum(scalars[k // 8, k % 8 : k % 8 + 1, :], axis=1, keepdims=True)
            m.append(jnp.broadcast_to(total, (8, LANES)))
        step = m[0] / m[1]
        norm_next = step * step * m[2] - m[0]
        grown = 1.0 + norm_next / m[0]
        curvature = grown * grown * m[1] - 2.0 * step * grown * m[2] + step * step * m[3]
        second = norm_next / curvature
        weights.append((step + second * grown, -second * step))

    def store(at, x):
        posterior[0, :, at] = x[0:4]
        posterior[1, :, at] = x[4:8]

    on_side, on_image = weights[0]
    for which in (0, 1):

        @pl.when(day == which)
        def _():
            for t in range(tiles - 1):
                here, there = which * (tiles - 1), (1 - which) * (tiles - 1)
                own = on_side * mine[0, :, tile(t + which)] + on_image * image[which, 0, :, tile(t + which)]
                store(tile(here + t), own)
                store(tile(there + t), on_side * give[0, :, tile(t + 1 - which)] + on_image * theirs[t, :, :])

    wide = {(f, half): (Shift(1), Shift(-1)) for f in (1, 2) for half in (0, 1)}
    kept = {}
    for t in range(tiles + 1):
        if t < tiles:
            at = tile(t)
            for f in (1, 2):
                on_side, on_image = weights[f]
                for half in (0, 1):
                    x = on_side * pairs[half, f, :, at] + on_image * image[half, f, :, at]
                    rim = on_side * side_rims[half, f - 1, :, at] + on_image * image_rims[half, f - 1, :, at]
                    up = jnp.where(row % 4 == 0, rim, rolled(x, 1, 0))
                    down = jnp.where(row % 4 == 3, rim, rolled(x, -1, 0))
                    box = x + up + down
                    wide[f, half][0].push(box)
                    wide[f, half][1].push(box)
                    kept[f, half, t] = (x, box)
        if t >= 1:
            q = t - 1
            totals = [0.0] * 5
            for f in (1, 2):
                (x0, box0), (x1, box1) = kept.pop((f, 0, q)), kept.pop((f, 1, q))
                targets = (rolled(jnp.where(low, x1, x0), 4, 0), rolled(x1, 4, 0))
                for half, (x, box) in enumerate(((x0, box0), (x1, box1))):
                    lap = box + wide[f, half][0].take(q) + wide[f, half][1].take(q) - 9.0 * x
                    if half == 1:
                        x, lap = jnp.where(low, x, 0.0), jnp.where(low, lap, 0.0)
                    target = targets[half]
                    for k, term in enumerate((x * x, x * lap, lap * lap, x * target, lap * target)):
                        totals[k] = totals[k] + term
            m = [x + rolled(x, 4, 0) for x in totals]
            first, second = m[0] + RIDGE, m[2] + RIDGE
            inverse = 1.0 / (first * second - m[1] * m[1])
            persistence = (second * m[3] - m[1] * m[4]) * inverse
            diffusion = (first * m[4] - m[1] * m[3]) * inverse

            def write(to):
                fitted[0, :, tile(to)] = persistence[0:4]
                fitted[1, :, tile(to)] = diffusion[0:4]

            if q < tiles - 1:
                pl.when(day == 0)(lambda: write(q))
            if q > 0:
                pl.when(day == 1)(lambda: write(q - 1))


def call(kernel, outs, *args, flops=2_000_000):
    vmem = pl.BlockSpec(memory_space=pltpu.VMEM)
    size = sum(x.size * x.dtype.itemsize for x in args)
    return pl.pallas_call(
        kernel,
        out_shape=[jax.ShapeDtypeStruct(s, F32) for s in outs],
        in_specs=[vmem] * len(args),
        out_specs=[vmem] * len(outs),
        cost_estimate=pl.CostEstimate(flops=flops, bytes_accessed=size, transcendentals=0),
        compiler_params=pltpu.CompilerParams(vmem_limit_bytes=32 << 20),
    )(*args)


def shards(observed, gap_mask, sea_mask, stencil, precision, noise_precision, perturbation):
    cols = observed.shape[-1]
    spaces = lax.axis_size("space")
    half = cols // 2
    width = half + LANES
    tiles = width // LANES
    pair = (8, width)

    mine, give = call(
        right_sides_kernel, [(4, *pair)] * 2, observed, gap_mask, sea_mask, precision, noise_precision, perturbation
    )
    got = send(give, lambda s: s, lambda d: 1 - d)
    planes, cells = call(coefficients_kernel, [(PLANES, *pair), (2, *pair)], stencil, sea_mask, precision)
    to_below, to_above = call(edges_kernel, [(10, 1, width)] * 2, mine, got, cells)
    above = send(to_below, lambda s: s + 1)
    below = send(to_above, lambda s: s - 1)
    pairs, moved = call(inside_kernel, [(2, 4, *pair), (2, 3, *pair)], mine, got, planes)
    part, side_rims, to_below, to_above = call(
        image_kernel, [(2, 3, *pair), (2, 2, *pair), (18, 1, width), (18, 1, width)], pairs, moved, planes, cells, above, below
    )
    from_above = send(to_below, lambda s: s + 1)
    from_below = send(to_above, lambda s: s - 1)
    image, image_rims, swap = call(
        sums_kernel,
        [(2, 3, *pair), (2, 2, *pair), (tiles + 1, 8, LANES)],
        pairs, part, planes, cells, above, below, to_below, to_above, from_above, from_below,
    )
    theirs = send(swap, lambda s: s, lambda d: 1 - d)
    scalars = swap[tiles - 1 :]
    if spaces & (spaces - 1) == 0:
        scalars = scalars + theirs[tiles - 1 :]
        bit = 1
        while bit < spaces:
            scalars = scalars + send(scalars, lambda s: s ^ bit)
            bit *= 2
    else:
        scalars = lax.psum(scalars, ("space", "day"))
    posterior, fitted = call(
        fit_kernel,
        [observed.shape, (2, observed.shape[1], half)],
        scalars, mine, give, pairs, image, theirs, side_rims, image_rims,
    )
    return posterior, fitted


def solution(mesh):
    placed_args = (
        P("day", ("region", "space"), None),
        P("day", ("region", "space"), None),
        P(("region", "space"), None),
        P(None, ("region", "space"), None),
        P(("region", "space"), None),
        P(("region", "space"), None),
        P(None, "day", ("region", "space"), None),
    )
    return jax.shard_map(
        shards,
        mesh=mesh,
        in_specs=placed_args,
        out_specs=(P("day", ("region", "space"), None), P(None, ("region", "space"), "day")),
        check_vma=False,
    )
```

time: 86.5 us -> 50.7 us (0.59)
  local copies, waits for them, and re-layouts: 30.7 us -> 6.18 us
  other arithmetic: 15 us -> 0.01 us
  Pallas kernels: 0 us -> 7.42 us
  waiting for transfers between devices: 20.8 us -> 18 us
    slice x21 -> x0, local copies, waits for them, and re-layouts: 9.87 us -> none  [the longest x2 3.02 us: shards(): sea_above, sea_below = (above[9], below[9])]
    pallas_call x0 -> x7, Pallas kernels: none -> 7.42 us  [call(): pl.pallas_call(kernel, out_shape=[jax.ShapeDtypeStruct(s, F32) for s in o...]
    another operation x7 -> x0, other arithmetic: 3.24 us -> none  [the longest x3 1.81 us: shards(): jnp.stack([base, base + spread * perturbation[0].astype(jnp.float32), bas...]
    squeeze x4 -> x0, local copies, waits for them, and re-layouts: 3.24 us -> none  [the longest x2 3.17 us: shards(): image_above = from_above[0] - sea_above * scattered[:, :, 0]]
    broadcast_in_dim x2 -> x0, local copies, waits for them, and re-layouts: 3.06 us -> none  [the longest x1 1.53 us: shards(): below[1:, :, None]]
    add x9 -> x1, other arithmetic: 2.96 us -> 0.01 us  [shards(): scalars = scalars + theirs[tiles - 1:]]
    ppermute x10 -> x9, waiting for transfers between devices: 20.8 us -> 18 us  [send(): return lax.ppermute(x, ('space', 'day'), pairs)]
    another operation x7 -> x0, local copies, waits for them, and re-layouts: 2.43 us -> none  [the longest x1 1.58 us: shards(): from_above[1][:, :, None]]
  transfers between devices with their start and end apart: 10 -> 9, of which waited for: 7 -> 8; matrix products, arithmetic and copies ran while one was open for 19% -> 0% of each run, Pallas kernels for 0% -> 1%
where the time goes in v2:
time: 50.7 us; the launch traced here: 50.3 us
  waiting for transfers between devices  18 us (36%)
  starting transfers between devices  17.9 us (35%)
  Pallas kernels  7.42 us (15%)
  local copies, waits for them, and re-layouts  6.18 us (12%)
  between operations  0.73 us (1%)
    ppermute x9, waiting for transfers between devices, send(): return lax.ppermute(x, ('space', 'day'), pairs)  18 us
    ppermute x9, starting transfers between devices, send(): return lax.ppermute(x, ('space', 'day'), pairs)  17.9 us
    pallas_call x7, Pallas kernels, call(): pl.pallas_call(kernel, out_shape=[jax.ShapeDtypeStruct(s, F32) for s in o...  7.42 us
    unnamed x14, local copies, waits for them, and re-layouts  6.18 us
  transfers between devices with their start and end apart: 9, of which 8 were waited for; matrix products, arithmetic and copies ran while one was open for 0% of the time, Pallas kernels for 1%

profile of v2, /device:TPU:0, one launch (start us, length us, event | category | flops | bytes accessed | tf_op | source)
XLA Modules:
  0.0 50.3 jit_solution(16786945540828950993)
XLA Ops:
  0.6 0.0 copy-start.1
  0.6 0.8 %copy-done.1 = s32[4,4096]{1,0:T(4,128)S(1)} copy-done((s32[4,4096]{1,0:T(4,128)S(1)}, s32[4,4096]{1,0:T(4,128)}, u32[]{:S(2)}) %copy-start.1) | copy-done | bytes 65560
  1.5 0.8 %copy-done.2 = f32[4,4096]{1,0:T(4,128)S(1)} copy-done((f32[4,4096]{1,0:T(4,128)S(1)}, f32[4,4096]{1,0:T(4,128)}, u32[]{:S(2)}) %copy-start.2) | copy-done | bytes 65560
  2.3 0.9 %copy-done.3 = f32[2,4,4096]{2,1,0:T(4,128)S(1)} copy-done((f32[2,4,4096]{2,1,0:T(4,128)S(1)}, f32[2,4,4096]{2,1,0:T(4,128)}, u32[]{:S(2)}) %copy-start.3) | copy-done | bytes 131096
  3.2 0.9 %copy-done.4 = s32[2,4,4096]{2,1,0:T(4,128)S(1)} copy-done((s32[2,4,4096]{2,1,0:T(4,128)S(1)}, s32[2,4,4096]{2,1,0:T(4,128)}, u32[]{:S(2)}) %copy-start.4) | copy-done | bytes 131096
  4.1 0.9 %copy-done.5 = bf16[2,2,4,4096]{3,2,1,0:T(4,128)(2,1)S(1)} copy-done((bf16[2,2,4,4096]{3,2,1,0:T(4,128)(2,1)S(1)}, bf16[2,2,4,4096]{3,2,1,0:T(4,128)(2,1)}, u32[]{:S(2)}) %copy-start.5) | copy-done | bytes 131096
  5.0 0.8 %copy-done.6 = f32[4,4096]{1,0:T(4,128)S(1)} copy-done((f32[4,4096]{1,0:T(4,128)S(1)}, f32[4,4096]{1,0:T(4,128)}, u32[]{:S(2)}) %copy-start.6) | copy-done | bytes 65560
  5.9 0.2 shard_map.86
  6.1 0.5 %collective-permute-start = (f32[4,8,2176]{2,1,0:T(8,128)S(1)}, f32[4,8,2176]{2,1,0:T(8,128)S(1)}, u32[]{:S(2)}, u32[]{:S(2)}) collective-permute-start(f32[4,8,2176]{2,1,0:T(8,128)S(1)} %get-tuple-element.18.give), channel_id=1, source_target_pairs={{0,1},{1,0},{2,3},{3,2},{4,5},{5,4},{6,7},{7,6},{8,9},{9,8},{10,11... | collective-permute-start | bytes 835592 | tf_op jit(solution)/shard_map/ppermute | solution.py:24
  6.6 1.0 %copy-done = bf16[9,4,4096]{2,1,0:T(4,128)(2,1)S(1)} copy-done((bf16[9,4,4096]{2,1,0:T(4,128)(2,1)S(1)}, bf16[9,4,4096]{2,1,0:T(4,128)(2,1)}, u32[]{:S(2)}) %copy-start) | copy-done | bytes 294936
  7.6 0.2 shard_map.87
  7.8 0.0 collective-permute-done.got
  7.8 4.8 %collective-permute-start.1 = (f32[10,1,2176]{2,1,0:T(1,128)S(1)}, f32[10,1,2176]{2,1,0:T(1,128)S(1)}, u32[]{:S(2)}, u32[]{:S(2)}) collective-permute-start(f32[10,1,2176]{2,1,0:T(1,128)S(1)} %get-tuple-element.23), channel_id=1, source_target_pairs={{0,2},{1,3},{2,4},{3,5},{4,6},{5,7},{6,8},{7,9},{8,10},{9,11},{10,... | collective-permute-start | bytes 261128 | tf_op jit(solution)/shard_map/ppermute | solution.py:24
  12.6 1.3 %collective-permute-start.2 = (f32[10,1,2176]{2,1,0:T(1,128)S(1)}, f32[10,1,2176]{2,1,0:T(1,128)S(1)}, u32[]{:S(2)}, u32[]{:S(2)}) collective-permute-start(f32[10,1,2176]{2,1,0:T(1,128)S(1)} %get-tuple-element.24), channel_id=1, source_target_pairs={{2,0},{3,1},{4,2},{5,3},{6,4},{7,5},{8,6},{9,7},{10,8},{11,9},{12,... | collective-permute-start | bytes 261128 | tf_op jit(solution)/shard_map/ppermute | solution.py:24
  13.9 0.4 shard_map.88
  14.3 0.4 collective-permute-done.1.above.sea_above
  14.7 4.3 %collective-permute-done.2.below.sea_below = f32[10,1,2176]{2,1,0:T(1,128)S(1)} collective-permute-done((f32[10,1,2176]{2,1,0:T(1,128)S(1)}, f32[10,1,2176]{2,1,0:T(1,128)S(1)}, u32[]{:S(2)}, u32[]{:S(2)}) %collective-permute-start.2) | collective-permute-done | bytes 87072 | tf_op jit(solution)/shard_map/ppermute | solution.py:24
  19.0 3.4 %shard_map.90 = (f32[2,3,8,2176]{3,2,1,0:T(8,128)S(1)}, f32[2,2,8,2176]{3,2,1,0:T(8,128)S(1)}, f32[18,1,2176]{2,1,0:T(1,128)S(1)}, f32[18,1,2176]{2,1,0:T(1,128)S(1)}) custom-call(f32[2,4,8,2176]{3,2,1,0:T(8,128)S(1)} %get-tuple-element.20.pairs, f32[2,3,8,2176]{3,2,1,0:T(8,128)S(1)} %get-tuple-element.21.moved, ...), custom_call_target="tpu_custom_call" | custom-call | flops 2000000 | bytes 2959360 | tf_op jit(solution)/shard_map/pallas_call | solution.py:389
  22.4 4.4 %collective-permute-start.3 = (f32[18,1,2176]{2,1,0:T(1,128)S(1)}, f32[18,1,2176]{2,1,0:T(1,128)S(1)}, u32[]{:S(2)}, u32[]{:S(2)}) collective-permute-start(f32[18,1,2176]{2,1,0:T(1,128)S(1)} %get-tuple-element.26.to_below), channel_id=1, source_target_pairs={{0,2},{1,3},{2,4},{3,5},{4,6},{5,7},{6,8},{7,9},{8,10},{9,11},{10,... | collective-permute-start | bytes 470024 | tf_op jit(solution)/shard_map/ppermute | solution.py:24
  26.8 1.3 %collective-permute-start.4 = (f32[18,1,2176]{2,1,0:T(1,128)S(1)}, f32[18,1,2176]{2,1,0:T(1,128)S(1)}, u32[]{:S(2)}, u32[]{:S(2)}) collective-permute-start(f32[18,1,2176]{2,1,0:T(1,128)S(1)} %get-tuple-element.27.to_above), channel_id=1, source_target_pairs={{2,0},{3,1},{4,2},{5,3},{6,4},{7,5},{8,6},{9,7},{10,8},{11,9},{12,... | collective-permute-start | bytes 470024 | tf_op jit(solution)/shard_map/ppermute | solution.py:24
  28.1 3.1 %collective-permute-done.3.above = f32[18,1,2176]{2,1,0:T(1,128)S(1)} collective-permute-done((f32[18,1,2176]{2,1,0:T(1,128)S(1)}, f32[18,1,2176]{2,1,0:T(1,128)S(1)}, u32[]{:S(2)}, u32[]{:S(2)}) %collective-permute-start.3) | collective-permute-done | bytes 156704 | tf_op jit(solution)/shard_map/ppermute | solution.py:24
  31.2 2.7 %collective-permute-done.4.below = f32[18,1,2176]{2,1,0:T(1,128)S(1)} collective-permute-done((f32[18,1,2176]{2,1,0:T(1,128)S(1)}, f32[18,1,2176]{2,1,0:T(1,128)S(1)}, u32[]{:S(2)}, u32[]{:S(2)}) %collective-permute-start.4) | collective-permute-done | bytes 156704 | tf_op jit(solution)/shard_map/ppermute | solution.py:24
  33.9 0.8 %shard_map.91 = (f32[2,3,8,2176]{3,2,1,0:T(8,128)S(1)}, f32[2,2,8,2176]{3,2,1,0:T(8,128)S(1)}, f32[18,8,128]{2,1,0:T(8,128)S(1)}) custom-call(f32[2,4,8,2176]{3,2,1,0:T(8,128)S(1)} %get-tuple-element.20.pairs, f32[2,3,8,2176]{3,2,1,0:T(8,128)S(1)} %get-tuple-element.25.part, f32[24,8,2176]{2,1,0:T(8,128)S(1)} %get-tuple-element.19.planes, ...), custom_call_target="tpu_custom_call" | custom-call | flops 2000000 | bytes 3586048 | tf_op jit(solution)/shard_map/pallas_call | solution.py:389
  34.7 0.1 collective-permute-start.5
  34.8 1.3 %collective-permute-done.5.theirs = f32[18,8,128]{2,1,0:T(8,128)S(1)} collective-permute-done((f32[18,8,128]{2,1,0:T(8,128)S(1)}, f32[18,8,128]{2,1,0:T(8,128)S(1)}, u32[]{:S(2)}, u32[]{:S(2)}) %collective-permute-start.5) | collective-permute-done | bytes 73760 | tf_op jit(solution)/shard_map/ppermute | solution.py:24
  36.1 1.5 %collective-permute-start.6 = (f32[2,8,128]{2,1,0:T(8,128)S(1)}, f32[2,8,128]{2,1,0:T(8,128)S(1)}, u32[]{:S(2)}, u32[]{:S(2)}) collective-permute-start(f32[2,8,128]{2,1,0:T(8,128)S(1)} %slice_add_fusion), channel_id=1, source_target_pairs={{0,2},{1,3},{2,0},{3,1},{4,6},{5,7},{6,4},{7,5},{8,10},{9,11},{10,... | collective-permute-start | bytes 24584 | tf_op jit(solution)/shard_map/ppermute | solution.py:24
  37.5 2.2 %collective-permute-done.6 = f32[2,8,128]{2,1,0:T(8,128)S(1)} collective-permute-done((f32[2,8,128]{2,1,0:T(8,128)S(1)}, f32[2,8,128]{2,1,0:T(8,128)S(1)}, u32[]{:S(2)}, u32[]{:S(2)}) %collective-permute-start.6) | collective-permute-done | bytes 8224 | tf_op jit(solution)/shard_map/ppermute | solution.py:24
  39.7 1.6 %collective-permute-start.7 = (f32[2,8,128]{2,1,0:T(8,128)S(1)}, f32[2,8,128]{2,1,0:T(8,128)S(1)}, u32[]{:S(2)}, u32[]{:S(2)}) collective-permute-start(f32[2,8,128]{2,1,0:T(8,128)S(1)} %add.13), channel_id=1, source_target_pairs={{0,4},{1,5},{2,6},{3,7},{4,0},{5,1},{6,2},{7,3},{8,12},{9,13},{10,... | collective-permute-start | bytes 24584 | tf_op jit(solution)/shard_map/ppermute | solution.py:24
  41.3 2.1 %collective-permute-done.7 = f32[2,8,128]{2,1,0:T(8,128)S(1)} collective-permute-done((f32[2,8,128]{2,1,0:T(8,128)S(1)}, f32[2,8,128]{2,1,0:T(8,128)S(1)}, u32[]{:S(2)}, u32[]{:S(2)}) %collective-permute-start.7) | collective-permute-done | bytes 8224 | tf_op jit(solution)/shard_map/ppermute | solution.py:24
  43.4 2.6 %collective-permute-start.8 = (f32[2,8,128]{2,1,0:T(8,128)S(1)}, f32[2,8,128]{2,1,0:T(8,128)S(1)}, u32[]{:S(2)}, u32[]{:S(2)}) collective-permute-start(f32[2,8,128]{2,1,0:T(8,128)S(1)} %add.14), channel_id=1, source_target_pairs={{0,8},{1,9},{2,10},{3,11},{4,12},{5,13},{6,14},{7,15},{8,0},{9,1},... | collective-permute-start | bytes 24584 | tf_op jit(solution)/shard_map/ppermute | solution.py:24
  46.0 2.0 %collective-permute-done.8 = f32[2,8,128]{2,1,0:T(8,128)S(1)} collective-permute-done((f32[2,8,128]{2,1,0:T(8,128)S(1)}, f32[2,8,128]{2,1,0:T(8,128)S(1)}, u32[]{:S(2)}, u32[]{:S(2)}) %collective-permute-start.8) | collective-permute-done | bytes 8224 | tf_op jit(solution)/shard_map/ppermute | solution.py:24
  47.9 2.4 %shard_map.92 = (f32[2,4,4096]{2,1,0:T(4,128)}, f32[2,4,2048]{2,1,0:T(4,128)}) custom-call(f32[2,8,128]{2,1,0:T(8,128)S(1)} %add.15.scalars, f32[4,8,2176]{2,1,0:T(8,128)S(1)} %get-tuple-element.17.mine, f32[4,8,2176]{2,1,0:T(8,128)S(1)} %get-tuple-element.18.give, f32[2,4,8,2176]{3,2,1,0:T(8,128)S(1)} %get-tuple-element.20.pairs, ...), custom_call_target="tpu_custom_call" | custom-call | flops 2000000 | bytes 2170880 | tf_op jit(solution)/shard_map/pallas_call | solution.py:389
  (11 shorter events, 0.1 us)
Async XLA Ops:
  0.6 0.8 %copy-start.1 = (s32[4,4096]{1,0:T(4,128)S(1)}, s32[4,4096]{1,0:T(4,128)}, u32[]{:S(2)}) copy-start(s32[4,4096]{1,0:T(4,128)} %sea.3) | copy-start | bytes 196612
  1.5 0.8 %copy-start.2 = (f32[4,4096]{1,0:T(4,128)S(1)}, f32[4,4096]{1,0:T(4,128)}, u32[]{:S(2)}) copy-start(f32[4,4096]{1,0:T(4,128)} %precision.3) | copy-start | bytes 196612
  2.3 0.9 %copy-start.3 = (f32[2,4,4096]{2,1,0:T(4,128)S(1)}, f32[2,4,4096]{2,1,0:T(4,128)}, u32[]{:S(2)}) copy-start(f32[2,4,4096]{2,1,0:T(4,128)} %observed.1) | copy-start | bytes 393220
  3.2 0.9 %copy-start.4 = (s32[2,4,4096]{2,1,0:T(4,128)S(1)}, s32[2,4,4096]{2,1,0:T(4,128)}, u32[]{:S(2)}) copy-start(s32[2,4,4096]{2,1,0:T(4,128)} %gap.1) | copy-start | bytes 393220
  4.1 0.9 %copy-start.5 = (bf16[2,2,4,4096]{3,2,1,0:T(4,128)(2,1)S(1)}, bf16[2,2,4,4096]{3,2,1,0:T(4,128)(2,1)}, u32[]{:S(2)}) copy-start(bf16[2,2,4,4096]{3,2,1,0:T(4,128)(2,1)} %perturbation.1) | copy-start | bytes 393220
  5.0 0.8 %copy-start.6 = (f32[4,4096]{1,0:T(4,128)S(1)}, f32[4,4096]{1,0:T(4,128)}, u32[]{:S(2)}) copy-start(f32[4,4096]{1,0:T(4,128)} %noise.1) | copy-start | bytes 196612
  6.1 1.7 %collective-permute-start = (f32[4,8,2176]{2,1,0:T(8,128)S(1)}, f32[4,8,2176]{2,1,0:T(8,128)S(1)}, u32[]{:S(2)}, u32[]{:S(2)}) collective-permute-start(f32[4,8,2176]{2,1,0:T(8,128)S(1)} %get-tuple-element.18.give), channel_id=1, source_target_pairs={{0,1},{1,0},{2,3},{3,2},{4,5},{5,4},{6,7},{7,6},{8,9},{9,8},{10,11... | collective-permute-start | bytes 835592 | tf_op jit(solution)/shard_map/ppermute | solution.py:24
  6.6 1.0 %copy-start = (bf16[9,4,4096]{2,1,0:T(4,128)(2,1)S(1)}, bf16[9,4,4096]{2,1,0:T(4,128)(2,1)}, u32[]{:S(2)}) copy-start(bf16[9,4,4096]{2,1,0:T(4,128)(2,1)} %stencil.1) | copy-start | bytes 884740
  7.8 6.9 %collective-permute-start.1 = (f32[10,1,2176]{2,1,0:T(1,128)S(1)}, f32[10,1,2176]{2,1,0:T(1,128)S(1)}, u32[]{:S(2)}, u32[]{:S(2)}) collective-permute-start(f32[10,1,2176]{2,1,0:T(1,128)S(1)} %get-tuple-element.23), channel_id=1, source_target_pairs={{0,2},{1,3},{2,4},{3,5},{4,6},{5,7},{6,8},{7,9},{8,10},{9,11},{10,... | collective-permute-start | bytes 261128 | tf_op jit(solution)/shard_map/ppermute | solution.py:24
  12.6 6.4 %collective-permute-start.2 = (f32[10,1,2176]{2,1,0:T(1,128)S(1)}, f32[10,1,2176]{2,1,0:T(1,128)S(1)}, u32[]{:S(2)}, u32[]{:S(2)}) collective-permute-start(f32[10,1,2176]{2,1,0:T(1,128)S(1)} %get-tuple-element.24), channel_id=1, source_target_pairs={{2,0},{3,1},{4,2},{5,3},{6,4},{7,5},{8,6},{9,7},{10,8},{11,9},{12,... | collective-permute-start | bytes 261128 | tf_op jit(solution)/shard_map/ppermute | solution.py:24
  22.4 8.8 %collective-permute-start.3 = (f32[18,1,2176]{2,1,0:T(1,128)S(1)}, f32[18,1,2176]{2,1,0:T(1,128)S(1)}, u32[]{:S(2)}, u32[]{:S(2)}) collective-permute-start(f32[18,1,2176]{2,1,0:T(1,128)S(1)} %get-tuple-element.26.to_below), channel_id=1, source_target_pairs={{0,2},{1,3},{2,4},{3,5},{4,6},{5,7},{6,8},{7,9},{8,10},{9,11},{10,... | collective-permute-start | bytes 470024 | tf_op jit(solution)/shard_map/ppermute | solution.py:24
  26.8 7.1 %collective-permute-start.4 = (f32[18,1,2176]{2,1,0:T(1,128)S(1)}, f32[18,1,2176]{2,1,0:T(1,128)S(1)}, u32[]{:S(2)}, u32[]{:S(2)}) collective-permute-start(f32[18,1,2176]{2,1,0:T(1,128)S(1)} %get-tuple-element.27.to_above), channel_id=1, source_target_pairs={{2,0},{3,1},{4,2},{5,3},{6,4},{7,5},{8,6},{9,7},{10,8},{11,9},{12,... | collective-permute-start | bytes 470024 | tf_op jit(solution)/shard_map/ppermute | solution.py:24
  34.7 1.3 %collective-permute-start.5 = (f32[18,8,128]{2,1,0:T(8,128)S(1)}, f32[18,8,128]{2,1,0:T(8,128)S(1)}, u32[]{:S(2)}, u32[]{:S(2)}) collective-permute-start(f32[18,8,128]{2,1,0:T(8,128)S(1)} %get-tuple-element.28), channel_id=1, source_target_pairs={{0,1},{1,0},{2,3},{3,2},{4,5},{5,4},{6,7},{7,6},{8,9},{9,8},{10,11... | collective-permute-start | bytes 221192 | tf_op jit(solution)/shard_map/ppermute | solution.py:24
  36.1 3.7 %collective-permute-start.6 = (f32[2,8,128]{2,1,0:T(8,128)S(1)}, f32[2,8,128]{2,1,0:T(8,128)S(1)}, u32[]{:S(2)}, u32[]{:S(2)}) collective-permute-start(f32[2,8,128]{2,1,0:T(8,128)S(1)} %slice_add_fusion), channel_id=1, source_target_pairs={{0,2},{1,3},{2,0},{3,1},{4,6},{5,7},{6,4},{7,5},{8,10},{9,11},{10,... | collective-permute-start | bytes 24584 | tf_op jit(solution)/shard_map/ppermute | solution.py:24
  39.7 3.7 %collective-permute-start.7 = (f32[2,8,128]{2,1,0:T(8,128)S(1)}, f32[2,8,128]{2,1,0:T(8,128)S(1)}, u32[]{:S(2)}, u32[]{:S(2)}) collective-permute-start(f32[2,8,128]{2,1,0:T(8,128)S(1)} %add.13), channel_id=1, source_target_pairs={{0,4},{1,5},{2,6},{3,7},{4,0},{5,1},{6,2},{7,3},{8,12},{9,13},{10,... | collective-permute-start | bytes 24584 | tf_op jit(solution)/shard_map/ppermute | solution.py:24
  43.4 4.5 %collective-permute-start.8 = (f32[2,8,128]{2,1,0:T(8,128)S(1)}, f32[2,8,128]{2,1,0:T(8,128)S(1)}, u32[]{:S(2)}, u32[]{:S(2)}) collective-permute-start(f32[2,8,128]{2,1,0:T(8,128)S(1)} %add.14), channel_id=1, source_target_pairs={{0,8},{1,9},{2,10},{3,11},{4,12},{5,13},{6,14},{7,15},{8,0},{9,1},... | collective-permute-start | bytes 24584 | tf_op jit(solution)/shard_map/ppermute | solution.py:24

commit v3 on v2

--- a/solution.py
+++ b/solution.py
@@ -58,7 +58,18 @@
         return jnp.where(position(1) == self.edge, other, here)
 
 
-def right_sides_kernel(observed, gap, sea, precision, noise, perturbation, mine, give):
+def fetch(sources, buffers, semaphores):
+    copies = [pltpu.make_async_copy(x, y, semaphores.at[k]) for k, (x, y) in enumerate(zip(sources, buffers))]
+    for copy in copies:
+        copy.start()
+    for copy in copies:
+        copy.wait()
+
+
+def right_sides_kernel(*refs):
+    sources, (mine, give), buffers, semaphores = refs[:6], refs[6:8], refs[8:14], refs[14]
+    fetch(sources, buffers, semaphores)
+    observed, gap, sea, precision, noise, perturbation = buffers
     day = lax.axis_index("day")
     tiles = mine.shape[-1] // LANES
     reach = observed.shape[-1] - mine.shape[-1]
@@ -77,7 +88,10 @@
             out[3, :, tile(t)] = seen
 
 
-def coefficients_kernel(stencil, sea, precision, planes, cells):
+def coefficients_kernel(*refs):
+    sources, (planes, cells), buffers, semaphores = refs[:3], refs[3:5], refs[5:8], refs[8]
+    fetch(sources, buffers, semaphores)
+    stencil, sea, precision = buffers
     day = lax.axis_index("day")
     width = planes.shape[-1]
     tiles = width // LANES
@@ -113,21 +127,47 @@
                 planes[H_PLANE + c + 1, :, tile(t - 1)] = jnp.where(row == 0, got[-1], jnp.where(row == 3, got[1], 0.0))
 
 
-def edges_kernel(mine, got, cells, to_below, to_above):
-    day = lax.axis_index("day")
-    for which in (0, 1):
-        early, late = ((mine, got), (got, mine))[which]
-
-        @pl.when(day == which)
+def even_strip():
+    return lax.axis_index("space") % 2 == 0
+
+
+def pack_rows(plane, blocks, paired, crossed):
+    for even in (True, False):
+        to_below, to_above = (paired, crossed) if even else (crossed, paired)
+
+        @pl.when(even_strip() == even)
         def _():
             for out, r in ((to_below, 3), (to_above, 0)):
                 for f in range(FIELDS):
-                    out[3 * f, :, :] = early[f, r : r + 1, :]
-                    out[3 * f + 1, :, :] = early[f, 4 + r : 5 + r, :]
-                    out[3 * f + 2, :, :] = late[f, r : r + 1, :]
-
-    to_below[9, :, :] = cells[0, 3:4, :]
-    to_above[9, :, :] = cells[0, 0:1, :]
+                    early, late = blocks(f)
+                    out[plane + 3 * f, :, :] = early[r : r + 1, :]
+                    out[plane + 3 * f + 1, :, :] = early[4 + r : 5 + r, :]
+                    out[plane + 3 * f + 2, :, :] = late[r : r + 1, :]
+
+
+def unpack_rows(paired, crossed, above, below):
+    for even in (True, False):
+
+        @pl.when(even_strip() == even)
+        def _():
+            below[...] = (paired if even else crossed)[...]
+            above[...] = (crossed if even else paired)[...]
+
+
+def edges_kernel(mine, got, cells, paired, crossed):
+    for day in (0, 1):
+
+        @pl.when(lax.axis_index("day") == day)
+        def _():
+            early, late = (mine, got) if day == 0 else (got, mine)
+            pack_rows(0, lambda f: (early.at[f], late.at[f]), paired, crossed)
+
+    for even in (True, False):
+
+        @pl.when(even_strip() == even)
+        def _():
+            paired[9, :, :] = cells[0, 3:4, :] if even else cells[0, 0:1, :]
+            crossed[9, :, :] = cells[0, 0:1, :] if even else cells[0, 3:4, :]
 
 
 def apply_rows(planes, at, base, terms):
@@ -176,16 +216,8 @@
     return out
 
 
-def split_rows(below, above, plane, x, at, first, second):
-    if first is not None:
-        above[plane + first, :, at] = x[0:1]
-        below[plane + first, :, at] = x[3:4]
-    if second is not None:
-        above[plane + second, :, at] = x[4:5]
-        below[plane + second, :, at] = x[7:8]
-
-
-def image_kernel(pairs, moved, planes, cells, above, below, image, rims, to_below, to_above):
+def image_kernel(pairs, moved, planes, cells, came_paired, came_crossed, image, leaves, rims, paired, crossed, above, below):
+    unpack_rows(came_paired, came_crossed, above, below)
     tiles = moved.shape[-1] // LANES
     row = position(0)
     low = row < 4
@@ -231,15 +263,19 @@
                     out.append(edge + leaving[half][0].take(q) + leaving[half][1].take(q))
                     kept["own", half] = own
                 after = (rolled(jnp.where(low, s[1], s[0]), 4, 0), jnp.where(low, rolled(s[1], 4, 0), 0.0))
-                for half in (0, 1):
-                    z = cells[0, :, at] * (kept.pop(("own", half)) - after[half])
-                    image[half, f, :, at] = z
-                    split_rows(to_below, to_above, 0, z, at, 3 * f + 2 * half, 3 * f + 1 if half == 0 else None)
-                split_rows(to_below, to_above, 9, out[0], at, None, 3 * f)
-                split_rows(to_below, to_above, 9, out[1], at, 3 * f + 1, 3 * f + 2)
-
-
-def sums_kernel(pairs, part, planes, cells, sea_above, sea_below, to_below, to_above, above, below, image, rims, swap):
+                leaves[0, f, :, at] = rolled(jnp.where(low, out[1], out[0]), 4, 0)
+                leaves[1, f, :, at] = rolled(out[1], 4, 0)
+                for half in (0, 1):
+                    image[half, f, :, at] = cells[0, :, at] * (kept.pop(("own", half)) - after[half])
+    pack_rows(0, lambda f: (image.at[0, f], image.at[1, f]), paired, crossed)
+    pack_rows(9, lambda f: (leaves.at[0, f], leaves.at[1, f]), paired, crossed)
+
+
+def sums_kernel(*refs):
+    pairs, part, leaves, planes, cells, first_paired, first_crossed, came_paired, came_crossed = refs[:9]
+    image, rims, swap, sums, sea_above, sea_below, above, below = refs[9:]
+    unpack_rows(first_paired.at[9:10], first_crossed.at[9:10], sea_above, sea_below)
+    unpack_rows(came_paired, came_crossed, above, below)
     day = lax.axis_index("day")
     tiles = part.shape[-1] // LANES
     row = position(0)
@@ -254,14 +290,14 @@
             if t < tiles:
                 at = tile(t)
                 wet = cells[0, :, at]
-                wet_rim = placed(sea_above, sea_below, (9, 9), at)
+                wet_rim = placed(sea_above, sea_below, (0, 0), at)
                 for half in (0, 1):
                     days = (3 * f, 3 * f + 1) if half == 0 else (3 * f + 2, None)
                     late = tuple(None if k is None else 9 + k for k in days)
                     came = placed(above, below, late, at)
                     keep = edge if half == 0 else edge & low
                     z = part[half, f, :, at] - jnp.where(keep, wet * came, 0.0)
-                    rim = placed(above, below, days, at) - wet_rim * placed(to_above, to_below, late, at)
+                    rim = placed(above, below, days, at) - wet_rim * leaves[half, f, :, at]
                     image[half, f, :, at] = z
                     if f > 0:
                         rims[half, f - 1, :, at] = rim
@@ -293,10 +329,13 @@
                 elif q == tiles - 1:
                     terms = [jnp.where(day == 0, 0.0, x) for x in terms]
                 totals = [x if y is None else x + y for x, y in zip(terms, totals)]
-        rows += [jnp.sum(x, axis=0, keepdims=True) for x in totals]
+        rows += [jnp.sum(jnp.sum(x, axis=0, keepdims=True), axis=1, keepdims=True) for x in totals]
+    lane = lax.broadcasted_iota(jnp.int32, (1, LANES), 1)
+    line = jnp.zeros((1, LANES), F32)
     for k, x in enumerate(rows):
-        swap[tiles - 1 + k // 8, k % 8 : k % 8 + 1, :] = x
-    swap[tiles, 4:8, :] = jnp.zeros((4, LANES), F32)
+        line = jnp.where(lane == k, x, line)
+    for k in range(sums.shape[0]):
+        sums[k, :, :] = line
     for which in (0, 1):
 
         @pl.when(day == which)
@@ -305,17 +344,17 @@
                 swap[t, :, :] = image[1 - which, 0, :, tile(t + which)]
 
 
-def fit_kernel(scalars, mine, give, pairs, image, theirs, side_rims, image_rims, posterior, fitted):
+def fit_kernel(sums, mine, give, pairs, image, theirs, side_rims, image_rims, posterior, fitted, mean, cells, ready, semaphores):
     day = lax.axis_index("day")
     tiles = mine.shape[-1] // LANES
     row = position(0)
     low = row < 4
+    line = sums[0, :, :]
+    for k in range(1, sums.shape[0]):
+        line = line + sums[k, :, :]
     weights = []
     for f in range(FIELDS):
-        m = []
-        for k in range(4 * f, 4 * f + 4):
-            total = jnp.sum(scalars[k // 8, k % 8 : k % 8 + 1, :], axis=1, keepdims=True)
-            m.append(jnp.broadcast_to(total, (8, LANES)))
+        m = [jnp.broadcast_to(line[:, k : k + 1], (8, LANES)) for k in range(4 * f, 4 * f + 4)]
         step = m[0] / m[1]
         norm_next = step * step * m[2] - m[0]
         grown = 1.0 + norm_next / m[0]
@@ -324,8 +363,8 @@
         weights.append((step + second * grown, -second * step))
 
     def store(at, x):
-        posterior[0, :, at] = x[0:4]
-        posterior[1, :, at] = x[4:8]
+        mean[0, :, at] = x[0:4]
+        mean[1, :, at] = x[4:8]
 
     on_side, on_image = weights[0]
     for which in (0, 1):
@@ -337,6 +376,9 @@
                 own = on_side * mine[0, :, tile(t + which)] + on_image * image[which, 0, :, tile(t + which)]
                 store(tile(here + t), own)
                 store(tile(there + t), on_side * give[0, :, tile(t + 1 - which)] + on_image * theirs[t, :, :])
+
+    out_mean = pltpu.make_async_copy(mean, posterior, semaphores.at[0])
+    out_mean.start()
 
     wide = {(f, half): (Shift(1), Shift(-1)) for f in (1, 2) for half in (0, 1)}
     kept = {}
@@ -373,70 +415,89 @@
             persistence = (second * m[3] - m[1] * m[4]) * inverse
             diffusion = (first * m[4] - m[1] * m[3]) * inverse
 
-            def write(to):
-                fitted[0, :, tile(to)] = persistence[0:4]
-                fitted[1, :, tile(to)] = diffusion[0:4]
-
-            if q < tiles - 1:
-                pl.when(day == 0)(lambda: write(q))
-            if q > 0:
-                pl.when(day == 1)(lambda: write(q - 1))
-
-
-def call(kernel, outs, *args, flops=2_000_000):
-    vmem = pl.BlockSpec(memory_space=pltpu.VMEM)
+            cells[0, :, tile(q)] = persistence[0:4]
+            cells[1, :, tile(q)] = diffusion[0:4]
+    for which in (0, 1):
+
+        @pl.when(day == which)
+        def _():
+            ready[...] = cells[:, :, which * LANES : which * LANES + ready.shape[-1]]
+
+    out_fit = pltpu.make_async_copy(ready, fitted, semaphores.at[1])
+    out_fit.start()
+    out_mean.wait()
+    out_fit.wait()
+
+
+VMEM = pl.BlockSpec(memory_space=pltpu.VMEM)
+HBM = pl.BlockSpec(memory_space=pltpu.HBM)
+
+
+def call(kernel, outs, *args, scratch=(), source=VMEM, target=VMEM, flops=2_000_000):
     size = sum(x.size * x.dtype.itemsize for x in args)
     return pl.pallas_call(
         kernel,
-        out_shape=[jax.ShapeDtypeStruct(s, F32) for s in outs],
-        in_specs=[vmem] * len(args),
-        out_specs=[vmem] * len(outs),
+        out_shape=[jax.ShapeDtypeStruct(shape, F32) for shape in outs],
+        in_specs=[source] * len(args),
+        out_specs=[target] * len(outs),
+        scratch_shapes=scratch,
         cost_estimate=pl.CostEstimate(flops=flops, bytes_accessed=size, transcendentals=0),
         compiler_params=pltpu.CompilerParams(vmem_limit_bytes=32 << 20),
     )(*args)
 
 
+def buffers(*args):
+    return [pltpu.VMEM(x.shape, x.dtype) for x in args] + [pltpu.SemaphoreType.DMA((len(args),))]
+
+
 def shards(observed, gap_mask, sea_mask, stencil, precision, noise_precision, perturbation):
     cols = observed.shape[-1]
-    spaces = lax.axis_size("space")
+    devices = lax.axis_size("space") * lax.axis_size("day")
     half = cols // 2
     width = half + LANES
-    tiles = width // LANES
     pair = (8, width)
-
-    mine, give = call(
-        right_sides_kernel, [(4, *pair)] * 2, observed, gap_mask, sea_mask, precision, noise_precision, perturbation
+    row = (1, width)
+    same = lambda s: s
+    paired_space = lambda s: s ^ 1
+    crossed_space = lambda s: ((s + 1) ^ 1) - 1
+
+    raw = (observed, gap_mask, sea_mask, precision, noise_precision, perturbation)
+    mine, give = call(right_sides_kernel, [(4, *pair)] * 2, *raw, scratch=buffers(*raw), source=HBM)
+    got = send(give, same, lambda d: 1 - d)
+    raw = (stencil, sea_mask, precision)
+    planes, cells = call(coefficients_kernel, [(PLANES, *pair), (2, *pair)], *raw, scratch=buffers(*raw), source=HBM)
+    paired, crossed = call(edges_kernel, [(10, *row)] * 2, mine, got, cells)
+    first_crossed = send(crossed, crossed_space)
+    first_paired = send(paired, paired_space)
+    pairs, moved = call(inside_kernel, [(2, 4, *pair), (2, 3, *pair)], mine, got, planes)
+    part, leaves, side_rims, paired, crossed = call(
+        image_kernel,
+        [(2, 3, *pair), (2, 3, *pair), (2, 2, *pair), (18, *row), (18, *row)],
+        pairs, moved, planes, cells, first_paired, first_crossed,
+        scratch=[pltpu.VMEM((10, *row), F32)] * 2,
     )
-    got = send(give, lambda s: s, lambda d: 1 - d)
-    planes, cells = call(coefficients_kernel, [(PLANES, *pair), (2, *pair)], stencil, sea_mask, precision)
-    to_below, to_above = call(edges_kernel, [(10, 1, width)] * 2, mine, got, cells)
-    above = send(to_below, lambda s: s + 1)
-    below = send(to_above, lambda s: s - 1)
-    pairs, moved = call(inside_kernel, [(2, 4, *pair), (2, 3, *pair)], mine, got, planes)
-    part, side_rims, to_below, to_above = call(
-        image_kernel, [(2, 3, *pair), (2, 2, *pair), (18, 1, width), (18, 1, width)], pairs, moved, planes, cells, above, below
+    crossed = send(crossed, crossed_space)
+    paired = send(paired, paired_space)
+    image, image_rims, swap, sums = call(
+        sums_kernel,
+        [(2, 3, *pair), (2, 2, *pair), (half // LANES, 8, LANES), (devices, 1, LANES)],
+        pairs, part, leaves, planes, cells, first_paired, first_crossed, paired, crossed,
+        scratch=[pltpu.VMEM((1, *row), F32)] * 2 + [pltpu.VMEM((18, *row), F32)] * 2,
     )
-    from_above = send(to_below, lambda s: s + 1)
-    from_below = send(to_above, lambda s: s - 1)
-    image, image_rims, swap = call(
-        sums_kernel,
-        [(2, 3, *pair), (2, 2, *pair), (tiles + 1, 8, LANES)],
-        pairs, part, planes, cells, above, below, to_below, to_above, from_above, from_below,
-    )
-    theirs = send(swap, lambda s: s, lambda d: 1 - d)
-    scalars = swap[tiles - 1 :]
-    if spaces & (spaces - 1) == 0:
-        scalars = scalars + theirs[tiles - 1 :]
-        bit = 1
-        while bit < spaces:
-            scalars = scalars + send(scalars, lambda s: s ^ bit)
-            bit *= 2
-    else:
-        scalars = lax.psum(scalars, ("space", "day"))
+    theirs = send(swap, same, lambda d: 1 - d)
+    sums = lax.all_to_all(sums, ("space", "day"), 0, 0)
+    fit = (2, observed.shape[1])
     posterior, fitted = call(
         fit_kernel,
-        [observed.shape, (2, observed.shape[1], half)],
-        scalars, mine, give, pairs, image, theirs, side_rims, image_rims,
+        [observed.shape, (*fit, half)],
+        sums, mine, give, pairs, image, theirs, side_rims, image_rims,
+        scratch=[
+            pltpu.VMEM(observed.shape, F32),
+            pltpu.VMEM((*fit, width), F32),
+            pltpu.VMEM((*fit, half), F32),
+            pltpu.SemaphoreType.DMA((2,)),
+        ],
+        target=HBM,
     )
     return posterior, fitted
 

time: 50.7 us -> 44.8 us (0.88)
  blocking collectives: 0 us -> 13 us
  waiting for transfers between devices: 18 us -> 7.92 us
  starting transfers between devices: 17.9 us -> 9.26 us
    all_to_all x0 -> x1, blocking collectives: none -> 13 us  [shards(): sums = lax.all_to_all(sums, ('space', 'day'), 0, 0)]
    ppermute x9 -> x6, waiting for transfers between devices: 18 us -> 7.92 us  [send(): return lax.ppermute(x, ('space', 'day'), pairs)]
    ppermute x9 -> x6, starting transfers between devices: 17.9 us -> 9.26 us  [send(): return lax.ppermute(x, ('space', 'day'), pairs)]
  transfers between devices with their start and end apart: 9 -> 6, of which waited for: 8 -> 2; matrix products, arithmetic and copies ran while one was open for 0% -> 0% of each run, Pallas kernels for 1% -> 2%
where the time goes in v3:
time: 44.8 us; the launch traced here: 44.4 us
  blocking collectives  13 us (29%)
  starting transfers between devices  9.26 us (21%)
  waiting for transfers between devices  7.92 us (18%)
  Pallas kernels  7.35 us (16%)
  local copies, waits for them, and re-layouts  6.18 us (14%)
  between operations  0.72 us (2%)
    all_to_all x1, blocking collectives, shards(): sums = lax.all_to_all(sums, ('space', 'day'), 0, 0)  13 us
    ppermute x6, starting transfers between devices, send(): return lax.ppermute(x, ('space', 'day'), pairs)  9.26 us
    ppermute x6, waiting for transfers between devices, send(): return lax.ppermute(x, ('space', 'day'), pairs)  7.92 us
    pallas_call x7, Pallas kernels, call(): pl.pallas_call(kernel, out_shape=[jax.ShapeDtypeStruct(shape, F32) for sh...  7.35 us
    unnamed x14, local copies, waits for them, and re-layouts  6.18 us
  transfers between devices with their start and end apart: 6, of which 2 were waited for; matrix products, arithmetic and copies ran while one was open for 0% of the time, Pallas kernels for 2%

profile of v3, /device:TPU:0, one launch (start us, length us, event | category | flops | bytes accessed | tf_op | source)
XLA Modules:
  0.0 44.4 jit_solution(14707522034635410914)
XLA Ops:
  0.6 0.0 copy-start.1
  0.6 0.8 %copy-done.1 = s32[4,4096]{1,0:T(4,128)S(1)} copy-done((s32[4,4096]{1,0:T(4,128)S(1)}, s32[4,4096]{1,0:T(4,128)}, u32[]{:S(2)}) %copy-start.1) | copy-done | bytes 65560
  1.5 0.0 copy-start.2
  1.5 0.8 %copy-done.2 = f32[4,4096]{1,0:T(4,128)S(1)} copy-done((f32[4,4096]{1,0:T(4,128)S(1)}, f32[4,4096]{1,0:T(4,128)}, u32[]{:S(2)}) %copy-start.2) | copy-done | bytes 65560
  2.3 0.0 copy-start.3
  2.3 0.9 %copy-done.3 = f32[2,4,4096]{2,1,0:T(4,128)S(1)} copy-done((f32[2,4,4096]{2,1,0:T(4,128)S(1)}, f32[2,4,4096]{2,1,0:T(4,128)}, u32[]{:S(2)}) %copy-start.3) | copy-done | bytes 131096
  3.2 0.0 copy-start.4
  3.2 0.9 %copy-done.4 = s32[2,4,4096]{2,1,0:T(4,128)S(1)} copy-done((s32[2,4,4096]{2,1,0:T(4,128)S(1)}, s32[2,4,4096]{2,1,0:T(4,128)}, u32[]{:S(2)}) %copy-start.4) | copy-done | bytes 131096
  4.1 0.0 copy-start.5
  4.1 0.9 %copy-done.5 = bf16[2,2,4,4096]{3,2,1,0:T(4,128)(2,1)S(1)} copy-done((bf16[2,2,4,4096]{3,2,1,0:T(4,128)(2,1)S(1)}, bf16[2,2,4,4096]{3,2,1,0:T(4,128)(2,1)}, u32[]{:S(2)}) %copy-start.5) | copy-done | bytes 131096
  5.0 0.8 %copy-done.6 = f32[4,4096]{1,0:T(4,128)S(1)} copy-done((f32[4,4096]{1,0:T(4,128)S(1)}, f32[4,4096]{1,0:T(4,128)}, u32[]{:S(2)}) %copy-start.6) | copy-done | bytes 65560
  5.9 1.0 %shard_map.86 = (f32[4,8,2176]{2,1,0:T(8,128)S(1)}, f32[4,8,2176]{2,1,0:T(8,128)S(1)}) custom-call(f32[2,4,4096]{2,1,0:T(4,128)S(1)} %copy-done.3, s32[2,4,4096]{2,1,0:T(4,128)S(1)} %copy-done.4, s32[4,4096]{1,0:T(4,128)S(1)} %copy-done.1, f32[4,4096]{1,0:T(4,128)S(1)} %copy-done.2, f32[4,4096]{1,0:T(4,128)S(1)} %copy-done.6, ...), custom_call_target="tpu_custom_call" | custom-call | flops 2000000 | bytes 589824 | tf_op jit(solution)/shard_map/pallas_call | solution.py:438
  6.9 0.5 %collective-permute-start = (f32[4,8,2176]{2,1,0:T(8,128)S(1)}, f32[4,8,2176]{2,1,0:T(8,128)S(1)}, u32[]{:S(2)}, u32[]{:S(2)}) collective-permute-start(f32[4,8,2176]{2,1,0:T(8,128)S(1)} %get-tuple-element.20.give), channel_id=1, source_target_pairs={{0,1},{1,0},{2,3},{3,2},{4,5},{5,4},{6,7},{7,6},{8,9},{9,8},{10,11... | collective-permute-start | bytes 835592 | tf_op jit(solution)/shard_map/ppermute | solution.py:24
  7.4 1.0 %copy-done = bf16[9,4,4096]{2,1,0:T(4,128)(2,1)S(1)} copy-done((bf16[9,4,4096]{2,1,0:T(4,128)(2,1)S(1)}, bf16[9,4,4096]{2,1,0:T(4,128)(2,1)}, u32[]{:S(2)}) %copy-start) | copy-done | bytes 294936
  8.3 0.5 %shard_map.87 = (f32[24,8,2176]{2,1,0:T(8,128)S(1)}, f32[2,8,2176]{2,1,0:T(8,128)S(1)}) custom-call(bf16[9,4,4096]{2,1,0:T(4,128)(2,1)S(1)} %copy-done, s32[4,4096]{1,0:T(4,128)S(1)} %copy-done.1, f32[4,4096]{1,0:T(4,128)S(1)} %copy-done.2), custom_call_target="tpu_custom_call" | custom-call | flops 2000000 | bytes 425984 | tf_op jit(solution)/shard_map/pallas_call | solution.py:438
  8.8 0.0 collective-permute-done.got
  8.8 0.1 shard_map.89
  8.9 2.6 %collective-permute-start.1 = (f32[10,1,2176]{2,1,0:T(1,128)S(1)}, f32[10,1,2176]{2,1,0:T(1,128)S(1)}, u32[]{:S(2)}, u32[]{:S(2)}) collective-permute-start(f32[10,1,2176]{2,1,0:T(1,128)S(1)} %get-tuple-element.25), channel_id=1, source_target_pairs={{0,2},{1,3},{2,0},{3,1},{4,6},{5,7},{6,4},{7,5},{8,10},{9,11},{10,... | collective-permute-start | bytes 261128 | tf_op jit(solution)/shard_map/ppermute | solution.py:24
  11.6 0.7 %collective-permute-start.2 = (f32[10,1,2176]{2,1,0:T(1,128)S(1)}, f32[10,1,2176]{2,1,0:T(1,128)S(1)}, u32[]{:S(2)}, u32[]{:S(2)}) collective-permute-start(f32[10,1,2176]{2,1,0:T(1,128)S(1)} %get-tuple-element.26), channel_id=1, source_target_pairs={{2,4},{3,5},{4,2},{5,3},{6,8},{7,9},{8,6},{9,7},{10,12},{11,13},{1... | collective-permute-start | bytes 261128 | tf_op jit(solution)/shard_map/ppermute | solution.py:24
  12.2 0.4 shard_map.88
  12.6 2.1 %collective-permute-done.1.came_paired.refs_5_ = f32[10,1,2176]{2,1,0:T(1,128)S(1)} collective-permute-done((f32[10,1,2176]{2,1,0:T(1,128)S(1)}, f32[10,1,2176]{2,1,0:T(1,128)S(1)}, u32[]{:S(2)}, u32[]{:S(2)}) %collective-permute-start.1) | collective-permute-done | bytes 87072 | tf_op jit(solution)/shard_map/ppermute | solution.py:24
  14.7 0.0 collective-permute-done.2.came_crossed.refs_6_
  14.7 3.5 %shard_map.90 = (f32[2,3,8,2176]{3,2,1,0:T(8,128)S(1)}, f32[2,3,8,2176]{3,2,1,0:T(8,128)S(1)}, f32[2,2,8,2176]{3,2,1,0:T(8,128)S(1)}, f32[18,1,2176]{2,1,0:T(1,128)S(1)}, f32[18,1,2176]{2,1,0:T(1,128)S(1)}) custom-call(f32[2,4,8,2176]{3,2,1,0:T(8,128)S(1)} %get-tuple-element.22.pairs.refs_0_, f32[2,3,8,2176]{3,2,1,0:T(8,128)S(1)} %get-tuple-element.23.moved, ...), custom_call_target="tpu_custom_call" | custom-call | flops 2000000 | bytes 2959360 | tf_op jit(solution)/shard_map/pallas_call | solution.py:438
  18.2 4.7 %collective-permute-start.3 = (f32[18,1,2176]{2,1,0:T(1,128)S(1)}, f32[18,1,2176]{2,1,0:T(1,128)S(1)}, u32[]{:S(2)}, u32[]{:S(2)}) collective-permute-start(f32[18,1,2176]{2,1,0:T(1,128)S(1)} %get-tuple-element.29), channel_id=1, source_target_pairs={{0,2},{1,3},{2,0},{3,1},{4,6},{5,7},{6,4},{7,5},{8,10},{9,11},{10,... | collective-permute-start | bytes 470024 | tf_op jit(solution)/shard_map/ppermute | solution.py:24
  22.9 0.7 %collective-permute-start.4 = (f32[18,1,2176]{2,1,0:T(1,128)S(1)}, f32[18,1,2176]{2,1,0:T(1,128)S(1)}, u32[]{:S(2)}, u32[]{:S(2)}) collective-permute-start(f32[18,1,2176]{2,1,0:T(1,128)S(1)} %get-tuple-element.30), channel_id=1, source_target_pairs={{2,4},{3,5},{4,2},{5,3},{6,8},{7,9},{8,6},{9,7},{10,12},{11,13},{1... | collective-permute-start | bytes 470024 | tf_op jit(solution)/shard_map/ppermute | solution.py:24
  23.6 5.8 %collective-permute-done.3.refs_7_ = f32[18,1,2176]{2,1,0:T(1,128)S(1)} collective-permute-done((f32[18,1,2176]{2,1,0:T(1,128)S(1)}, f32[18,1,2176]{2,1,0:T(1,128)S(1)}, u32[]{:S(2)}, u32[]{:S(2)}) %collective-permute-start.3) | collective-permute-done | bytes 156704 | tf_op jit(solution)/shard_map/ppermute | solution.py:24
  29.4 0.0 collective-permute-done.4.refs_8_
  29.4 0.8 %shard_map.91 = (f32[2,3,8,2176]{3,2,1,0:T(8,128)S(1)}, f32[2,2,8,2176]{3,2,1,0:T(8,128)S(1)}, f32[16,8,128]{2,1,0:T(8,128)S(1)}, f32[16,1,128]{2,1,0:T(1,128)S(1)}) custom-call(f32[2,4,8,2176]{3,2,1,0:T(8,128)S(1)} %get-tuple-element.22.pairs.refs_0_, f32[2,3,8,2176]{3,2,1,0:T(8,128)S(1)} %get-tuple-element.27.refs_1_, ...), custom_call_target="tpu_custom_call" | custom-call | flops 2000000 | bytes 3690496 | tf_op jit(solution)/shard_map/pallas_call | solution.py:438
  30.2 0.0 collective-permute-start.5
  30.3 13.0 %all_to_all.5.sums = f32[16,1,128]{2,1,0:T(1,128)S(1)} all-to-all(f32[16,1,128]{2,1,0:T(1,128)S(1)} %get-tuple-element.31), channel_id=1, replica_groups=mesh['region'=2,'space'=8,'day'=2] {'space','day'}, dimensions={0} | all-to-all | bytes 16384 | tf_op jit(solution)/shard_map/all_to_all | solution.py:488
  43.3 0.0 collective-permute-done.5.theirs
  43.3 1.1 %shard_map.92 = (f32[2,4,4096]{2,1,0:T(4,128)}, f32[2,4,2048]{2,1,0:T(4,128)}) custom-call(f32[16,1,128]{2,1,0:T(1,128)S(1)} %all_to_all.5.sums, f32[4,8,2176]{2,1,0:T(8,128)S(1)} %get-tuple-element.19.mine, f32[4,8,2176]{2,1,0:T(8,128)S(1)} %get-tuple-element.20.give, f32[2,4,8,2176]{3,2,1,0:T(8,128)S(1)} %get-tuple-element.22.pairs.refs_0_, ...), custom_call_target="tpu_custom_call" | custom-call | flops 2000000 | bytes 2162688 | tf_op jit(solution)/shard_map/pallas_call | solution.py:438
  (2 shorter events, 0.0 us)
Async XLA Ops:
  0.6 0.8 %copy-start.1 = (s32[4,4096]{1,0:T(4,128)S(1)}, s32[4,4096]{1,0:T(4,128)}, u32[]{:S(2)}) copy-start(s32[4,4096]{1,0:T(4,128)} %refs_1_.3) | copy-start | bytes 196612
  1.5 0.8 %copy-start.2 = (f32[4,4096]{1,0:T(4,128)S(1)}, f32[4,4096]{1,0:T(4,128)}, u32[]{:S(2)}) copy-start(f32[4,4096]{1,0:T(4,128)} %refs_2_.3) | copy-start | bytes 196612
  2.3 0.9 %copy-start.3 = (f32[2,4,4096]{2,1,0:T(4,128)S(1)}, f32[2,4,4096]{2,1,0:T(4,128)}, u32[]{:S(2)}) copy-start(f32[2,4,4096]{2,1,0:T(4,128)} %refs_0_.2) | copy-start | bytes 393220
  3.2 0.9 %copy-start.4 = (s32[2,4,4096]{2,1,0:T(4,128)S(1)}, s32[2,4,4096]{2,1,0:T(4,128)}, u32[]{:S(2)}) copy-start(s32[2,4,4096]{2,1,0:T(4,128)} %refs_1_.2) | copy-start | bytes 393220
  4.1 0.9 %copy-start.5 = (bf16[2,2,4,4096]{3,2,1,0:T(4,128)(2,1)S(1)}, bf16[2,2,4,4096]{3,2,1,0:T(4,128)(2,1)}, u32[]{:S(2)}) copy-start(bf16[2,2,4,4096]{3,2,1,0:T(4,128)(2,1)} %refs_5_.1) | copy-start | bytes 393220
  5.0 0.8 %copy-start.6 = (f32[4,4096]{1,0:T(4,128)S(1)}, f32[4,4096]{1,0:T(4,128)}, u32[]{:S(2)}) copy-start(f32[4,4096]{1,0:T(4,128)} %refs_4_.1) | copy-start | bytes 196612
  6.9 1.9 %collective-permute-start = (f32[4,8,2176]{2,1,0:T(8,128)S(1)}, f32[4,8,2176]{2,1,0:T(8,128)S(1)}, u32[]{:S(2)}, u32[]{:S(2)}) collective-permute-start(f32[4,8,2176]{2,1,0:T(8,128)S(1)} %get-tuple-element.20.give), channel_id=1, source_target_pairs={{0,1},{1,0},{2,3},{3,2},{4,5},{5,4},{6,7},{7,6},{8,9},{9,8},{10,11... | collective-permute-start | bytes 835592 | tf_op jit(solution)/shard_map/ppermute | solution.py:24
  7.4 1.0 %copy-start = (bf16[9,4,4096]{2,1,0:T(4,128)(2,1)S(1)}, bf16[9,4,4096]{2,1,0:T(4,128)(2,1)}, u32[]{:S(2)}) copy-start(bf16[9,4,4096]{2,1,0:T(4,128)(2,1)} %refs_0_.3) | copy-start | bytes 884740
  8.9 5.8 %collective-permute-start.1 = (f32[10,1,2176]{2,1,0:T(1,128)S(1)}, f32[10,1,2176]{2,1,0:T(1,128)S(1)}, u32[]{:S(2)}, u32[]{:S(2)}) collective-permute-start(f32[10,1,2176]{2,1,0:T(1,128)S(1)} %get-tuple-element.25), channel_id=1, source_target_pairs={{0,2},{1,3},{2,0},{3,1},{4,6},{5,7},{6,4},{7,5},{8,10},{9,11},{10,... | collective-permute-start | bytes 261128 | tf_op jit(solution)/shard_map/ppermute | solution.py:24
  11.6 3.1 %collective-permute-start.2 = (f32[10,1,2176]{2,1,0:T(1,128)S(1)}, f32[10,1,2176]{2,1,0:T(1,128)S(1)}, u32[]{:S(2)}, u32[]{:S(2)}) collective-permute-start(f32[10,1,2176]{2,1,0:T(1,128)S(1)} %get-tuple-element.26), channel_id=1, source_target_pairs={{2,4},{3,5},{4,2},{5,3},{6,8},{7,9},{8,6},{9,7},{10,12},{11,13},{1... | collective-permute-start | bytes 261128 | tf_op jit(solution)/shard_map/ppermute | solution.py:24
  18.2 11.2 %collective-permute-start.3 = (f32[18,1,2176]{2,1,0:T(1,128)S(1)}, f32[18,1,2176]{2,1,0:T(1,128)S(1)}, u32[]{:S(2)}, u32[]{:S(2)}) collective-permute-start(f32[18,1,2176]{2,1,0:T(1,128)S(1)} %get-tuple-element.29), channel_id=1, source_target_pairs={{0,2},{1,3},{2,0},{3,1},{4,6},{5,7},{6,4},{7,5},{8,10},{9,11},{10,... | collective-permute-start | bytes 470024 | tf_op jit(solution)/shard_map/ppermute | solution.py:24
  22.9 6.5 %collective-permute-start.4 = (f32[18,1,2176]{2,1,0:T(1,128)S(1)}, f32[18,1,2176]{2,1,0:T(1,128)S(1)}, u32[]{:S(2)}, u32[]{:S(2)}) collective-permute-start(f32[18,1,2176]{2,1,0:T(1,128)S(1)} %get-tuple-element.30), channel_id=1, source_target_pairs={{2,4},{3,5},{4,2},{5,3},{6,8},{7,9},{8,6},{9,7},{10,12},{11,13},{1... | collective-permute-start | bytes 470024 | tf_op jit(solution)/shard_map/ppermute | solution.py:24
  30.2 13.1 %collective-permute-start.5 = (f32[16,8,128]{2,1,0:T(8,128)S(1)}, f32[16,8,128]{2,1,0:T(8,128)S(1)}, u32[]{:S(2)}, u32[]{:S(2)}) collective-permute-start(f32[16,8,128]{2,1,0:T(8,128)S(1)} %get-tuple-element.33), channel_id=1, source_target_pairs={{0,1},{1,0},{2,3},{3,2},{4,5},{5,4},{6,7},{7,6},{8,9},{9,8},{10,11... | collective-permute-start | bytes 196616 | tf_op jit(solution)/shard_map/ppermute | solution.py:24

commit v4 on v3

--- a/solution.py
+++ b/solution.py
@@ -67,7 +67,7 @@
 
 
 def right_sides_kernel(*refs):
-    sources, (mine, give), buffers, semaphores = refs[:6], refs[6:8], refs[8:14], refs[14]
+    sources, (mine, give, cells), buffers, semaphores = refs[:6], refs[6:9], refs[9:15], refs[15]
     fetch(sources, buffers, semaphores)
     observed, gap, sea, precision, noise, perturbation = buffers
     day = lax.axis_index("day")
@@ -79,6 +79,9 @@
             at = dynamic_tile(start, t)
             both = lambda ref, *lead: jnp.concatenate([ref[(*lead, 0, slice(None), at)], ref[(*lead, 1, slice(None), at)]], 0)
             wet = doubled(sea[:, at].astype(F32))
+            if out is mine:
+                cells[0, :, tile(t)] = wet
+                cells[1, :, tile(t)] = doubled(precision[:, at])
             seen = doubled(noise[:, at]) * both(gap).astype(F32)
             base = wet * seen * both(observed)
             spread = wet * jnp.sqrt(doubled(precision[:, at]) + seen)
@@ -88,10 +91,7 @@
             out[3, :, tile(t)] = seen
 
 
-def coefficients_kernel(*refs):
-    sources, (planes, cells), buffers, semaphores = refs[:3], refs[3:5], refs[5:8], refs[8]
-    fetch(sources, buffers, semaphores)
-    stencil, sea, precision = buffers
+def coefficients(stencil, planes):
     day = lax.axis_index("day")
     width = planes.shape[-1]
     tiles = width // LANES
@@ -101,8 +101,6 @@
     for t in range(tiles + 1):
         if t < tiles:
             at = dynamic_tile(start, t)
-            cells[0, :, tile(t)] = doubled(sea[:, at].astype(F32))
-            cells[1, :, tile(t)] = doubled(precision[:, at])
             own = {}
             for a in (-1, 0, 1):
                 for c in (-1, 0, 1):
@@ -180,7 +178,9 @@
     return sums
 
 
-def inside_kernel(mine, got, planes, pairs, moved):
+def inside_kernel(stencil, mine, got, planes, pairs, moved, buffer, semaphores):
+    fetch((stencil,), (buffer,), semaphores)
+    coefficients(buffer, planes)
     day = lax.axis_index("day")
     tiles = mine.shape[-1] // LANES
     row = position(0) % 4
@@ -221,7 +221,8 @@
     tiles = moved.shape[-1] // LANES
     row = position(0)
     low = row < 4
-    for f in range(FIELDS):
+    @pl.loop(0, FIELDS)
+    def _(f):
         incoming = [(Shift(1), Shift(-1)) for _ in (0, 1)]
         scatter = [(Shift(-1), Shift(1)) for _ in (0, 1)]
         leaving = [(Shift(-1), Shift(1)) for _ in (0, 1)]
@@ -231,8 +232,7 @@
                 at = tile(t)
                 for half in (0, 1):
                     rim = placed(above, below, (3 * f, 3 * f + 1) if half == 0 else (3 * f + 2, None), at)
-                    if f > 0:
-                        rims[half, f - 1, :, at] = rim
+                    rims[half, f, :, at] = rim
                     incoming[half][0].push(planes[H_PLANE, :, at] * rim)
                     kept["in", half, t] = planes[H_PLANE + 1, :, at] * rim
                     incoming[half][1].push(planes[H_PLANE + 2, :, at] * rim)
@@ -267,13 +267,14 @@
                 leaves[1, f, :, at] = rolled(out[1], 4, 0)
                 for half in (0, 1):
                     image[half, f, :, at] = cells[0, :, at] * (kept.pop(("own", half)) - after[half])
+
     pack_rows(0, lambda f: (image.at[0, f], image.at[1, f]), paired, crossed)
     pack_rows(9, lambda f: (leaves.at[0, f], leaves.at[1, f]), paired, crossed)
 
 
 def sums_kernel(*refs):
     pairs, part, leaves, planes, cells, first_paired, first_crossed, came_paired, came_crossed = refs[:9]
-    image, rims, swap, sums, sea_above, sea_below, above, below = refs[9:]
+    image, rims, swap, sums, sea_above, sea_below, above, below, kept_sums = refs[9:]
     unpack_rows(first_paired.at[9:10], first_crossed.at[9:10], sea_above, sea_below)
     unpack_rows(came_paired, came_crossed, above, below)
     day = lax.axis_index("day")
@@ -281,8 +282,8 @@
     row = position(0)
     low = row < 4
     edge = (row % 4 == 0) | (row % 4 == 3)
-    rows = []
-    for f in range(FIELDS):
+    @pl.loop(0, FIELDS)
+    def _(f):
         shifts = [(Shift(1), Shift(-1)) for _ in (0, 1)]
         kept = {}
         totals = [None] * 4
@@ -299,8 +300,7 @@
                     z = part[half, f, :, at] - jnp.where(keep, wet * came, 0.0)
                     rim = placed(above, below, days, at) - wet_rim * leaves[half, f, :, at]
                     image[half, f, :, at] = z
-                    if f > 0:
-                        rims[half, f - 1, :, at] = rim
+                    rims[half, f, :, at] = rim
                     up = jnp.where(row % 4 == 0, rim, rolled(z, 1, 0))
                     down = jnp.where(row % 4 == 3, rim, rolled(z, -1, 0))
                     left, centre, right = apply_rows(planes, at, M_PLANE, (up, z, down))
@@ -329,11 +329,14 @@
                 elif q == tiles - 1:
                     terms = [jnp.where(day == 0, 0.0, x) for x in terms]
                 totals = [x if y is None else x + y for x, y in zip(terms, totals)]
-        rows += [jnp.sum(jnp.sum(x, axis=0, keepdims=True), axis=1, keepdims=True) for x in totals]
+        for k, x in enumerate(totals):
+            kept_sums[4 * f + k, :, :] = x
+
     lane = lax.broadcasted_iota(jnp.int32, (1, LANES), 1)
     line = jnp.zeros((1, LANES), F32)
-    for k, x in enumerate(rows):
-        line = jnp.where(lane == k, x, line)
+    for k in range(4 * FIELDS):
+        total = jnp.sum(jnp.sum(kept_sums[k, :, :], axis=0, keepdims=True), axis=1, keepdims=True)
+        line = jnp.where(lane == k, total, line)
     for k in range(sums.shape[0]):
         sums[k, :, :] = line
     for which in (0, 1):
@@ -389,7 +392,7 @@
                 on_side, on_image = weights[f]
                 for half in (0, 1):
                     x = on_side * pairs[half, f, :, at] + on_image * image[half, f, :, at]
-                    rim = on_side * side_rims[half, f - 1, :, at] + on_image * image_rims[half, f - 1, :, at]
+                    rim = on_side * side_rims[half, f, :, at] + on_image * image_rims[half, f, :, at]
                     up = jnp.where(row % 4 == 0, rim, rolled(x, 1, 0))
                     down = jnp.where(row % 4 == 3, rim, rolled(x, -1, 0))
                     box = x + up + down
@@ -433,17 +436,21 @@
 HBM = pl.BlockSpec(memory_space=pltpu.HBM)
 
 
-def call(kernel, outs, *args, scratch=(), source=VMEM, target=VMEM, flops=2_000_000):
+def call(kernel, outs, *args, scratch=(), source=None, target=VMEM, flops=2_000_000):
     size = sum(x.size * x.dtype.itemsize for x in args)
     return pl.pallas_call(
         kernel,
         out_shape=[jax.ShapeDtypeStruct(shape, F32) for shape in outs],
-        in_specs=[source] * len(args),
+        in_specs=source or [VMEM] * len(args),
         out_specs=[target] * len(outs),
         scratch_shapes=scratch,
         cost_estimate=pl.CostEstimate(flops=flops, bytes_accessed=size, transcendentals=0),
         compiler_params=pltpu.CompilerParams(vmem_limit_bytes=32 << 20),
     )(*args)
+
+
+def kept_in_hbm(*args):
+    return tuple(pltpu.with_memory_space_constraint(x, pltpu.HBM) for x in args)
 
 
 def buffers(*args):
@@ -461,28 +468,35 @@
     paired_space = lambda s: s ^ 1
     crossed_space = lambda s: ((s + 1) ^ 1) - 1
 
-    raw = (observed, gap_mask, sea_mask, precision, noise_precision, perturbation)
-    mine, give = call(right_sides_kernel, [(4, *pair)] * 2, *raw, scratch=buffers(*raw), source=HBM)
+    raw = kept_in_hbm(observed, gap_mask, sea_mask, precision, noise_precision, perturbation)
+    mine, give, cells = call(
+        right_sides_kernel, [(4, *pair)] * 2 + [(2, *pair)], *raw, scratch=buffers(*raw), source=[HBM] * len(raw)
+    )
     got = send(give, same, lambda d: 1 - d)
-    raw = (stencil, sea_mask, precision)
-    planes, cells = call(coefficients_kernel, [(PLANES, *pair), (2, *pair)], *raw, scratch=buffers(*raw), source=HBM)
     paired, crossed = call(edges_kernel, [(10, *row)] * 2, mine, got, cells)
+    first_paired = send(paired, paired_space)
     first_crossed = send(crossed, crossed_space)
-    first_paired = send(paired, paired_space)
-    pairs, moved = call(inside_kernel, [(2, 4, *pair), (2, 3, *pair)], mine, got, planes)
+    raw = kept_in_hbm(stencil)
+    planes, pairs, moved = call(
+        inside_kernel,
+        [(PLANES, *pair), (2, 4, *pair), (2, 3, *pair)],
+        *raw, mine, got,
+        scratch=buffers(*raw),
+        source=[HBM, VMEM, VMEM],
+    )
     part, leaves, side_rims, paired, crossed = call(
         image_kernel,
-        [(2, 3, *pair), (2, 3, *pair), (2, 2, *pair), (18, *row), (18, *row)],
+        [(2, 3, *pair)] * 3 + [(18, *row)] * 2,
         pairs, moved, planes, cells, first_paired, first_crossed,
         scratch=[pltpu.VMEM((10, *row), F32)] * 2,
     )
+    paired = send(paired, paired_space)
     crossed = send(crossed, crossed_space)
-    paired = send(paired, paired_space)
     image, image_rims, swap, sums = call(
         sums_kernel,
-        [(2, 3, *pair), (2, 2, *pair), (half // LANES, 8, LANES), (devices, 1, LANES)],
+        [(2, 3, *pair), (2, 3, *pair), (half // LANES, 8, LANES), (devices, 1, LANES)],
         pairs, part, leaves, planes, cells, first_paired, first_crossed, paired, crossed,
-        scratch=[pltpu.VMEM((1, *row), F32)] * 2 + [pltpu.VMEM((18, *row), F32)] * 2,
+        scratch=[pltpu.VMEM((1, *row), F32)] * 2 + [pltpu.VMEM((18, *row), F32)] * 2 + [pltpu.VMEM((4 * FIELDS, 8, LANES), F32)],
     )
     theirs = send(swap, same, lambda d: 1 - d)
     sums = lax.all_to_all(sums, ("space", "day"), 0, 0)

time: 44.8 us -> 38.3 us (0.85)
  local copies, waits for them, and re-layouts: 6.18 us -> 0 us
  waiting for transfers between devices: 7.92 us -> 5.65 us
  blocking collectives: 13 us -> 15.2 us
    unnamed x14 -> x0, local copies, waits for them, and re-layouts: 6.18 us -> none
    ppermute x6, waiting for transfers between devices: 7.92 us -> 5.65 us  [send(): return lax.ppermute(x, ('space', 'day'), pairs)]
    all_to_all x1, blocking collectives: 13 us -> 15.2 us  [shards(): sums = lax.all_to_all(sums, ('space', 'day'), 0, 0)]
    pallas_call x7 -> x6, Pallas kernels: 7.35 us -> 7.06 us  [call(): pl.pallas_call(kernel, out_shape=[jax.ShapeDtypeStruct(shape, F32) for sh...]
  transfers between devices with their start and end apart: 6 -> 6, of which waited for: 2 -> 3; matrix products, arithmetic and copies ran while one was open for 0% -> 0% of each run, Pallas kernels for 2% -> 4%
where the time goes in v4:
time: 38.3 us; the launch traced here: 38.1 us
  blocking collectives  15.2 us (40%)
  starting transfers between devices  9.53 us (25%)
  Pallas kernels  7.06 us (18%)
  waiting for transfers between devices  5.65 us (15%)
  between operations  0.7 us (2%)
    all_to_all x1, blocking collectives, shards(): sums = lax.all_to_all(sums, ('space', 'day'), 0, 0)  15.2 us
    ppermute x6, starting transfers between devices, send(): return lax.ppermute(x, ('space', 'day'), pairs)  9.53 us
    pallas_call x6, Pallas kernels, call(): pl.pallas_call(kernel, out_shape=[jax.ShapeDtypeStruct(shape, F32) for sh...  7.06 us
    ppermute x6, waiting for transfers between devices, send(): return lax.ppermute(x, ('space', 'day'), pairs)  5.65 us
  transfers between devices with their start and end apart: 6, of which 3 were waited for; matrix products, arithmetic and copies ran while one was open for 0% of the time, Pallas kernels for 4%

profile of v4, /device:TPU:0, one launch (start us, length us, event | category | flops | bytes accessed | tf_op | source)
XLA Modules:
  0.0 38.1 jit_solution(6132619607921696492)
XLA Ops:
  0.6 1.4 %shard_map.86 = (f32[4,8,2176]{2,1,0:T(8,128)S(1)}, f32[4,8,2176]{2,1,0:T(8,128)S(1)}, f32[2,8,2176]{2,1,0:T(8,128)S(1)}) custom-call(f32[2,4,4096]{2,1,0:T(4,128)} %refs_0_.1, s32[2,4,4096]{2,1,0:T(4,128)} %refs_1_.1, s32[4,4096]{1,0:T(4,128)} %refs_2_.1, f32[4,4096]{1,0:T(4,128)} %refs_3_.1, f32[4,4096]{1,0:T(4,128)} %refs_4_.1, ...), custom_call_target="tpu_custom_call" | custom-call | flops 2000000 | bytes 589824 | tf_op jit(solution)/shard_map/pallas_call | solution.py:441
  2.0 0.5 %collective-permute-start = (f32[4,8,2176]{2,1,0:T(8,128)S(1)}, f32[4,8,2176]{2,1,0:T(8,128)S(1)}, u32[]{:S(2)}, u32[]{:S(2)}) collective-permute-start(f32[4,8,2176]{2,1,0:T(8,128)S(1)} %get-tuple-element.20.give), channel_id=1, source_target_pairs={{0,1},{1,0},{2,3},{3,2},{4,5},{5,4},{6,7},{7,6},{8,9},{9,8},{10,11... | collective-permute-start | bytes 835592 | tf_op jit(solution)/shard_map/ppermute | solution.py:24
  2.5 1.2 %collective-permute-done.got = f32[4,8,2176]{2,1,0:T(8,128)S(1)} collective-permute-done((f32[4,8,2176]{2,1,0:T(8,128)S(1)}, f32[4,8,2176]{2,1,0:T(8,128)S(1)}, u32[]{:S(2)}, u32[]{:S(2)}) %collective-permute-start) | collective-permute-done | bytes 278560 | tf_op jit(solution)/shard_map/ppermute | solution.py:24
  3.7 0.1 shard_map.88
  3.8 2.9 %collective-permute-start.1 = (f32[10,1,2176]{2,1,0:T(1,128)S(1)}, f32[10,1,2176]{2,1,0:T(1,128)S(1)}, u32[]{:S(2)}, u32[]{:S(2)}) collective-permute-start(f32[10,1,2176]{2,1,0:T(1,128)S(1)} %get-tuple-element.25), channel_id=1, source_target_pairs={{0,2},{1,3},{2,0},{3,1},{4,6},{5,7},{6,4},{7,5},{8,10},{9,11},{10,... | collective-permute-start | bytes 261128 | tf_op jit(solution)/shard_map/ppermute | solution.py:24
  6.7 0.7 %collective-permute-start.2 = (f32[10,1,2176]{2,1,0:T(1,128)S(1)}, f32[10,1,2176]{2,1,0:T(1,128)S(1)}, u32[]{:S(2)}, u32[]{:S(2)}) collective-permute-start(f32[10,1,2176]{2,1,0:T(1,128)S(1)} %get-tuple-element.26), channel_id=1, source_target_pairs={{2,4},{3,5},{4,2},{5,3},{6,8},{7,9},{8,6},{9,7},{10,12},{11,13},{1... | collective-permute-start | bytes 261128 | tf_op jit(solution)/shard_map/ppermute | solution.py:24
  7.4 1.5 %shard_map.87 = (f32[24,8,2176]{2,1,0:T(8,128)S(1)}, f32[2,4,8,2176]{3,2,1,0:T(8,128)S(1)}, f32[2,3,8,2176]{3,2,1,0:T(8,128)S(1)}) custom-call(bf16[9,4,4096]{2,1,0:T(4,128)(2,1)} %stencil.1, f32[4,8,2176]{2,1,0:T(8,128)S(1)} %get-tuple-element.19.mine, f32[4,8,2176]{2,1,0:T(8,128)S(1)} %collective-permute-done.got), custom_call_target="tpu_custom_call" | custom-call | flops 2000000 | bytes 851968 | tf_op jit(solution)/shard_map/pallas_call | solution.py:441
  8.9 0.6 %collective-permute-done.1.came_paired.refs_5_ = f32[10,1,2176]{2,1,0:T(1,128)S(1)} collective-permute-done((f32[10,1,2176]{2,1,0:T(1,128)S(1)}, f32[10,1,2176]{2,1,0:T(1,128)S(1)}, u32[]{:S(2)}, u32[]{:S(2)}) %collective-permute-start.1) | collective-permute-done | bytes 87072 | tf_op jit(solution)/shard_map/ppermute | solution.py:24
  9.6 0.0 collective-permute-done.2.came_crossed.refs_6_
  9.6 2.0 %shard_map.89 = (f32[2,3,8,2176]{3,2,1,0:T(8,128)S(1)}, f32[2,3,8,2176]{3,2,1,0:T(8,128)S(1)}, f32[2,3,8,2176]{3,2,1,0:T(8,128)S(1)}, f32[18,1,2176]{2,1,0:T(1,128)S(1)}, f32[18,1,2176]{2,1,0:T(1,128)S(1)}) custom-call(f32[2,4,8,2176]{3,2,1,0:T(8,128)S(1)} %get-tuple-element.21.pairs.refs_0_, f32[2,3,8,2176]{3,2,1,0:T(8,128)S(1)} %get-tuple-element.22.moved, ...), custom_call_target="tpu_custom_call" | custom-call | flops 2000000 | bytes 2959360 | tf_op jit(solution)/shard_map/pallas_call | solution.py:441
  11.6 4.7 %collective-permute-start.3 = (f32[18,1,2176]{2,1,0:T(1,128)S(1)}, f32[18,1,2176]{2,1,0:T(1,128)S(1)}, u32[]{:S(2)}, u32[]{:S(2)}) collective-permute-start(f32[18,1,2176]{2,1,0:T(1,128)S(1)} %get-tuple-element.29), channel_id=1, source_target_pairs={{0,2},{1,3},{2,0},{3,1},{4,6},{5,7},{6,4},{7,5},{8,10},{9,11},{10,... | collective-permute-start | bytes 470024 | tf_op jit(solution)/shard_map/ppermute | solution.py:24
  16.3 0.7 %collective-permute-start.4 = (f32[18,1,2176]{2,1,0:T(1,128)S(1)}, f32[18,1,2176]{2,1,0:T(1,128)S(1)}, u32[]{:S(2)}, u32[]{:S(2)}) collective-permute-start(f32[18,1,2176]{2,1,0:T(1,128)S(1)} %get-tuple-element.30), channel_id=1, source_target_pairs={{2,4},{3,5},{4,2},{5,3},{6,8},{7,9},{8,6},{9,7},{10,12},{11,13},{1... | collective-permute-start | bytes 470024 | tf_op jit(solution)/shard_map/ppermute | solution.py:24
  16.9 3.8 %collective-permute-done.3.refs_7_ = f32[18,1,2176]{2,1,0:T(1,128)S(1)} collective-permute-done((f32[18,1,2176]{2,1,0:T(1,128)S(1)}, f32[18,1,2176]{2,1,0:T(1,128)S(1)}, u32[]{:S(2)}, u32[]{:S(2)}) %collective-permute-start.3) | collective-permute-done | bytes 156704 | tf_op jit(solution)/shard_map/ppermute | solution.py:24
  20.8 0.0 collective-permute-done.4.refs_8_
  20.8 1.0 %shard_map.90 = (f32[2,3,8,2176]{3,2,1,0:T(8,128)S(1)}, f32[2,3,8,2176]{3,2,1,0:T(8,128)S(1)}, f32[16,8,128]{2,1,0:T(8,128)S(1)}, f32[16,1,128]{2,1,0:T(1,128)S(1)}) custom-call(f32[2,4,8,2176]{3,2,1,0:T(8,128)S(1)} %get-tuple-element.21.pairs.refs_0_, f32[2,3,8,2176]{3,2,1,0:T(8,128)S(1)} %get-tuple-element.27.refs_1_, ...), custom_call_target="tpu_custom_call" | custom-call | flops 2000000 | bytes 3690496 | tf_op jit(solution)/shard_map/pallas_call | solution.py:441
  21.7 0.1 collective-permute-start.5
  21.8 15.2 %all_to_all.5.sums = f32[16,1,128]{2,1,0:T(1,128)S(1)} all-to-all(f32[16,1,128]{2,1,0:T(1,128)S(1)} %get-tuple-element.31), channel_id=1, replica_groups=mesh['region'=2,'space'=8,'day'=2] {'space','day'}, dimensions={0} | all-to-all | bytes 16384 | tf_op jit(solution)/shard_map/all_to_all | solution.py:502
  37.0 0.0 collective-permute-done.5.theirs
  37.0 1.1 %shard_map.91 = (f32[2,4,4096]{2,1,0:T(4,128)}, f32[2,4,2048]{2,1,0:T(4,128)}) custom-call(f32[16,1,128]{2,1,0:T(1,128)S(1)} %all_to_all.5.sums, f32[4,8,2176]{2,1,0:T(8,128)S(1)} %get-tuple-element.19.mine, f32[4,8,2176]{2,1,0:T(8,128)S(1)} %get-tuple-element.20.give, f32[2,4,8,2176]{3,2,1,0:T(8,128)S(1)} %get-tuple-element.21.pairs.refs_0_, ...), custom_call_target="tpu_custom_call" | custom-call | flops 2000000 | bytes 2441216 | tf_op jit(solution)/shard_map/pallas_call | solution.py:441
Async XLA Ops:
  2.0 1.7 %collective-permute-start = (f32[4,8,2176]{2,1,0:T(8,128)S(1)}, f32[4,8,2176]{2,1,0:T(8,128)S(1)}, u32[]{:S(2)}, u32[]{:S(2)}) collective-permute-start(f32[4,8,2176]{2,1,0:T(8,128)S(1)} %get-tuple-element.20.give), channel_id=1, source_target_pairs={{0,1},{1,0},{2,3},{3,2},{4,5},{5,4},{6,7},{7,6},{8,9},{9,8},{10,11... | collective-permute-start | bytes 835592 | tf_op jit(solution)/shard_map/ppermute | solution.py:24
  3.8 5.8 %collective-permute-start.1 = (f32[10,1,2176]{2,1,0:T(1,128)S(1)}, f32[10,1,2176]{2,1,0:T(1,128)S(1)}, u32[]{:S(2)}, u32[]{:S(2)}) collective-permute-start(f32[10,1,2176]{2,1,0:T(1,128)S(1)} %get-tuple-element.25), channel_id=1, source_target_pairs={{0,2},{1,3},{2,0},{3,1},{4,6},{5,7},{6,4},{7,5},{8,10},{9,11},{10,... | collective-permute-start | bytes 261128 | tf_op jit(solution)/shard_map/ppermute | solution.py:24
  6.7 2.9 %collective-permute-start.2 = (f32[10,1,2176]{2,1,0:T(1,128)S(1)}, f32[10,1,2176]{2,1,0:T(1,128)S(1)}, u32[]{:S(2)}, u32[]{:S(2)}) collective-permute-start(f32[10,1,2176]{2,1,0:T(1,128)S(1)} %get-tuple-element.26), channel_id=1, source_target_pairs={{2,4},{3,5},{4,2},{5,3},{6,8},{7,9},{8,6},{9,7},{10,12},{11,13},{1... | collective-permute-start | bytes 261128 | tf_op jit(solution)/shard_map/ppermute | solution.py:24
  11.6 9.2 %collective-permute-start.3 = (f32[18,1,2176]{2,1,0:T(1,128)S(1)}, f32[18,1,2176]{2,1,0:T(1,128)S(1)}, u32[]{:S(2)}, u32[]{:S(2)}) collective-permute-start(f32[18,1,2176]{2,1,0:T(1,128)S(1)} %get-tuple-element.29), channel_id=1, source_target_pairs={{0,2},{1,3},{2,0},{3,1},{4,6},{5,7},{6,4},{7,5},{8,10},{9,11},{10,... | collective-permute-start | bytes 470024 | tf_op jit(solution)/shard_map/ppermute | solution.py:24
  16.3 4.5 %collective-permute-start.4 = (f32[18,1,2176]{2,1,0:T(1,128)S(1)}, f32[18,1,2176]{2,1,0:T(1,128)S(1)}, u32[]{:S(2)}, u32[]{:S(2)}) collective-permute-start(f32[18,1,2176]{2,1,0:T(1,128)S(1)} %get-tuple-element.30), channel_id=1, source_target_pairs={{2,4},{3,5},{4,2},{5,3},{6,8},{7,9},{8,6},{9,7},{10,12},{11,13},{1... | collective-permute-start | bytes 470024 | tf_op jit(solution)/shard_map/ppermute | solution.py:24
  21.7 15.3 %collective-permute-start.5 = (f32[16,8,128]{2,1,0:T(8,128)S(1)}, f32[16,8,128]{2,1,0:T(8,128)S(1)}, u32[]{:S(2)}, u32[]{:S(2)}) collective-permute-start(f32[16,8,128]{2,1,0:T(8,128)S(1)} %get-tuple-element.33), channel_id=1, source_target_pairs={{0,1},{1,0},{2,3},{3,2},{4,5},{5,4},{6,7},{7,6},{8,9},{9,8},{10,11... | collective-permute-start | bytes 196616 | tf_op jit(solution)/shard_map/ppermute | solution.py:24

commit v5 on v4

--- a/solution.py
+++ b/solution.py
@@ -10,7 +10,7 @@
 FIELDS = 3
 F32 = jnp.float32
 
-M_PLANE, T_PLANE, Q_PLANE, H_PLANE, PLANES = 0, 9, 18, 21, 24
+M_PLANE, H_PLANE, PLANES = 0, 9, 12
 
 
 def send(x, space_of, day_of=lambda d: d):
@@ -92,35 +92,26 @@
 
 
 def coefficients(stencil, planes):
-    day = lax.axis_index("day")
     width = planes.shape[-1]
     tiles = width // LANES
-    start = day * (stencil.shape[-1] - width)
+    start = lax.axis_index("day") * (stencil.shape[-1] - width)
     row = position(0) % 4
     shifts = {(a, c): Shift(c) for a in (-1, 0, 1) for c in (-1, 1)}
+    middle = {}
     for t in range(tiles + 1):
         if t < tiles:
             at = dynamic_tile(start, t)
-            own = {}
             for a in (-1, 0, 1):
                 for c in (-1, 0, 1):
-                    k = 3 * (a + 1) + c + 1
-                    s = doubled(stencil[k, :, at].astype(F32))
-                    own[a, c] = s
-                    moved = s if a == 0 else jnp.where(row == (0 if a > 0 else 3), 0.0, rolled(s, a, 0))
-                    planes[T_PLANE + k, :, tile(t)] = moved
+                    s = doubled(stencil[3 * (a + 1) + c + 1, :, at].astype(F32))
                     if c == 0:
-                        planes[M_PLANE + k, :, tile(t)] = s
+                        middle[a, t] = s
                     else:
                         shifts[a, c].push(s)
+        if t >= 1:
             for c in (-1, 0, 1):
-                planes[Q_PLANE + c + 1, :, tile(t)] = jnp.where(row == 0, own[-1, c], jnp.where(row == 3, own[1, c], 0.0))
-            planes[H_PLANE + 1, :, tile(t)] = jnp.where(row == 0, own[-1, 0], jnp.where(row == 3, own[1, 0], 0.0))
-        if t >= 1:
-            for c in (-1, 1):
-                got = {}
+                got = {a: shifts[a, c].take(t - 1) if c else middle.pop((a, t - 1)) for a in (-1, 0, 1)}
                 for a in (-1, 0, 1):
-                    got[a] = shifts[a, c].take(t - 1)
                     planes[M_PLANE + 3 * (a + 1) + c + 1, :, tile(t - 1)] = got[a]
                 planes[H_PLANE + c + 1, :, tile(t - 1)] = jnp.where(row == 0, got[-1], jnp.where(row == 3, got[1], 0.0))
 
@@ -168,12 +159,22 @@
             crossed[9, :, :] = cells[0, 0:1, :] if even else cells[0, 3:4, :]
 
 
-def apply_rows(planes, at, base, terms):
+def apply_rows(planes, at, terms):
     sums = []
     for c in (0, 1, 2):
-        total = planes[base + c, :, at] * terms[0]
-        total = total + planes[base + 3 + c, :, at] * terms[1]
-        total = total + planes[base + 6 + c, :, at] * terms[2]
+        total = planes[M_PLANE + c, :, at] * terms[0]
+        total = total + planes[M_PLANE + 3 + c, :, at] * terms[1]
+        total = total + planes[M_PLANE + 6 + c, :, at] * terms[2]
+        sums.append(total)
+    return sums
+
+
+def apply_columns(planes, at, terms):
+    sums = []
+    for a in (0, 3, 6):
+        total = planes[M_PLANE + a, :, at] * terms[0]
+        total = total + planes[M_PLANE + a + 1, :, at] * terms[1]
+        total = total + planes[M_PLANE + a + 2, :, at] * terms[2]
         sums.append(total)
     return sums
 
@@ -197,7 +198,7 @@
                     if f < FIELDS:
                         up = jnp.where(row == 0, 0.0, rolled(u, 1, 0))
                         down = jnp.where(row == 3, 0.0, rolled(u, -1, 0))
-                        left, centre, right = apply_rows(planes, tile(t), M_PLANE, (up, u, down))
+                        left, centre, right = apply_rows(planes, tile(t), (up, u, down))
                         shifts[0].push(left)
                         shifts[1].push(right)
                         middle.append(centre)
@@ -221,11 +222,12 @@
     tiles = moved.shape[-1] // LANES
     row = position(0)
     low = row < 4
+    edge = row % 4
+
     @pl.loop(0, FIELDS)
     def _(f):
         incoming = [(Shift(1), Shift(-1)) for _ in (0, 1)]
-        scatter = [(Shift(-1), Shift(1)) for _ in (0, 1)]
-        leaving = [(Shift(-1), Shift(1)) for _ in (0, 1)]
+        beside = [(Shift(-1), Shift(1)) for _ in (0, 1)]
         kept = {}
         for t in range(tiles + 2):
             if t < tiles:
@@ -247,21 +249,18 @@
                 for half in (0, 1):
                     u = pairs[half, f, :, at]
                     w = cells[1, :, at] * (u - before[half])
-                    left, centre, right = apply_rows(planes, at, T_PLANE, (rolled(w, -1, 0), w, rolled(w, 1, 0)))
-                    scatter[half][0].push(left)
-                    scatter[half][1].push(right)
-                    leaving[half][0].push(planes[Q_PLANE, :, at] * w)
-                    leaving[half][1].push(planes[Q_PLANE + 2, :, at] * w)
-                    kept[half, q] = (w + pairs[half, FIELDS, :, at] * u, centre, planes[Q_PLANE + 1, :, at] * w)
+                    beside[half][0].push(w)
+                    beside[half][1].push(w)
+                    kept[half, q] = (w, w + pairs[half, FIELDS, :, at] * u)
             if t >= 2:
                 q = t - 2
                 at = tile(q)
                 s, out = [], []
                 for half in (0, 1):
-                    own, centre, edge = kept.pop((half, q))
-                    s.append(centre + scatter[half][0].take(q) + scatter[half][1].take(q))
-                    out.append(edge + leaving[half][0].take(q) + leaving[half][1].take(q))
-                    kept["own", half] = own
+                    w, kept["own", half] = kept.pop((half, q))
+                    up, stay, down = apply_columns(planes, at, (beside[half][0].take(q), w, beside[half][1].take(q)))
+                    s.append(stay + jnp.where(edge == 3, 0.0, rolled(up, -1, 0)) + jnp.where(edge == 0, 0.0, rolled(down, 1, 0)))
+                    out.append(jnp.where(edge == 0, up, down))
                 after = (rolled(jnp.where(low, s[1], s[0]), 4, 0), jnp.where(low, rolled(s[1], 4, 0), 0.0))
                 leaves[0, f, :, at] = rolled(jnp.where(low, out[1], out[0]), 4, 0)
                 leaves[1, f, :, at] = rolled(out[1], 4, 0)
@@ -282,6 +281,7 @@
     row = position(0)
     low = row < 4
     edge = (row % 4 == 0) | (row % 4 == 3)
+
     @pl.loop(0, FIELDS)
     def _(f):
         shifts = [(Shift(1), Shift(-1)) for _ in (0, 1)]
@@ -303,7 +303,7 @@
                     rims[half, f, :, at] = rim
                     up = jnp.where(row % 4 == 0, rim, rolled(z, 1, 0))
                     down = jnp.where(row % 4 == 3, rim, rolled(z, -1, 0))
-                    left, centre, right = apply_rows(planes, at, M_PLANE, (up, z, down))
+                    left, centre, right = apply_rows(planes, at, (up, z, down))
                     shifts[half][0].push(left)
                     shifts[half][1].push(right)
                     kept[half, t] = (z, centre)

time: 38.3 us -> 37.5 us (0.979)
  Pallas kernels: 7.06 us -> 6.25 us
    pallas_call x6, Pallas kernels: 7.06 us -> 6.25 us  [call(): pl.pallas_call(kernel, out_shape=[jax.ShapeDtypeStruct(shape, F32) for sh...]
where the time goes in v5:
time: 37.5 us; the launch traced here: 37.3 us
  blocking collectives  15.2 us (41%)
  starting transfers between devices  9.53 us (25%)
  Pallas kernels  6.25 us (17%)
  waiting for transfers between devices  5.66 us (15%)
  between operations  0.7 us (2%)
    all_to_all x1, blocking collectives, shards(): sums = lax.all_to_all(sums, ('space', 'day'), 0, 0)  15.2 us
    ppermute x6, starting transfers between devices, send(): return lax.ppermute(x, ('space', 'day'), pairs)  9.53 us
    pallas_call x6, Pallas kernels, call(): pl.pallas_call(kernel, out_shape=[jax.ShapeDtypeStruct(shape, F32) for sh...  6.25 us
    ppermute x6, waiting for transfers between devices, send(): return lax.ppermute(x, ('space', 'day'), pairs)  5.66 us
  transfers between devices with their start and end apart: 6, of which 3 were waited for; matrix products, arithmetic and copies ran while one was open for 0% of the time, Pallas kernels for 4%

profile of v5, /device:TPU:0, one launch (start us, length us, event | category | flops | bytes accessed | tf_op | source)
XLA Modules:
  0.0 37.3 jit_solution(10606155915817341202)
XLA Ops:
  0.6 1.4 %shard_map.86 = (f32[4,8,2176]{2,1,0:T(8,128)S(1)}, f32[4,8,2176]{2,1,0:T(8,128)S(1)}, f32[2,8,2176]{2,1,0:T(8,128)S(1)}) custom-call(f32[2,4,4096]{2,1,0:T(4,128)} %refs_0_.1, s32[2,4,4096]{2,1,0:T(4,128)} %refs_1_.1, s32[4,4096]{1,0:T(4,128)} %refs_2_.1, f32[4,4096]{1,0:T(4,128)} %refs_3_.1, f32[4,4096]{1,0:T(4,128)} %refs_4_.1, ...), custom_call_target="tpu_custom_call" | custom-call | flops 2000000 | bytes 589824 | tf_op jit(solution)/shard_map/pallas_call | solution.py:441
  2.0 0.5 %collective-permute-start = (f32[4,8,2176]{2,1,0:T(8,128)S(1)}, f32[4,8,2176]{2,1,0:T(8,128)S(1)}, u32[]{:S(2)}, u32[]{:S(2)}) collective-permute-start(f32[4,8,2176]{2,1,0:T(8,128)S(1)} %get-tuple-element.20.give), channel_id=1, source_target_pairs={{0,1},{1,0},{2,3},{3,2},{4,5},{5,4},{6,7},{7,6},{8,9},{9,8},{10,11... | collective-permute-start | bytes 835592 | tf_op jit(solution)/shard_map/ppermute | solution.py:24
  2.5 1.2 %collective-permute-done.got = f32[4,8,2176]{2,1,0:T(8,128)S(1)} collective-permute-done((f32[4,8,2176]{2,1,0:T(8,128)S(1)}, f32[4,8,2176]{2,1,0:T(8,128)S(1)}, u32[]{:S(2)}, u32[]{:S(2)}) %collective-permute-start) | collective-permute-done | bytes 278560 | tf_op jit(solution)/shard_map/ppermute | solution.py:24
  3.7 0.1 shard_map.88
  3.8 2.9 %collective-permute-start.1 = (f32[10,1,2176]{2,1,0:T(1,128)S(1)}, f32[10,1,2176]{2,1,0:T(1,128)S(1)}, u32[]{:S(2)}, u32[]{:S(2)}) collective-permute-start(f32[10,1,2176]{2,1,0:T(1,128)S(1)} %get-tuple-element.25), channel_id=1, source_target_pairs={{0,2},{1,3},{2,0},{3,1},{4,6},{5,7},{6,4},{7,5},{8,10},{9,11},{10,... | collective-permute-start | bytes 261128 | tf_op jit(solution)/shard_map/ppermute | solution.py:24
  6.7 0.7 %collective-permute-start.2 = (f32[10,1,2176]{2,1,0:T(1,128)S(1)}, f32[10,1,2176]{2,1,0:T(1,128)S(1)}, u32[]{:S(2)}, u32[]{:S(2)}) collective-permute-start(f32[10,1,2176]{2,1,0:T(1,128)S(1)} %get-tuple-element.26), channel_id=1, source_target_pairs={{2,4},{3,5},{4,2},{5,3},{6,8},{7,9},{8,6},{9,7},{10,12},{11,13},{1... | collective-permute-start | bytes 261128 | tf_op jit(solution)/shard_map/ppermute | solution.py:24
  7.4 1.5 %shard_map.87 = (f32[12,8,2176]{2,1,0:T(8,128)S(1)}, f32[2,4,8,2176]{3,2,1,0:T(8,128)S(1)}, f32[2,3,8,2176]{3,2,1,0:T(8,128)S(1)}) custom-call(bf16[9,4,4096]{2,1,0:T(4,128)(2,1)} %stencil.1, f32[4,8,2176]{2,1,0:T(8,128)S(1)} %get-tuple-element.19.mine, f32[4,8,2176]{2,1,0:T(8,128)S(1)} %collective-permute-done.got), custom_call_target="tpu_custom_call" | custom-call | flops 2000000 | bytes 851968 | tf_op jit(solution)/shard_map/pallas_call | solution.py:441
  8.9 0.7 %collective-permute-done.1.came_paired.refs_5_ = f32[10,1,2176]{2,1,0:T(1,128)S(1)} collective-permute-done((f32[10,1,2176]{2,1,0:T(1,128)S(1)}, f32[10,1,2176]{2,1,0:T(1,128)S(1)}, u32[]{:S(2)}, u32[]{:S(2)}) %collective-permute-start.1) | collective-permute-done | bytes 87072 | tf_op jit(solution)/shard_map/ppermute | solution.py:24
  9.6 0.0 collective-permute-done.2.came_crossed.refs_6_
  9.6 1.2 %shard_map.89 = (f32[2,3,8,2176]{3,2,1,0:T(8,128)S(1)}, f32[2,3,8,2176]{3,2,1,0:T(8,128)S(1)}, f32[2,3,8,2176]{3,2,1,0:T(8,128)S(1)}, f32[18,1,2176]{2,1,0:T(1,128)S(1)}, f32[18,1,2176]{2,1,0:T(1,128)S(1)}) custom-call(f32[2,4,8,2176]{3,2,1,0:T(8,128)S(1)} %get-tuple-element.21.pairs.refs_0_, f32[2,3,8,2176]{3,2,1,0:T(8,128)S(1)} %get-tuple-element.22.moved, ...), custom_call_target="tpu_custom_call" | custom-call | flops 2000000 | bytes 2123776 | tf_op jit(solution)/shard_map/pallas_call | solution.py:441
  10.8 4.7 %collective-permute-start.3 = (f32[18,1,2176]{2,1,0:T(1,128)S(1)}, f32[18,1,2176]{2,1,0:T(1,128)S(1)}, u32[]{:S(2)}, u32[]{:S(2)}) collective-permute-start(f32[18,1,2176]{2,1,0:T(1,128)S(1)} %get-tuple-element.29), channel_id=1, source_target_pairs={{0,2},{1,3},{2,0},{3,1},{4,6},{5,7},{6,4},{7,5},{8,10},{9,11},{10,... | collective-permute-start | bytes 470024 | tf_op jit(solution)/shard_map/ppermute | solution.py:24
  15.5 0.7 %collective-permute-start.4 = (f32[18,1,2176]{2,1,0:T(1,128)S(1)}, f32[18,1,2176]{2,1,0:T(1,128)S(1)}, u32[]{:S(2)}, u32[]{:S(2)}) collective-permute-start(f32[18,1,2176]{2,1,0:T(1,128)S(1)} %get-tuple-element.30), channel_id=1, source_target_pairs={{2,4},{3,5},{4,2},{5,3},{6,8},{7,9},{8,6},{9,7},{10,12},{11,13},{1... | collective-permute-start | bytes 470024 | tf_op jit(solution)/shard_map/ppermute | solution.py:24
  16.1 3.8 %collective-permute-done.3.refs_7_ = f32[18,1,2176]{2,1,0:T(1,128)S(1)} collective-permute-done((f32[18,1,2176]{2,1,0:T(1,128)S(1)}, f32[18,1,2176]{2,1,0:T(1,128)S(1)}, u32[]{:S(2)}, u32[]{:S(2)}) %collective-permute-start.3) | collective-permute-done | bytes 156704 | tf_op jit(solution)/shard_map/ppermute | solution.py:24
  20.0 0.0 collective-permute-done.4.refs_8_
  20.0 1.0 %shard_map.90 = (f32[2,3,8,2176]{3,2,1,0:T(8,128)S(1)}, f32[2,3,8,2176]{3,2,1,0:T(8,128)S(1)}, f32[16,8,128]{2,1,0:T(8,128)S(1)}, f32[16,1,128]{2,1,0:T(1,128)S(1)}) custom-call(f32[2,4,8,2176]{3,2,1,0:T(8,128)S(1)} %get-tuple-element.21.pairs.refs_0_, f32[2,3,8,2176]{3,2,1,0:T(8,128)S(1)} %get-tuple-element.27.refs_1_, ...), custom_call_target="tpu_custom_call" | custom-call | flops 2000000 | bytes 2854912 | tf_op jit(solution)/shard_map/pallas_call | solution.py:441
  20.9 0.1 collective-permute-start.5
  21.0 15.2 %all_to_all.5.sums = f32[16,1,128]{2,1,0:T(1,128)S(1)} all-to-all(f32[16,1,128]{2,1,0:T(1,128)S(1)} %get-tuple-element.31), channel_id=1, replica_groups=mesh['region'=2,'space'=8,'day'=2] {'space','day'}, dimensions={0} | all-to-all | bytes 16384 | tf_op jit(solution)/shard_map/all_to_all | solution.py:502
  36.2 0.0 collective-permute-done.5.theirs
  36.2 1.1 %shard_map.91 = (f32[2,4,4096]{2,1,0:T(4,128)}, f32[2,4,2048]{2,1,0:T(4,128)}) custom-call(f32[16,1,128]{2,1,0:T(1,128)S(1)} %all_to_all.5.sums, f32[4,8,2176]{2,1,0:T(8,128)S(1)} %get-tuple-element.19.mine, f32[4,8,2176]{2,1,0:T(8,128)S(1)} %get-tuple-element.20.give, f32[2,4,8,2176]{3,2,1,0:T(8,128)S(1)} %get-tuple-element.21.pairs.refs_0_, ...), custom_call_target="tpu_custom_call" | custom-call | flops 2000000 | bytes 2441216 | tf_op jit(solution)/shard_map/pallas_call | solution.py:441
Async XLA Ops:
  2.0 1.7 %collective-permute-start = (f32[4,8,2176]{2,1,0:T(8,128)S(1)}, f32[4,8,2176]{2,1,0:T(8,128)S(1)}, u32[]{:S(2)}, u32[]{:S(2)}) collective-permute-start(f32[4,8,2176]{2,1,0:T(8,128)S(1)} %get-tuple-element.20.give), channel_id=1, source_target_pairs={{0,1},{1,0},{2,3},{3,2},{4,5},{5,4},{6,7},{7,6},{8,9},{9,8},{10,11... | collective-permute-start | bytes 835592 | tf_op jit(solution)/shard_map/ppermute | solution.py:24
  3.8 5.8 %collective-permute-start.1 = (f32[10,1,2176]{2,1,0:T(1,128)S(1)}, f32[10,1,2176]{2,1,0:T(1,128)S(1)}, u32[]{:S(2)}, u32[]{:S(2)}) collective-permute-start(f32[10,1,2176]{2,1,0:T(1,128)S(1)} %get-tuple-element.25), channel_id=1, source_target_pairs={{0,2},{1,3},{2,0},{3,1},{4,6},{5,7},{6,4},{7,5},{8,10},{9,11},{10,... | collective-permute-start | bytes 261128 | tf_op jit(solution)/shard_map/ppermute | solution.py:24
  6.7 2.9 %collective-permute-start.2 = (f32[10,1,2176]{2,1,0:T(1,128)S(1)}, f32[10,1,2176]{2,1,0:T(1,128)S(1)}, u32[]{:S(2)}, u32[]{:S(2)}) collective-permute-start(f32[10,1,2176]{2,1,0:T(1,128)S(1)} %get-tuple-element.26), channel_id=1, source_target_pairs={{2,4},{3,5},{4,2},{5,3},{6,8},{7,9},{8,6},{9,7},{10,12},{11,13},{1... | collective-permute-start | bytes 261128 | tf_op jit(solution)/shard_map/ppermute | solution.py:24
  10.8 9.2 %collective-permute-start.3 = (f32[18,1,2176]{2,1,0:T(1,128)S(1)}, f32[18,1,2176]{2,1,0:T(1,128)S(1)}, u32[]{:S(2)}, u32[]{:S(2)}) collective-permute-start(f32[18,1,2176]{2,1,0:T(1,128)S(1)} %get-tuple-element.29), channel_id=1, source_target_pairs={{0,2},{1,3},{2,0},{3,1},{4,6},{5,7},{6,4},{7,5},{8,10},{9,11},{10,... | collective-permute-start | bytes 470024 | tf_op jit(solution)/shard_map/ppermute | solution.py:24
  15.5 4.5 %collective-permute-start.4 = (f32[18,1,2176]{2,1,0:T(1,128)S(1)}, f32[18,1,2176]{2,1,0:T(1,128)S(1)}, u32[]{:S(2)}, u32[]{:S(2)}) collective-permute-start(f32[18,1,2176]{2,1,0:T(1,128)S(1)} %get-tuple-element.30), channel_id=1, source_target_pairs={{2,4},{3,5},{4,2},{5,3},{6,8},{7,9},{8,6},{9,7},{10,12},{11,13},{1... | collective-permute-start | bytes 470024 | tf_op jit(solution)/shard_map/ppermute | solution.py:24
  20.9 15.3 %collective-permute-start.5 = (f32[16,8,128]{2,1,0:T(8,128)S(1)}, f32[16,8,128]{2,1,0:T(8,128)S(1)}, u32[]{:S(2)}, u32[]{:S(2)}) collective-permute-start(f32[16,8,128]{2,1,0:T(8,128)S(1)} %get-tuple-element.33), channel_id=1, source_target_pairs={{0,1},{1,0},{2,3},{3,2},{4,5},{5,4},{6,7},{7,6},{8,9},{9,8},{10,11... | collective-permute-start | bytes 196616 | tf_op jit(solution)/shard_map/ppermute | solution.py:24

commit v6 on v5

--- a/solution.py
+++ b/solution.py
@@ -217,7 +217,13 @@
     return out
 
 
-def image_kernel(pairs, moved, planes, cells, came_paired, came_crossed, image, leaves, rims, paired, crossed, above, below):
+def total(x):
+    return jnp.sum(jnp.sum(x, axis=0, keepdims=True), axis=1, keepdims=True)
+
+
+def image_kernel(*refs):
+    pairs, moved, planes, cells, came_paired, came_crossed = refs[:6]
+    image, leaves, rims, gaps, centres, paired, crossed, above, below = refs[6:]
     unpack_rows(came_paired, came_crossed, above, below)
     tiles = moved.shape[-1] // LANES
     row = position(0)
@@ -229,6 +235,7 @@
         incoming = [(Shift(1), Shift(-1)) for _ in (0, 1)]
         beside = [(Shift(-1), Shift(1)) for _ in (0, 1)]
         kept = {}
+        along = square = jnp.zeros((8, LANES), F32)
         for t in range(tiles + 2):
             if t < tiles:
                 at = tile(t)
@@ -248,7 +255,9 @@
                 before = (jnp.where(low, 0.0, rolled(m[0], 4, 0)), rolled(jnp.where(low, m[1], m[0]), 4, 0))
                 for half in (0, 1):
                     u = pairs[half, f, :, at]
-                    w = cells[1, :, at] * (u - before[half])
+                    gap = u - before[half]
+                    gaps[half, f, :, at] = gap
+                    w = cells[1, :, at] * gap
                     beside[half][0].push(w)
                     beside[half][1].push(w)
                     kept[half, q] = (w, w + pairs[half, FIELDS, :, at] * u)
@@ -265,15 +274,23 @@
                 leaves[0, f, :, at] = rolled(jnp.where(low, out[1], out[0]), 4, 0)
                 leaves[1, f, :, at] = rolled(out[1], 4, 0)
                 for half in (0, 1):
-                    image[half, f, :, at] = cells[0, :, at] * (kept.pop(("own", half)) - after[half])
+                    z = cells[0, :, at] * (kept.pop(("own", half)) - after[half])
+                    image[half, f, :, at] = z
+                    u = pairs[half, f, :, at]
+                    along = along + u * z
+                    square = square + u * u
+        along, square = total(along), total(square)
+        centre = jnp.where(square > 0.0, along / jnp.where(square > 0.0, square, 1.0), 0.0)
+        centres[f, :, :] = jnp.broadcast_to(centre, (8, LANES))
 
     pack_rows(0, lambda f: (image.at[0, f], image.at[1, f]), paired, crossed)
     pack_rows(9, lambda f: (leaves.at[0, f], leaves.at[1, f]), paired, crossed)
 
 
 def sums_kernel(*refs):
-    pairs, part, leaves, planes, cells, first_paired, first_crossed, came_paired, came_crossed = refs[:9]
-    image, rims, swap, sums, sea_above, sea_below, above, below, kept_sums = refs[9:]
+    pairs, part, leaves, gaps, centres, planes, cells = refs[:7]
+    first_paired, first_crossed, came_paired, came_crossed = refs[7:11]
+    image, rims, swap, sums, sea_above, sea_below, above, below, kept_sums = refs[11:]
     unpack_rows(first_paired.at[9:10], first_crossed.at[9:10], sea_above, sea_below)
     unpack_rows(came_paired, came_crossed, above, below)
     day = lax.axis_index("day")
@@ -286,7 +303,8 @@
     def _(f):
         shifts = [(Shift(1), Shift(-1)) for _ in (0, 1)]
         kept = {}
-        totals = [None] * 4
+        totals = [None] * 6
+        ratio = centres[f, :, :]
         for t in range(tiles + 1):
             if t < tiles:
                 at = tile(t)
@@ -316,27 +334,36 @@
                     z.append(own)
                     m.append(centre + shifts[half][0].take(q) + shifts[half][1].take(q))
                 before = (jnp.where(low, 0.0, rolled(m[0], 4, 0)), rolled(jnp.where(low, m[1], m[0]), 4, 0))
-                terms = [0.0] * 4
+                terms = [0.0] * 6
                 for half in (0, 1):
                     b = pairs[half, f, :, at]
-                    gap = z[half] - before[half]
-                    terms[0] = terms[0] + b * b
-                    terms[1] = terms[1] + b * z[half]
-                    terms[2] = terms[2] + z[half] * z[half]
-                    terms[3] = terms[3] + (cells[1, :, at] * gap * gap + pairs[half, FIELDS, :, at] * z[half] * z[half])
+                    y = z[half] - ratio * b
+                    seen, gap = pairs[half, FIELDS, :, at], gaps[half, f, :, at]
+                    weighted = cells[1, :, at] * gap
+                    beside = (z[half] - before[half]) - ratio * gap
+                    products = (
+                        b * b,
+                        b * y,
+                        y * y,
+                        weighted * gap + seen * b * b,
+                        weighted * beside + seen * b * y,
+                        cells[1, :, at] * beside * beside + seen * y * y,
+                    )
+                    terms = [x + product for x, product in zip(terms, products)]
                 if q == 0:
                     terms = [jnp.where(day == 0, x, 0.0) for x in terms]
                 elif q == tiles - 1:
                     terms = [jnp.where(day == 0, 0.0, x) for x in terms]
                 totals = [x if y is None else x + y for x, y in zip(terms, totals)]
         for k, x in enumerate(totals):
-            kept_sums[4 * f + k, :, :] = x
+            kept_sums[3 * k + f, :, :] = x
 
     lane = lax.broadcasted_iota(jnp.int32, (1, LANES), 1)
     line = jnp.zeros((1, LANES), F32)
-    for k in range(4 * FIELDS):
-        total = jnp.sum(jnp.sum(kept_sums[k, :, :], axis=0, keepdims=True), axis=1, keepdims=True)
-        line = jnp.where(lane == k, total, line)
+    for k in range(6 * FIELDS):
+        line = jnp.where(lane == k, total(kept_sums[k, :, :]), line)
+    for f in range(FIELDS):
+        line = jnp.where(lane == 6 * FIELDS + f, centres[f, 0:1, :], line)
     for k in range(sums.shape[0]):
         sums[k, :, :] = line
     for which in (0, 1):
@@ -347,23 +374,29 @@
                 swap[t, :, :] = image[1 - which, 0, :, tile(t + which)]
 
 
-def fit_kernel(sums, mine, give, pairs, image, theirs, side_rims, image_rims, posterior, fitted, mean, cells, ready, semaphores):
+def fit_kernel(sums, mine, give, pairs, image, theirs, side_rims, image_rims, posterior, fitted, mean, cells, ready, lines, semaphores):
     day = lax.axis_index("day")
     tiles = mine.shape[-1] // LANES
     row = position(0)
     low = row < 4
-    line = sums[0, :, :]
-    for k in range(1, sums.shape[0]):
-        line = line + sums[k, :, :]
-    weights = []
-    for f in range(FIELDS):
-        m = [jnp.broadcast_to(line[:, k : k + 1], (8, LANES)) for k in range(4 * f, 4 * f + 4)]
-        step = m[0] / m[1]
-        norm_next = step * step * m[2] - m[0]
-        grown = 1.0 + norm_next / m[0]
-        curvature = grown * grown * m[1] - 2.0 * step * grown * m[2] + step * step * m[3]
-        second = norm_next / curvature
-        weights.append((step + second * grown, -second * step))
+    for k in range(sums.shape[0]):
+        lines[k : k + 1, :] = sums[k, :, :]
+    own = [lines[...]] + [rolled(lines[...], -3 * k, 1) for k in range(1, 7)]
+    side_side, side_off, off_off, side_energy, cross_energy, off_energy, centre = own
+    add = lambda x: jnp.sum(x, axis=0, keepdims=True)
+    norm = add(side_side)
+    ratio = add(centre * side_side + side_off) / norm
+    move = ratio - centre
+    off_norm = add(off_off - 2.0 * move * side_off + move * move * side_side)
+    off_energy = add(off_energy - 2.0 * move * cross_energy + move * move * side_energy)
+    cross_energy = add(cross_energy - move * side_energy)
+    step = 1.0 / ratio
+    norm_next = step * step * off_norm
+    grown = norm_next / norm
+    curvature = step * step * off_energy - 2.0 * step * grown * cross_energy + grown * grown * add(side_energy)
+    second = norm_next / curvature
+    on_both = (step + second * (1.0 + grown), -second * step)
+    weights = [[jnp.broadcast_to(x[:, f : f + 1], (8, LANES)) for x in on_both] for f in range(FIELDS)]
 
     def store(at, x):
         mean[0, :, at] = x[0:4]
@@ -484,9 +517,9 @@
         scratch=buffers(*raw),
         source=[HBM, VMEM, VMEM],
     )
-    part, leaves, side_rims, paired, crossed = call(
+    part, leaves, side_rims, gaps, centres, paired, crossed = call(
         image_kernel,
-        [(2, 3, *pair)] * 3 + [(18, *row)] * 2,
+        [(2, 3, *pair)] * 4 + [(FIELDS, 8, LANES)] + [(18, *row)] * 2,
         pairs, moved, planes, cells, first_paired, first_crossed,
         scratch=[pltpu.VMEM((10, *row), F32)] * 2,
     )
@@ -495,8 +528,8 @@
     image, image_rims, swap, sums = call(
         sums_kernel,
         [(2, 3, *pair), (2, 3, *pair), (half // LANES, 8, LANES), (devices, 1, LANES)],
-        pairs, part, leaves, planes, cells, first_paired, first_crossed, paired, crossed,
-        scratch=[pltpu.VMEM((1, *row), F32)] * 2 + [pltpu.VMEM((18, *row), F32)] * 2 + [pltpu.VMEM((4 * FIELDS, 8, LANES), F32)],
+        pairs, part, leaves, gaps, centres, planes, cells, first_paired, first_crossed, paired, crossed,
+        scratch=[pltpu.VMEM((1, *row), F32)] * 2 + [pltpu.VMEM((18, *row), F32)] * 2 + [pltpu.VMEM((6 * FIELDS, 8, LANES), F32)],
     )
     theirs = send(swap, same, lambda d: 1 - d)
     sums = lax.all_to_all(sums, ("space", "day"), 0, 0)
@@ -509,6 +542,7 @@
             pltpu.VMEM(observed.shape, F32),
             pltpu.VMEM((*fit, width), F32),
             pltpu.VMEM((*fit, half), F32),
+            pltpu.VMEM((devices, LANES), F32),
             pltpu.SemaphoreType.DMA((2,)),
         ],
         target=HBM,

time: 37.5 us -> 37.9 us (1.011)
  Pallas kernels: 6.25 us -> 6.66 us
    pallas_call x6, Pallas kernels: 6.25 us -> 6.66 us  [call(): pl.pallas_call(kernel, out_shape=[jax.ShapeDtypeStruct(shape, F32) for sh...]
where the time goes in v6:
time: 37.9 us; the launch traced here: 37.7 us
  blocking collectives  15.2 us (40%)
  starting transfers between devices  9.53 us (25%)
  Pallas kernels  6.66 us (18%)
  waiting for transfers between devices  5.65 us (15%)
  between operations  0.7 us (2%)
    all_to_all x1, blocking collectives, shards(): sums = lax.all_to_all(sums, ('space', 'day'), 0, 0)  15.2 us
    ppermute x6, starting transfers between devices, send(): return lax.ppermute(x, ('space', 'day'), pairs)  9.53 us
    pallas_call x6, Pallas kernels, call(): pl.pallas_call(kernel, out_shape=[jax.ShapeDtypeStruct(shape, F32) for sh...  6.66 us
    ppermute x6, waiting for transfers between devices, send(): return lax.ppermute(x, ('space', 'day'), pairs)  5.65 us
  transfers between devices with their start and end apart: 6, of which 3 were waited for; matrix products, arithmetic and copies ran while one was open for 0% of the time, Pallas kernels for 4%

profile of v6, /device:TPU:0, one launch (start us, length us, event | category | flops | bytes accessed | tf_op | source)
XLA Modules:
  0.0 37.7 jit_solution(9685858885796638619)
XLA Ops:
  0.6 1.4 %shard_map.86 = (f32[4,8,2176]{2,1,0:T(8,128)S(1)}, f32[4,8,2176]{2,1,0:T(8,128)S(1)}, f32[2,8,2176]{2,1,0:T(8,128)S(1)}) custom-call(f32[2,4,4096]{2,1,0:T(4,128)} %refs_0_.1, s32[2,4,4096]{2,1,0:T(4,128)} %refs_1_.1, s32[4,4096]{1,0:T(4,128)} %refs_2_.1, f32[4,4096]{1,0:T(4,128)} %refs_3_.1, f32[4,4096]{1,0:T(4,128)} %refs_4_.1, ...), custom_call_target="tpu_custom_call" | custom-call | flops 2000000 | bytes 589824 | tf_op jit(solution)/shard_map/pallas_call | solution.py:474
  2.0 0.5 %collective-permute-start = (f32[4,8,2176]{2,1,0:T(8,128)S(1)}, f32[4,8,2176]{2,1,0:T(8,128)S(1)}, u32[]{:S(2)}, u32[]{:S(2)}) collective-permute-start(f32[4,8,2176]{2,1,0:T(8,128)S(1)} %get-tuple-element.22.give), channel_id=1, source_target_pairs={{0,1},{1,0},{2,3},{3,2},{4,5},{5,4},{6,7},{7,6},{8,9},{9,8},{10,11... | collective-permute-start | bytes 835592 | tf_op jit(solution)/shard_map/ppermute | solution.py:24
  2.5 1.2 %collective-permute-done.got = f32[4,8,2176]{2,1,0:T(8,128)S(1)} collective-permute-done((f32[4,8,2176]{2,1,0:T(8,128)S(1)}, f32[4,8,2176]{2,1,0:T(8,128)S(1)}, u32[]{:S(2)}, u32[]{:S(2)}) %collective-permute-start) | collective-permute-done | bytes 278560 | tf_op jit(solution)/shard_map/ppermute | solution.py:24
  3.7 0.1 shard_map.88
  3.8 2.9 %collective-permute-start.1 = (f32[10,1,2176]{2,1,0:T(1,128)S(1)}, f32[10,1,2176]{2,1,0:T(1,128)S(1)}, u32[]{:S(2)}, u32[]{:S(2)}) collective-permute-start(f32[10,1,2176]{2,1,0:T(1,128)S(1)} %get-tuple-element.27), channel_id=1, source_target_pairs={{0,2},{1,3},{2,0},{3,1},{4,6},{5,7},{6,4},{7,5},{8,10},{9,11},{10,... | collective-permute-start | bytes 261128 | tf_op jit(solution)/shard_map/ppermute | solution.py:24
  6.7 0.7 %collective-permute-start.2 = (f32[10,1,2176]{2,1,0:T(1,128)S(1)}, f32[10,1,2176]{2,1,0:T(1,128)S(1)}, u32[]{:S(2)}, u32[]{:S(2)}) collective-permute-start(f32[10,1,2176]{2,1,0:T(1,128)S(1)} %get-tuple-element.28), channel_id=1, source_target_pairs={{2,4},{3,5},{4,2},{5,3},{6,8},{7,9},{8,6},{9,7},{10,12},{11,13},{1... | collective-permute-start | bytes 261128 | tf_op jit(solution)/shard_map/ppermute | solution.py:24
  7.4 1.5 %shard_map.87 = (f32[12,8,2176]{2,1,0:T(8,128)S(1)}, f32[2,4,8,2176]{3,2,1,0:T(8,128)S(1)}, f32[2,3,8,2176]{3,2,1,0:T(8,128)S(1)}) custom-call(bf16[9,4,4096]{2,1,0:T(4,128)(2,1)} %stencil.1, f32[4,8,2176]{2,1,0:T(8,128)S(1)} %get-tuple-element.21.mine, f32[4,8,2176]{2,1,0:T(8,128)S(1)} %collective-permute-done.got), custom_call_target="tpu_custom_call" | custom-call | flops 2000000 | bytes 851968 | tf_op jit(solution)/shard_map/pallas_call | solution.py:474
  8.9 0.6 %collective-permute-done.1.refs_4_.refs_7_ = f32[10,1,2176]{2,1,0:T(1,128)S(1)} collective-permute-done((f32[10,1,2176]{2,1,0:T(1,128)S(1)}, f32[10,1,2176]{2,1,0:T(1,128)S(1)}, u32[]{:S(2)}, u32[]{:S(2)}) %collective-permute-start.1) | collective-permute-done | bytes 87072 | tf_op jit(solution)/shard_map/ppermute | solution.py:24
  9.6 0.0 collective-permute-done.2.refs_5_.refs_8_
  9.6 1.3 %shard_map.89 = (f32[2,3,8,2176]{3,2,1,0:T(8,128)S(1)}, f32[2,3,8,2176]{3,2,1,0:T(8,128)S(1)}, f32[2,3,8,2176]{3,2,1,0:T(8,128)S(1)}, f32[2,3,8,2176]{3,2,1,0:T(...) custom-call(f32[2,4,8,2176]{3,2,1,0:T(8,128)S(1)} %get-tuple-element.23.refs_0_.pairs, ...), custom_call_target="tpu_custom_call" | custom-call | flops 2000000 | bytes 2123776 | tf_op jit(solution)/shard_map/pallas_call | solution.py:474
  10.9 4.7 %collective-permute-start.3 = (f32[18,1,2176]{2,1,0:T(1,128)S(1)}, f32[18,1,2176]{2,1,0:T(1,128)S(1)}, u32[]{:S(2)}, u32[]{:S(2)}) collective-permute-start(f32[18,1,2176]{2,1,0:T(1,128)S(1)} %get-tuple-element.33), channel_id=1, source_target_pairs={{0,2},{1,3},{2,0},{3,1},{4,6},{5,7},{6,4},{7,5},{8,10},{9,11},{10,... | collective-permute-start | bytes 470024 | tf_op jit(solution)/shard_map/ppermute | solution.py:24
  15.6 0.7 %collective-permute-start.4 = (f32[18,1,2176]{2,1,0:T(1,128)S(1)}, f32[18,1,2176]{2,1,0:T(1,128)S(1)}, u32[]{:S(2)}, u32[]{:S(2)}) collective-permute-start(f32[18,1,2176]{2,1,0:T(1,128)S(1)} %get-tuple-element.34), channel_id=1, source_target_pairs={{2,4},{3,5},{4,2},{5,3},{6,8},{7,9},{8,6},{9,7},{10,12},{11,13},{1... | collective-permute-start | bytes 470024 | tf_op jit(solution)/shard_map/ppermute | solution.py:24
  16.3 3.8 %collective-permute-done.3.refs_9_ = f32[18,1,2176]{2,1,0:T(1,128)S(1)} collective-permute-done((f32[18,1,2176]{2,1,0:T(1,128)S(1)}, f32[18,1,2176]{2,1,0:T(1,128)S(1)}, u32[]{:S(2)}, u32[]{:S(2)}) %collective-permute-start.3) | collective-permute-done | bytes 156704 | tf_op jit(solution)/shard_map/ppermute | solution.py:24
  20.1 0.0 collective-permute-done.4.refs_10_
  20.1 1.1 %shard_map.90 = (f32[2,3,8,2176]{3,2,1,0:T(8,128)S(1)}, f32[2,3,8,2176]{3,2,1,0:T(8,128)S(1)}, f32[16,8,128]{2,1,0:T(8,128)S(1)}, f32[16,1,128]{2,1,0:T(1,128)S(1)}) custom-call(f32[2,4,8,2176]{3,2,1,0:T(8,128)S(1)} %get-tuple-element.23.refs_0_.pairs, f32[2,3,8,2176]{3,2,1,0:T(8,128)S(1)} %get-tuple-element.29.refs_1_, ...), custom_call_target="tpu_custom_call" | custom-call | flops 2000000 | bytes 3284992 | tf_op jit(solution)/shard_map/pallas_call | solution.py:474
  21.2 0.1 collective-permute-start.5
  21.3 15.2 %all_to_all.5.sums = f32[16,1,128]{2,1,0:T(1,128)S(1)} all-to-all(f32[16,1,128]{2,1,0:T(1,128)S(1)} %get-tuple-element.35), channel_id=1, replica_groups=mesh['region'=2,'space'=8,'day'=2] {'space','day'}, dimensions={0} | all-to-all | bytes 16384 | tf_op jit(solution)/shard_map/all_to_all | solution.py:535
  36.5 0.0 collective-permute-done.5.theirs
  36.5 1.2 %shard_map.91 = (f32[2,4,4096]{2,1,0:T(4,128)}, f32[2,4,2048]{2,1,0:T(4,128)}) custom-call(f32[16,1,128]{2,1,0:T(1,128)S(1)} %all_to_all.5.sums, f32[4,8,2176]{2,1,0:T(8,128)S(1)} %get-tuple-element.21.mine, f32[4,8,2176]{2,1,0:T(8,128)S(1)} %get-tuple-element.22.give, f32[2,4,8,2176]{3,2,1,0:T(8,128)S(1)} %get-tuple-element.23.refs_0_.pairs, ...), custom_call_target="tpu_custom_call" | custom-call | flops 2000000 | bytes 2441216 | tf_op jit(solution)/shard_map/pallas_call | solution.py:474
Async XLA Ops:
  2.0 1.7 %collective-permute-start = (f32[4,8,2176]{2,1,0:T(8,128)S(1)}, f32[4,8,2176]{2,1,0:T(8,128)S(1)}, u32[]{:S(2)}, u32[]{:S(2)}) collective-permute-start(f32[4,8,2176]{2,1,0:T(8,128)S(1)} %get-tuple-element.22.give), channel_id=1, source_target_pairs={{0,1},{1,0},{2,3},{3,2},{4,5},{5,4},{6,7},{7,6},{8,9},{9,8},{10,11... | collective-permute-start | bytes 835592 | tf_op jit(solution)/shard_map/ppermute | solution.py:24
  3.8 5.8 %collective-permute-start.1 = (f32[10,1,2176]{2,1,0:T(1,128)S(1)}, f32[10,1,2176]{2,1,0:T(1,128)S(1)}, u32[]{:S(2)}, u32[]{:S(2)}) collective-permute-start(f32[10,1,2176]{2,1,0:T(1,128)S(1)} %get-tuple-element.27), channel_id=1, source_target_pairs={{0,2},{1,3},{2,0},{3,1},{4,6},{5,7},{6,4},{7,5},{8,10},{9,11},{10,... | collective-permute-start | bytes 261128 | tf_op jit(solution)/shard_map/ppermute | solution.py:24
  6.7 2.9 %collective-permute-start.2 = (f32[10,1,2176]{2,1,0:T(1,128)S(1)}, f32[10,1,2176]{2,1,0:T(1,128)S(1)}, u32[]{:S(2)}, u32[]{:S(2)}) collective-permute-start(f32[10,1,2176]{2,1,0:T(1,128)S(1)} %get-tuple-element.28), channel_id=1, source_target_pairs={{2,4},{3,5},{4,2},{5,3},{6,8},{7,9},{8,6},{9,7},{10,12},{11,13},{1... | collective-permute-start | bytes 261128 | tf_op jit(solution)/shard_map/ppermute | solution.py:24
  10.9 9.2 %collective-permute-start.3 = (f32[18,1,2176]{2,1,0:T(1,128)S(1)}, f32[18,1,2176]{2,1,0:T(1,128)S(1)}, u32[]{:S(2)}, u32[]{:S(2)}) collective-permute-start(f32[18,1,2176]{2,1,0:T(1,128)S(1)} %get-tuple-element.33), channel_id=1, source_target_pairs={{0,2},{1,3},{2,0},{3,1},{4,6},{5,7},{6,4},{7,5},{8,10},{9,11},{10,... | collective-permute-start | bytes 470024 | tf_op jit(solution)/shard_map/ppermute | solution.py:24
  15.6 4.5 %collective-permute-start.4 = (f32[18,1,2176]{2,1,0:T(1,128)S(1)}, f32[18,1,2176]{2,1,0:T(1,128)S(1)}, u32[]{:S(2)}, u32[]{:S(2)}) collective-permute-start(f32[18,1,2176]{2,1,0:T(1,128)S(1)} %get-tuple-element.34), channel_id=1, source_target_pairs={{2,4},{3,5},{4,2},{5,3},{6,8},{7,9},{8,6},{9,7},{10,12},{11,13},{1... | collective-permute-start | bytes 470024 | tf_op jit(solution)/shard_map/ppermute | solution.py:24
  21.2 15.3 %collective-permute-start.5 = (f32[16,8,128]{2,1,0:T(8,128)S(1)}, f32[16,8,128]{2,1,0:T(8,128)S(1)}, u32[]{:S(2)}, u32[]{:S(2)}) collective-permute-start(f32[16,8,128]{2,1,0:T(8,128)S(1)} %get-tuple-element.37), channel_id=1, source_target_pairs={{0,1},{1,0},{2,3},{3,2},{4,5},{5,4},{6,7},{7,6},{8,9},{9,8},{10,11... | collective-permute-start | bytes 196616 | tf_op jit(solution)/shard_map/ppermute | solution.py:24

commit v7 on v6

--- a/solution.py
+++ b/solution.py
@@ -223,7 +223,7 @@
 
 def image_kernel(*refs):
     pairs, moved, planes, cells, came_paired, came_crossed = refs[:6]
-    image, leaves, rims, gaps, centres, paired, crossed, above, below = refs[6:]
+    image, leaves, rims, gaps, parts, paired, crossed, above, below = refs[6:]
     unpack_rows(came_paired, came_crossed, above, below)
     tiles = moved.shape[-1] // LANES
     row = position(0)
@@ -279,12 +279,18 @@
                     u = pairs[half, f, :, at]
                     along = along + u * z
                     square = square + u * u
-        along, square = total(along), total(square)
+        parts[0, f, :, :] = along
+        parts[1, f, :, :] = square
+
+    pack_rows(0, lambda f: (image.at[0, f], image.at[1, f]), paired, crossed)
+    pack_rows(9, lambda f: (leaves.at[0, f], leaves.at[1, f]), paired, crossed)
+
+
+def centres_kernel(parts, centres):
+    for f in range(FIELDS):
+        along, square = total(parts[0, f, :, :]), total(parts[1, f, :, :])
         centre = jnp.where(square > 0.0, along / jnp.where(square > 0.0, square, 1.0), 0.0)
         centres[f, :, :] = jnp.broadcast_to(centre, (8, LANES))
-
-    pack_rows(0, lambda f: (image.at[0, f], image.at[1, f]), paired, crossed)
-    pack_rows(9, lambda f: (leaves.at[0, f], leaves.at[1, f]), paired, crossed)
 
 
 def sums_kernel(*refs):
@@ -517,14 +523,15 @@
         scratch=buffers(*raw),
         source=[HBM, VMEM, VMEM],
     )
-    part, leaves, side_rims, gaps, centres, paired, crossed = call(
+    part, leaves, side_rims, gaps, parts, paired, crossed = call(
         image_kernel,
-        [(2, 3, *pair)] * 4 + [(FIELDS, 8, LANES)] + [(18, *row)] * 2,
+        [(2, 3, *pair)] * 4 + [(2, FIELDS, 8, LANES)] + [(18, *row)] * 2,
         pairs, moved, planes, cells, first_paired, first_crossed,
         scratch=[pltpu.VMEM((10, *row), F32)] * 2,
     )
     paired = send(paired, paired_space)
     crossed = send(crossed, crossed_space)
+    (centres,) = call(centres_kernel, [(FIELDS, 8, LANES)], parts)
     image, image_rims, swap, sums = call(
         sums_kernel,
         [(2, 3, *pair), (2, 3, *pair), (half // LANES, 8, LANES), (devices, 1, LANES)],

time: 37.9 us -> 37.7 us (level)
    pallas_call x6 -> x7, Pallas kernels: 6.66 us -> 6.49 us  [call(): pl.pallas_call(kernel, out_shape=[jax.ShapeDtypeStruct(shape, F32) for sh...]
where the time goes in v7:
time: 37.7 us; the launch traced here: 37.5 us
  blocking collectives  15.2 us (40%)
  starting transfers between devices  9.53 us (25%)
  Pallas kernels  6.49 us (17%)
  waiting for transfers between devices  5.56 us (15%)
  between operations  0.7 us (2%)
    all_to_all x1, blocking collectives, shards(): sums = lax.all_to_all(sums, ('space', 'day'), 0, 0)  15.2 us
    ppermute x6, starting transfers between devices, send(): return lax.ppermute(x, ('space', 'day'), pairs)  9.53 us
    pallas_call x7, Pallas kernels, call(): pl.pallas_call(kernel, out_shape=[jax.ShapeDtypeStruct(shape, F32) for sh...  6.49 us
    ppermute x6, waiting for transfers between devices, send(): return lax.ppermute(x, ('space', 'day'), pairs)  5.56 us
  transfers between devices with their start and end apart: 6, of which 3 were waited for; matrix products, arithmetic and copies ran while one was open for 0% of the time, Pallas kernels for 4%

profile of v7, /device:TPU:0, one launch (start us, length us, event | category | flops | bytes accessed | tf_op | source)
XLA Modules:
  0.0 37.5 jit_solution(15227570594600106524)
XLA Ops:
  0.6 1.4 %shard_map.86 = (f32[4,8,2176]{2,1,0:T(8,128)S(1)}, f32[4,8,2176]{2,1,0:T(8,128)S(1)}, f32[2,8,2176]{2,1,0:T(8,128)S(1)}) custom-call(f32[2,4,4096]{2,1,0:T(4,128)} %refs_0_.1, s32[2,4,4096]{2,1,0:T(4,128)} %refs_1_.1, s32[4,4096]{1,0:T(4,128)} %refs_2_.1, f32[4,4096]{1,0:T(4,128)} %refs_3_.1, f32[4,4096]{1,0:T(4,128)} %refs_4_.1, ...), custom_call_target="tpu_custom_call" | custom-call | flops 2000000 | bytes 589824 | tf_op jit(solution)/shard_map/pallas_call | solution.py:480
  2.0 0.5 %collective-permute-start = (f32[4,8,2176]{2,1,0:T(8,128)S(1)}, f32[4,8,2176]{2,1,0:T(8,128)S(1)}, u32[]{:S(2)}, u32[]{:S(2)}) collective-permute-start(f32[4,8,2176]{2,1,0:T(8,128)S(1)} %get-tuple-element.22.give), channel_id=1, source_target_pairs={{0,1},{1,0},{2,3},{3,2},{4,5},{5,4},{6,7},{7,6},{8,9},{9,8},{10,11... | collective-permute-start | bytes 835592 | tf_op jit(solution)/shard_map/ppermute | solution.py:24
  2.5 1.2 %collective-permute-done.got = f32[4,8,2176]{2,1,0:T(8,128)S(1)} collective-permute-done((f32[4,8,2176]{2,1,0:T(8,128)S(1)}, f32[4,8,2176]{2,1,0:T(8,128)S(1)}, u32[]{:S(2)}, u32[]{:S(2)}) %collective-permute-start) | collective-permute-done | bytes 278560 | tf_op jit(solution)/shard_map/ppermute | solution.py:24
  3.7 0.1 shard_map.88
  3.8 2.9 %collective-permute-start.1 = (f32[10,1,2176]{2,1,0:T(1,128)S(1)}, f32[10,1,2176]{2,1,0:T(1,128)S(1)}, u32[]{:S(2)}, u32[]{:S(2)}) collective-permute-start(f32[10,1,2176]{2,1,0:T(1,128)S(1)} %get-tuple-element.27), channel_id=1, source_target_pairs={{0,2},{1,3},{2,0},{3,1},{4,6},{5,7},{6,4},{7,5},{8,10},{9,11},{10,... | collective-permute-start | bytes 261128 | tf_op jit(solution)/shard_map/ppermute | solution.py:24
  6.7 0.7 %collective-permute-start.2 = (f32[10,1,2176]{2,1,0:T(1,128)S(1)}, f32[10,1,2176]{2,1,0:T(1,128)S(1)}, u32[]{:S(2)}, u32[]{:S(2)}) collective-permute-start(f32[10,1,2176]{2,1,0:T(1,128)S(1)} %get-tuple-element.28), channel_id=1, source_target_pairs={{2,4},{3,5},{4,2},{5,3},{6,8},{7,9},{8,6},{9,7},{10,12},{11,13},{1... | collective-permute-start | bytes 261128 | tf_op jit(solution)/shard_map/ppermute | solution.py:24
  7.4 1.5 %shard_map.87 = (f32[12,8,2176]{2,1,0:T(8,128)S(1)}, f32[2,4,8,2176]{3,2,1,0:T(8,128)S(1)}, f32[2,3,8,2176]{3,2,1,0:T(8,128)S(1)}) custom-call(bf16[9,4,4096]{2,1,0:T(4,128)(2,1)} %stencil.1, f32[4,8,2176]{2,1,0:T(8,128)S(1)} %get-tuple-element.21.mine, f32[4,8,2176]{2,1,0:T(8,128)S(1)} %collective-permute-done.got), custom_call_target="tpu_custom_call" | custom-call | flops 2000000 | bytes 851968 | tf_op jit(solution)/shard_map/pallas_call | solution.py:480
  8.9 0.6 %collective-permute-done.1.refs_4_.refs_7_ = f32[10,1,2176]{2,1,0:T(1,128)S(1)} collective-permute-done((f32[10,1,2176]{2,1,0:T(1,128)S(1)}, f32[10,1,2176]{2,1,0:T(1,128)S(1)}, u32[]{:S(2)}, u32[]{:S(2)}) %collective-permute-start.1) | collective-permute-done | bytes 87072 | tf_op jit(solution)/shard_map/ppermute | solution.py:24
  9.6 0.0 collective-permute-done.2.refs_5_.refs_8_
  9.6 1.1 %shard_map.89 = (f32[2,3,8,2176]{3,2,1,0:T(8,128)S(1)}, f32[2,3,8,2176]{3,2,1,0:T(8,128)S(1)}, f32[2,3,8,2176]{3,2,1,0:T(8,128)S(1)}, f32[2,3,8,2176]{3,2,1,0:T(...) custom-call(f32[2,4,8,2176]{3,2,1,0:T(8,128)S(1)} %get-tuple-element.23.refs_0_.pai, ...), custom_call_target="tpu_custom_call" | custom-call | flops 2000000 | bytes 2123776 | tf_op jit(solution)/shard_map/pallas_call | solution.py:480
  10.7 4.7 %collective-permute-start.3 = (f32[18,1,2176]{2,1,0:T(1,128)S(1)}, f32[18,1,2176]{2,1,0:T(1,128)S(1)}, u32[]{:S(2)}, u32[]{:S(2)}) collective-permute-start(f32[18,1,2176]{2,1,0:T(1,128)S(1)} %get-tuple-element.33), channel_id=1, source_target_pairs={{0,2},{1,3},{2,0},{3,1},{4,6},{5,7},{6,4},{7,5},{8,10},{9,11},{10,... | collective-permute-start | bytes 470024 | tf_op jit(solution)/shard_map/ppermute | solution.py:24
  15.4 0.7 %collective-permute-start.4 = (f32[18,1,2176]{2,1,0:T(1,128)S(1)}, f32[18,1,2176]{2,1,0:T(1,128)S(1)}, u32[]{:S(2)}, u32[]{:S(2)}) collective-permute-start(f32[18,1,2176]{2,1,0:T(1,128)S(1)} %get-tuple-element.34), channel_id=1, source_target_pairs={{2,4},{3,5},{4,2},{5,3},{6,8},{7,9},{8,6},{9,7},{10,12},{11,13},{1... | collective-permute-start | bytes 470024 | tf_op jit(solution)/shard_map/ppermute | solution.py:24
  16.0 0.1 shard_map.90.refs_4_
  16.1 3.7 %collective-permute-done.3.refs_9_ = f32[18,1,2176]{2,1,0:T(1,128)S(1)} collective-permute-done((f32[18,1,2176]{2,1,0:T(1,128)S(1)}, f32[18,1,2176]{2,1,0:T(1,128)S(1)}, u32[]{:S(2)}, u32[]{:S(2)}) %collective-permute-start.3) | collective-permute-done | bytes 156704 | tf_op jit(solution)/shard_map/ppermute | solution.py:24
  19.8 0.0 collective-permute-done.4.refs_10_
  19.9 1.1 %shard_map.91 = (f32[2,3,8,2176]{3,2,1,0:T(8,128)S(1)}, f32[2,3,8,2176]{3,2,1,0:T(8,128)S(1)}, f32[16,8,128]{2,1,0:T(8,128)S(1)}, f32[16,1,128]{2,1,0:T(1,128)S(1)}) custom-call(f32[2,4,8,2176]{3,2,1,0:T(8,128)S(1)} %get-tuple-element.23.refs_0_.pairs, f32[2,3,8,2176]{3,2,1,0:T(8,128)S(1)} %get-tuple-element.29.refs_1_, ...), custom_call_target="tpu_custom_call" | custom-call | flops 2000000 | bytes 3284992 | tf_op jit(solution)/shard_map/pallas_call | solution.py:480
  21.0 0.1 collective-permute-start.5
  21.1 15.2 %all_to_all.5.sums = f32[16,1,128]{2,1,0:T(1,128)S(1)} all-to-all(f32[16,1,128]{2,1,0:T(1,128)S(1)} %get-tuple-element.35), channel_id=1, replica_groups=mesh['region'=2,'space'=8,'day'=2] {'space','day'}, dimensions={0} | all-to-all | bytes 16384 | tf_op jit(solution)/shard_map/all_to_all | solution.py:542
  36.2 0.0 collective-permute-done.5.theirs
  36.2 1.2 %shard_map.92 = (f32[2,4,4096]{2,1,0:T(4,128)}, f32[2,4,2048]{2,1,0:T(4,128)}) custom-call(f32[16,1,128]{2,1,0:T(1,128)S(1)} %all_to_all.5.sums, f32[4,8,2176]{2,1,0:T(8,128)S(1)} %get-tuple-element.21.mine, f32[4,8,2176]{2,1,0:T(8,128)S(1)} %get-tuple-element.22.give, f32[2,4,8,2176]{3,2,1,0:T(8,128)S(1)} %get-tuple-element.23.refs_0_.pairs, ...), custom_call_target="tpu_custom_call" | custom-call | flops 2000000 | bytes 2441216 | tf_op jit(solution)/shard_map/pallas_call | solution.py:480
Async XLA Ops:
  2.0 1.7 %collective-permute-start = (f32[4,8,2176]{2,1,0:T(8,128)S(1)}, f32[4,8,2176]{2,1,0:T(8,128)S(1)}, u32[]{:S(2)}, u32[]{:S(2)}) collective-permute-start(f32[4,8,2176]{2,1,0:T(8,128)S(1)} %get-tuple-element.22.give), channel_id=1, source_target_pairs={{0,1},{1,0},{2,3},{3,2},{4,5},{5,4},{6,7},{7,6},{8,9},{9,8},{10,11... | collective-permute-start | bytes 835592 | tf_op jit(solution)/shard_map/ppermute | solution.py:24
  3.8 5.8 %collective-permute-start.1 = (f32[10,1,2176]{2,1,0:T(1,128)S(1)}, f32[10,1,2176]{2,1,0:T(1,128)S(1)}, u32[]{:S(2)}, u32[]{:S(2)}) collective-permute-start(f32[10,1,2176]{2,1,0:T(1,128)S(1)} %get-tuple-element.27), channel_id=1, source_target_pairs={{0,2},{1,3},{2,0},{3,1},{4,6},{5,7},{6,4},{7,5},{8,10},{9,11},{10,... | collective-permute-start | bytes 261128 | tf_op jit(solution)/shard_map/ppermute | solution.py:24
  6.7 2.9 %collective-permute-start.2 = (f32[10,1,2176]{2,1,0:T(1,128)S(1)}, f32[10,1,2176]{2,1,0:T(1,128)S(1)}, u32[]{:S(2)}, u32[]{:S(2)}) collective-permute-start(f32[10,1,2176]{2,1,0:T(1,128)S(1)} %get-tuple-element.28), channel_id=1, source_target_pairs={{2,4},{3,5},{4,2},{5,3},{6,8},{7,9},{8,6},{9,7},{10,12},{11,13},{1... | collective-permute-start | bytes 261128 | tf_op jit(solution)/shard_map/ppermute | solution.py:24
  10.7 9.2 %collective-permute-start.3 = (f32[18,1,2176]{2,1,0:T(1,128)S(1)}, f32[18,1,2176]{2,1,0:T(1,128)S(1)}, u32[]{:S(2)}, u32[]{:S(2)}) collective-permute-start(f32[18,1,2176]{2,1,0:T(1,128)S(1)} %get-tuple-element.33), channel_id=1, source_target_pairs={{0,2},{1,3},{2,0},{3,1},{4,6},{5,7},{6,4},{7,5},{8,10},{9,11},{10,... | collective-permute-start | bytes 470024 | tf_op jit(solution)/shard_map/ppermute | solution.py:24
  15.4 4.5 %collective-permute-start.4 = (f32[18,1,2176]{2,1,0:T(1,128)S(1)}, f32[18,1,2176]{2,1,0:T(1,128)S(1)}, u32[]{:S(2)}, u32[]{:S(2)}) collective-permute-start(f32[18,1,2176]{2,1,0:T(1,128)S(1)} %get-tuple-element.34), channel_id=1, source_target_pairs={{2,4},{3,5},{4,2},{5,3},{6,8},{7,9},{8,6},{9,7},{10,12},{11,13},{1... | collective-permute-start | bytes 470024 | tf_op jit(solution)/shard_map/ppermute | solution.py:24
  21.0 15.3 %collective-permute-start.5 = (f32[16,8,128]{2,1,0:T(8,128)S(1)}, f32[16,8,128]{2,1,0:T(8,128)S(1)}, u32[]{:S(2)}, u32[]{:S(2)}) collective-permute-start(f32[16,8,128]{2,1,0:T(8,128)S(1)} %get-tuple-element.37), channel_id=1, source_target_pairs={{0,1},{1,0},{2,3},{3,2},{4,5},{5,4},{6,7},{7,6},{8,9},{9,8},{10,11... | collective-permute-start | bytes 196616 | tf_op jit(solution)/shard_map/ppermute | solution.py:24

commit v8 on v7

--- a/solution.py
+++ b/solution.py
@@ -380,7 +380,7 @@
                 swap[t, :, :] = image[1 - which, 0, :, tile(t + which)]
 
 
-def fit_kernel(sums, mine, give, pairs, image, theirs, side_rims, image_rims, posterior, fitted, mean, cells, ready, lines, semaphores):
+def fit_kernel(sums, mine, give, pairs, image, theirs, side_rims, image_rims, posterior, fitted, mean, cells, lines, semaphores):
     day = lax.axis_index("day")
     tiles = mine.shape[-1] // LANES
     row = position(0)
@@ -421,6 +421,14 @@
 
     out_mean = pltpu.make_async_copy(mean, posterior, semaphores.at[0])
     out_mean.start()
+    middle = (tiles - 1) // 2
+    part = middle * LANES
+
+    def fit_copy(k):
+        source = pl.ds(pl.multiple_of(day * LANES + k * part, LANES), part)
+        return pltpu.make_async_copy(cells.at[:, :, source], fitted.at[:, :, k * part : (k + 1) * part], semaphores.at[1 + k])
+
+    out_fit = [fit_copy(0), fit_copy(1)]
 
     wide = {(f, half): (Shift(1), Shift(-1)) for f in (1, 2) for half in (0, 1)}
     kept = {}
@@ -459,16 +467,12 @@
 
             cells[0, :, tile(q)] = persistence[0:4]
             cells[1, :, tile(q)] = diffusion[0:4]
-    for which in (0, 1):
-
-        @pl.when(day == which)
-        def _():
-            ready[...] = cells[:, :, which * LANES : which * LANES + ready.shape[-1]]
-
-    out_fit = pltpu.make_async_copy(ready, fitted, semaphores.at[1])
-    out_fit.start()
+            if q == middle:
+                out_fit[0].start()
+    out_fit[1].start()
     out_mean.wait()
-    out_fit.wait()
+    for copy in out_fit:
+        copy.wait()
 
 
 VMEM = pl.BlockSpec(memory_space=pltpu.VMEM)
@@ -548,9 +552,8 @@
         scratch=[
             pltpu.VMEM(observed.shape, F32),
             pltpu.VMEM((*fit, width), F32),
-            pltpu.VMEM((*fit, half), F32),
             pltpu.VMEM((devices, LANES), F32),
-            pltpu.SemaphoreType.DMA((2,)),
+            pltpu.SemaphoreType.DMA((3,)),
         ],
         target=HBM,
     )

time: 37.7 us -> 37.7 us (level)
  no operation moved by 1% of the time
where the time goes in v8:
time: 37.7 us; the launch traced here: 37.4 us
  blocking collectives  15.2 us (40%)
  starting transfers between devices  9.53 us (25%)
  Pallas kernels  6.47 us (17%)
  waiting for transfers between devices  5.56 us (15%)
  between operations  0.7 us (2%)
    all_to_all x1, blocking collectives, shards(): sums = lax.all_to_all(sums, ('space', 'day'), 0, 0)  15.2 us
    ppermute x6, starting transfers between devices, send(): return lax.ppermute(x, ('space', 'day'), pairs)  9.53 us
    pallas_call x7, Pallas kernels, call(): pl.pallas_call(kernel, out_shape=[jax.ShapeDtypeStruct(shape, F32) for sh...  6.47 us
    ppermute x6, waiting for transfers between devices, send(): return lax.ppermute(x, ('space', 'day'), pairs)  5.56 us
  transfers between devices with their start and end apart: 6, of which 3 were waited for; matrix products, arithmetic and copies ran while one was open for 0% of the time, Pallas kernels for 4%

profile of v8, /device:TPU:0, one launch (start us, length us, event | category | flops | bytes accessed | tf_op | source)
XLA Modules:
  0.0 37.4 jit_solution(9648598551853023034)
XLA Ops:
  0.6 1.4 %shard_map.86 = (f32[4,8,2176]{2,1,0:T(8,128)S(1)}, f32[4,8,2176]{2,1,0:T(8,128)S(1)}, f32[2,8,2176]{2,1,0:T(8,128)S(1)}) custom-call(f32[2,4,4096]{2,1,0:T(4,128)} %refs_0_.1, s32[2,4,4096]{2,1,0:T(4,128)} %refs_1_.1, s32[4,4096]{1,0:T(4,128)} %refs_2_.1, f32[4,4096]{1,0:T(4,128)} %refs_3_.1, f32[4,4096]{1,0:T(4,128)} %refs_4_.1, ...), custom_call_target="tpu_custom_call" | custom-call | flops 2000000 | bytes 589824 | tf_op jit(solution)/shard_map/pallas_call | solution.py:484
  2.0 0.5 %collective-permute-start = (f32[4,8,2176]{2,1,0:T(8,128)S(1)}, f32[4,8,2176]{2,1,0:T(8,128)S(1)}, u32[]{:S(2)}, u32[]{:S(2)}) collective-permute-start(f32[4,8,2176]{2,1,0:T(8,128)S(1)} %get-tuple-element.22.give), channel_id=1, source_target_pairs={{0,1},{1,0},{2,3},{3,2},{4,5},{5,4},{6,7},{7,6},{8,9},{9,8},{10,11... | collective-permute-start | bytes 835592 | tf_op jit(solution)/shard_map/ppermute | solution.py:24
  2.5 1.2 %collective-permute-done.got = f32[4,8,2176]{2,1,0:T(8,128)S(1)} collective-permute-done((f32[4,8,2176]{2,1,0:T(8,128)S(1)}, f32[4,8,2176]{2,1,0:T(8,128)S(1)}, u32[]{:S(2)}, u32[]{:S(2)}) %collective-permute-start) | collective-permute-done | bytes 278560 | tf_op jit(solution)/shard_map/ppermute | solution.py:24
  3.7 0.1 shard_map.88
  3.8 2.9 %collective-permute-start.1 = (f32[10,1,2176]{2,1,0:T(1,128)S(1)}, f32[10,1,2176]{2,1,0:T(1,128)S(1)}, u32[]{:S(2)}, u32[]{:S(2)}) collective-permute-start(f32[10,1,2176]{2,1,0:T(1,128)S(1)} %get-tuple-element.27), channel_id=1, source_target_pairs={{0,2},{1,3},{2,0},{3,1},{4,6},{5,7},{6,4},{7,5},{8,10},{9,11},{10,... | collective-permute-start | bytes 261128 | tf_op jit(solution)/shard_map/ppermute | solution.py:24
  6.7 0.7 %collective-permute-start.2 = (f32[10,1,2176]{2,1,0:T(1,128)S(1)}, f32[10,1,2176]{2,1,0:T(1,128)S(1)}, u32[]{:S(2)}, u32[]{:S(2)}) collective-permute-start(f32[10,1,2176]{2,1,0:T(1,128)S(1)} %get-tuple-element.28), channel_id=1, source_target_pairs={{2,4},{3,5},{4,2},{5,3},{6,8},{7,9},{8,6},{9,7},{10,12},{11,13},{1... | collective-permute-start | bytes 261128 | tf_op jit(solution)/shard_map/ppermute | solution.py:24
  7.4 1.5 %shard_map.87 = (f32[12,8,2176]{2,1,0:T(8,128)S(1)}, f32[2,4,8,2176]{3,2,1,0:T(8,128)S(1)}, f32[2,3,8,2176]{3,2,1,0:T(8,128)S(1)}) custom-call(bf16[9,4,4096]{2,1,0:T(4,128)(2,1)} %stencil.1, f32[4,8,2176]{2,1,0:T(8,128)S(1)} %get-tuple-element.21.mine, f32[4,8,2176]{2,1,0:T(8,128)S(1)} %collective-permute-done.got), custom_call_target="tpu_custom_call" | custom-call | flops 2000000 | bytes 851968 | tf_op jit(solution)/shard_map/pallas_call | solution.py:484
  8.9 0.6 %collective-permute-done.1.refs_4_.refs_7_ = f32[10,1,2176]{2,1,0:T(1,128)S(1)} collective-permute-done((f32[10,1,2176]{2,1,0:T(1,128)S(1)}, f32[10,1,2176]{2,1,0:T(1,128)S(1)}, u32[]{:S(2)}, u32[]{:S(2)}) %collective-permute-start.1) | collective-permute-done | bytes 87072 | tf_op jit(solution)/shard_map/ppermute | solution.py:24
  9.6 0.0 collective-permute-done.2.refs_5_.refs_8_
  9.6 1.1 %shard_map.89 = (f32[2,3,8,2176]{3,2,1,0:T(8,128)S(1)}, f32[2,3,8,2176]{3,2,1,0:T(8,128)S(1)}, f32[2,3,8,2176]{3,2,1,0:T(8,128)S(1)}, f32[2,3,8,2176]{3,2,1,0:T(...) custom-call(f32[2,4,8,2176]{3,2,1,0:T(8,128)S(1)} %get-tuple-element.23.refs_0_.pai, ...), custom_call_target="tpu_custom_call" | custom-call | flops 2000000 | bytes 2123776 | tf_op jit(solution)/shard_map/pallas_call | solution.py:484
  10.7 4.7 %collective-permute-start.3 = (f32[18,1,2176]{2,1,0:T(1,128)S(1)}, f32[18,1,2176]{2,1,0:T(1,128)S(1)}, u32[]{:S(2)}, u32[]{:S(2)}) collective-permute-start(f32[18,1,2176]{2,1,0:T(1,128)S(1)} %get-tuple-element.33), channel_id=1, source_target_pairs={{0,2},{1,3},{2,0},{3,1},{4,6},{5,7},{6,4},{7,5},{8,10},{9,11},{10,... | collective-permute-start | bytes 470024 | tf_op jit(solution)/shard_map/ppermute | solution.py:24
  15.4 0.7 %collective-permute-start.4 = (f32[18,1,2176]{2,1,0:T(1,128)S(1)}, f32[18,1,2176]{2,1,0:T(1,128)S(1)}, u32[]{:S(2)}, u32[]{:S(2)}) collective-permute-start(f32[18,1,2176]{2,1,0:T(1,128)S(1)} %get-tuple-element.34), channel_id=1, source_target_pairs={{2,4},{3,5},{4,2},{5,3},{6,8},{7,9},{8,6},{9,7},{10,12},{11,13},{1... | collective-permute-start | bytes 470024 | tf_op jit(solution)/shard_map/ppermute | solution.py:24
  16.0 0.1 shard_map.90.refs_4_
  16.1 3.7 %collective-permute-done.3.refs_9_ = f32[18,1,2176]{2,1,0:T(1,128)S(1)} collective-permute-done((f32[18,1,2176]{2,1,0:T(1,128)S(1)}, f32[18,1,2176]{2,1,0:T(1,128)S(1)}, u32[]{:S(2)}, u32[]{:S(2)}) %collective-permute-start.3) | collective-permute-done | bytes 156704 | tf_op jit(solution)/shard_map/ppermute | solution.py:24
  19.8 0.0 collective-permute-done.4.refs_10_
  19.9 1.1 %shard_map.91 = (f32[2,3,8,2176]{3,2,1,0:T(8,128)S(1)}, f32[2,3,8,2176]{3,2,1,0:T(8,128)S(1)}, f32[16,8,128]{2,1,0:T(8,128)S(1)}, f32[16,1,128]{2,1,0:T(1,128)S(1)}) custom-call(f32[2,4,8,2176]{3,2,1,0:T(8,128)S(1)} %get-tuple-element.23.refs_0_.pairs, f32[2,3,8,2176]{3,2,1,0:T(8,128)S(1)} %get-tuple-element.29.refs_1_, ...), custom_call_target="tpu_custom_call" | custom-call | flops 2000000 | bytes 3284992 | tf_op jit(solution)/shard_map/pallas_call | solution.py:484
  21.0 0.1 collective-permute-start.5
  21.1 15.2 %all_to_all.5.sums = f32[16,1,128]{2,1,0:T(1,128)S(1)} all-to-all(f32[16,1,128]{2,1,0:T(1,128)S(1)} %get-tuple-element.35), channel_id=1, replica_groups=mesh['region'=2,'space'=8,'day'=2] {'space','day'}, dimensions={0} | all-to-all | bytes 16384 | tf_op jit(solution)/shard_map/all_to_all | solution.py:546
  36.2 0.0 collective-permute-done.5.theirs
  36.2 1.2 %shard_map.92 = (f32[2,4,4096]{2,1,0:T(4,128)}, f32[2,4,2048]{2,1,0:T(4,128)}) custom-call(f32[16,1,128]{2,1,0:T(1,128)S(1)} %all_to_all.5.sums, f32[4,8,2176]{2,1,0:T(8,128)S(1)} %get-tuple-element.21.mine, f32[4,8,2176]{2,1,0:T(8,128)S(1)} %get-tuple-element.22.give, f32[2,4,8,2176]{3,2,1,0:T(8,128)S(1)} %get-tuple-element.23.refs_0_.pairs, ...), custom_call_target="tpu_custom_call" | custom-call | flops 2000000 | bytes 2441216 | tf_op jit(solution)/shard_map/pallas_call | solution.py:484
Async XLA Ops:
  2.0 1.7 %collective-permute-start = (f32[4,8,2176]{2,1,0:T(8,128)S(1)}, f32[4,8,2176]{2,1,0:T(8,128)S(1)}, u32[]{:S(2)}, u32[]{:S(2)}) collective-permute-start(f32[4,8,2176]{2,1,0:T(8,128)S(1)} %get-tuple-element.22.give), channel_id=1, source_target_pairs={{0,1},{1,0},{2,3},{3,2},{4,5},{5,4},{6,7},{7,6},{8,9},{9,8},{10,11... | collective-permute-start | bytes 835592 | tf_op jit(solution)/shard_map/ppermute | solution.py:24
  3.8 5.8 %collective-permute-start.1 = (f32[10,1,2176]{2,1,0:T(1,128)S(1)}, f32[10,1,2176]{2,1,0:T(1,128)S(1)}, u32[]{:S(2)}, u32[]{:S(2)}) collective-permute-start(f32[10,1,2176]{2,1,0:T(1,128)S(1)} %get-tuple-element.27), channel_id=1, source_target_pairs={{0,2},{1,3},{2,0},{3,1},{4,6},{5,7},{6,4},{7,5},{8,10},{9,11},{10,... | collective-permute-start | bytes 261128 | tf_op jit(solution)/shard_map/ppermute | solution.py:24
  6.7 2.9 %collective-permute-start.2 = (f32[10,1,2176]{2,1,0:T(1,128)S(1)}, f32[10,1,2176]{2,1,0:T(1,128)S(1)}, u32[]{:S(2)}, u32[]{:S(2)}) collective-permute-start(f32[10,1,2176]{2,1,0:T(1,128)S(1)} %get-tuple-element.28), channel_id=1, source_target_pairs={{2,4},{3,5},{4,2},{5,3},{6,8},{7,9},{8,6},{9,7},{10,12},{11,13},{1... | collective-permute-start | bytes 261128 | tf_op jit(solution)/shard_map/ppermute | solution.py:24
  10.7 9.2 %collective-permute-start.3 = (f32[18,1,2176]{2,1,0:T(1,128)S(1)}, f32[18,1,2176]{2,1,0:T(1,128)S(1)}, u32[]{:S(2)}, u32[]{:S(2)}) collective-permute-start(f32[18,1,2176]{2,1,0:T(1,128)S(1)} %get-tuple-element.33), channel_id=1, source_target_pairs={{0,2},{1,3},{2,0},{3,1},{4,6},{5,7},{6,4},{7,5},{8,10},{9,11},{10,... | collective-permute-start | bytes 470024 | tf_op jit(solution)/shard_map/ppermute | solution.py:24
  15.4 4.5 %collective-permute-start.4 = (f32[18,1,2176]{2,1,0:T(1,128)S(1)}, f32[18,1,2176]{2,1,0:T(1,128)S(1)}, u32[]{:S(2)}, u32[]{:S(2)}) collective-permute-start(f32[18,1,2176]{2,1,0:T(1,128)S(1)} %get-tuple-element.34), channel_id=1, source_target_pairs={{2,4},{3,5},{4,2},{5,3},{6,8},{7,9},{8,6},{9,7},{10,12},{11,13},{1... | collective-permute-start | bytes 470024 | tf_op jit(solution)/shard_map/ppermute | solution.py:24
  21.0 15.3 %collective-permute-start.5 = (f32[16,8,128]{2,1,0:T(8,128)S(1)}, f32[16,8,128]{2,1,0:T(8,128)S(1)}, u32[]{:S(2)}, u32[]{:S(2)}) collective-permute-start(f32[16,8,128]{2,1,0:T(8,128)S(1)} %get-tuple-element.37), channel_id=1, source_target_pairs={{0,1},{1,0},{2,3},{3,2},{4,5},{5,4},{6,7},{7,6},{8,9},{9,8},{10,11... | collective-permute-start | bytes 196616 | tf_op jit(solution)/shard_map/ppermute | solution.py:24
